TPU v7x, 256 devices: a whole 4x4x8 slice. The times are simulated.
256 devices in a mesh: ctx: 64 (over z, x, core), head: 4 (over y).
Axes of the slice: x: 4, y: 4, z: 8, core: 2. Of those that a mesh axis runs over, the one named last changes fastest.
Arguments:
- mixer_input: bfloat16 [2, 4096, 16384], P(None, ('ctx', 'head')), may hold values from -6 to 6
- gate_input: bfloat16 [2, 4096, 16384], P(None, ('ctx', 'head')), may hold values from -6 to 6
- step_input: bfloat16 [2, 4096, 16384], P(None, ('ctx', 'head'))
- state_proj: bfloat16 [2, 4096, 32], P(None, 'ctx'), may hold values from -4 to 4
- conv_weight: bfloat16 [4, 16384], replicated, may hold values from -3 to 3
- conv_bias: float32 [16384], replicated, may hold values from -1 to 1
- step_bias: float32 [16384], P('head')
- decay_log: float32 [16, 16384], P(None, 'head'), may hold values from -0.7 to 0.7
- skip_gain: float32 [16384], P('head'), may hold values from 0.5 to 1.5
- query_states: bfloat16 [2, 4096, 8192], P(None, ('ctx', 'head')), may hold values from -5 to 5
- key_states: bfloat16 [2, 4096, 1024], P(None, ('ctx', 'head')), may hold values from -5 to 5
- value_states: bfloat16 [2, 4096, 1024], P(None, ('ctx', 'head')), may hold values from -6 to 6
- lengths: int32 [2], replicated, may hold values from 1024 to 4096, as said below
Outputs:
- mixer_output: bfloat16 [2, 4096, 16384], P(None, 'ctx', 'head')
- attention_output: bfloat16 [2, 4096, 8192], P(None, 'ctx', 'head')
Inputs may be any that keep to these rules, and one draw needn't show every extreme that they name: `lengths`: one of the 2 sequences has length 4096.
All inputs are finite; a program needn't handle non-finite values.
Results may differ from a plain program's by a relative error of at most 0.0043.
Values may be sent and summed in bfloat16 or wider, within the bound.
No kernel may reach another device: no remote copies, remote signals or barrier semaphores. Data moves between devices by JAX's collectives and lax.ppermute only.
A program may use at most 256 MiB of HBM per device.

v0:
```python
import math

import jax
import jax.numpy as jnp
from jax import lax
from jax.sharding import PartitionSpec as P

HD = 128


neg_large = -1e30


def passed_along(block, axis, distance):
    devices = range(lax.axis_size(axis))
    route = [(i - distance, i) for i in devices if i - distance in devices]
    return lax.ppermute(block, axis, route)


def carried_in(value, axis, join, neutral):
    count, mine = (lax.axis_size(axis), lax.axis_index(axis))
    pieces = jax.tree.map(lambda part: lax.all_gather(part, axis), value)
    total = jax.tree.map(
        lambda part, zero: jnp.full_like(part, 0) + jnp.asarray(zero, part.dtype), value, neutral
    )

    def step(position, total):
        longer = join(total, jax.tree.map(lambda part: part[position], pieces))
        return jax.tree.map(lambda new, old: jnp.where(position < mine, new, old), longer, total)

    return lax.fori_loop(0, count - 1, step, total)


def conv_rows(padded, conv_weight, conv_bias, row_count):
    running = (
        jnp.zeros((padded.shape[0], row_count, padded.shape[2]), jnp.float32)
        + conv_bias[None, None, :]
    )
    for tap_index in range(conv_weight.shape[0]):
        window = padded[:, tap_index : tap_index + row_count, :].astype(jnp.float32)
        running = running + window * conv_weight[tap_index].astype(jnp.float32)[None, None, :]
    return jax.nn.silu(running).astype(jnp.bfloat16)


def block_width(key_count):
    chosen = min(key_count, 512)
    while key_count % chosen != 0:
        chosen = chosen - 1
    return chosen


def empty_state(query_block):
    state_shape = (
        query_block.shape[0],
        query_block.shape[2],
        query_block.shape[3],
        query_block.shape[1],
    )
    return (
        jnp.full(state_shape, neg_large, jnp.float32),
        jnp.zeros(state_shape, jnp.float32),
        jnp.zeros(state_shape + (query_block.shape[4],), jnp.float32),
    )


def attend_block(
    carried, query_block, query_offset, key_block, value_block, key_offset, logit_scale_factor
):
    query_count = query_block.shape[1]
    key_count = key_block.shape[1]

    def compute(previous):
        row_peak, softmax_divisor, accumulated = previous
        score_matrix = (
            jnp.einsum(
                "brkgd,bskd->bkgrs", query_block, key_block, preferred_element_type=jnp.float32
            )
            * logit_scale_factor
        )
        query_pos = query_offset + jnp.arange(query_count, dtype=jnp.int32)
        key_pos = key_offset + jnp.arange(key_count, dtype=jnp.int32)
        allowed = key_pos[None, :] <= query_pos[:, None]
        score_matrix = jnp.where(allowed, score_matrix, neg_large)
        new_peak = jnp.maximum(row_peak, jnp.max(score_matrix, axis=-1))
        weights = jnp.where(allowed, jnp.exp(score_matrix - new_peak[..., None]), 0.0)
        fade_factor = jnp.exp(row_peak - new_peak)
        softmax_divisor = softmax_divisor * fade_factor + jnp.sum(weights, axis=-1)
        update = jnp.einsum(
            "bkgrs,bskd->bkgrd",
            weights.astype(jnp.bfloat16),
            value_block,
            preferred_element_type=jnp.float32,
        )
        accumulated = accumulated * fade_factor[..., None] + update
        return (new_peak, softmax_divisor, accumulated)

    def unchanged(previous):
        return previous

    return lax.cond(key_offset > query_offset + query_count - 1, unchanged, compute, carried)


def finish_rows(state_one):
    row_peak, softmax_divisor, accumulated = state_one
    normalised = accumulated / softmax_divisor[..., None]
    ordered = jnp.transpose(normalised, (0, 3, 1, 2, 4))
    return ordered.reshape(ordered.shape[0], ordered.shape[1], -1).astype(jnp.bfloat16)


def combine_carry(earlier, latter):
    return (earlier[0] * latter[0], latter[0] * earlier[1] + latter[1])


def shards(
    mixer_input,
    gate_input,
    step_input,
    state_proj,
    conv_weight,
    conv_bias,
    step_bias,
    decay_log,
    skip_gain,
    query_states,
    key_states,
    value_states,
    lengths,
):
    tap_count = conv_weight.shape[0]
    exchanged = (
        lax.all_to_all(mixer_input, "head", split_axis=2, concat_axis=1, tiled=True),
        lax.all_to_all(gate_input, "head", split_axis=2, concat_axis=1, tiled=True),
        lax.all_to_all(step_input, "head", split_axis=2, concat_axis=1, tiled=True),
        lax.all_to_all(query_states, "head", split_axis=2, concat_axis=1, tiled=True),
        lax.all_to_all(key_states, "head", split_axis=2, concat_axis=1, tiled=True),
        lax.all_to_all(value_states, "head", split_axis=2, concat_axis=1, tiled=True),
    )
    lead_local, gate_local, step_local, query_local, key_local, value_local = exchanged
    batch_size, row_count, channel_count = gate_local.shape
    channel_start = lax.axis_index("head") * channel_count
    weight_local = lax.dynamic_slice_in_dim(conv_weight, channel_start, channel_count, 1)
    bias_local = lax.dynamic_slice_in_dim(conv_bias, channel_start, channel_count, 0)
    tail_rows = lead_local[:, row_count - (tap_count - 1) :, :]
    before = passed_along(tail_rows, "ctx", 1)
    padded = jnp.concatenate([before, lead_local], axis=1)
    conv_out = conv_rows(padded, weight_local, bias_local, row_count)
    ctx_index = lax.axis_index("ctx")
    positions = ctx_index * row_count + jnp.arange(row_count, dtype=jnp.int32)
    live_rows = positions[None, :] < lengths[:, None]
    decay_rate = jnp.exp(decay_log)
    state_count = state_proj.shape[2] // 2
    conv_time = jnp.swapaxes(conv_out, 0, 1)
    step_time = jnp.swapaxes(step_local, 0, 1)
    proj_time = jnp.swapaxes(state_proj, 0, 1).astype(jnp.float32)
    readout_time = proj_time[:, :, state_count:]

    def advance(carry, inputs):
        state_now, elapsed_now = carry
        conv_row, step_row, proj_row = inputs
        step_row = jax.nn.softplus(step_row.astype(jnp.float32) + step_bias[None, :])
        elapsed_now = elapsed_now + step_row
        decay_now = jnp.exp(-step_row[:, None, :] * decay_rate[None])
        state_now = (
            decay_now * state_now
            + (step_row * conv_row.astype(jnp.float32))[:, None, :]
            * proj_row[:, :state_count, None]
        )
        return (
            (state_now, elapsed_now),
            (jnp.sum(proj_row[:, state_count:, None] * state_now, axis=1), elapsed_now),
        )

    start_state = jnp.zeros((batch_size, state_count, channel_count), jnp.float32)
    start_elapsed = jnp.zeros((batch_size, channel_count), jnp.float32)
    final_carry, scanned = lax.scan(
        advance, (start_state, start_elapsed), (conv_time, step_time, proj_time), unroll=8
    )
    final_state, total_elapsed = final_carry
    local_time, elapsed_time = scanned
    through = jnp.exp(-total_elapsed[:, None, :] * decay_rate[None])
    identity = (jnp.ones_like(through), jnp.zeros_like(final_state))
    prefix = carried_in((through, final_state), "ctx", combine_carry, identity)
    entering = prefix[1]
    carried = jnp.sum(
        readout_time[:, :, :, None]
        * jnp.exp(-elapsed_time[:, :, None, :] * decay_rate[None, None])
        * entering[None],
        axis=2,
    )
    mixed_time = (
        local_time + carried + skip_gain[None, None, :] * conv_time.astype(jnp.float32)
    ) * jax.nn.silu(jnp.swapaxes(gate_local, 0, 1).astype(jnp.float32))
    mixed_rows = jnp.swapaxes(mixed_time.astype(jnp.bfloat16), 0, 1)
    mixer_output = jnp.where(live_rows[:, :, None], mixed_rows, jnp.zeros((), jnp.bfloat16))
    kv_count = key_local.shape[2] // HD
    group_size = query_local.shape[2] // HD // kv_count
    query_five = query_local.reshape(batch_size, row_count, kv_count, group_size, HD)
    key_four = key_local.reshape(batch_size, row_count, kv_count, HD)
    value_four = value_local.reshape(batch_size, row_count, kv_count, HD)
    own_offset = ctx_index * row_count
    query_groups = [(query_five, own_offset)]
    logit_scale_factor = 1.0 / math.sqrt(HD)
    key_whole, value_whole = (
        lax.all_gather(key_four, "ctx", axis=1, tiled=True),
        lax.all_gather(value_four, "ctx", axis=1, tiled=True),
    )
    total_rows = key_whole.shape[1]
    chosen = block_width(total_rows)

    def one_block(block_index, current):
        key_block = lax.dynamic_slice_in_dim(key_whole, block_index * chosen, chosen, 1)
        value_block = lax.dynamic_slice_in_dim(value_whole, block_index * chosen, chosen, 1)
        key_offset = block_index * chosen
        return tuple(
            (
                attend_block(
                    state_one,
                    group[0],
                    group[1],
                    key_block,
                    value_block,
                    key_offset,
                    logit_scale_factor,
                )
                for state_one, group in zip(current, query_groups)
            )
        )

    initial = tuple((empty_state(group[0]) for group in query_groups))
    finished = lax.fori_loop(0, total_rows // chosen, one_block, initial)
    attended = finish_rows(finished[0])
    attention_output = jnp.where(live_rows[:, :, None], attended, jnp.zeros((), jnp.bfloat16))
    return (mixer_output, attention_output)


def solution(mesh):
    in_specs = (
        P(None, ("ctx", "head"), None),
        P(None, ("ctx", "head"), None),
        P(None, ("ctx", "head"), None),
        P(None, "ctx", None),
        P(),
        P(),
        P("head"),
        P(None, "head"),
        P("head"),
        P(None, ("ctx", "head"), None),
        P(None, ("ctx", "head"), None),
        P(None, ("ctx", "head"), None),
        P(),
    )
    out_specs = (P(None, "ctx", "head"), P(None, "ctx", "head"))
    return jax.shard_map(shards, mesh=mesh, in_specs=in_specs, out_specs=out_specs, check_vma=False)
```

profile of v0, /device:TPU:32, one launch (start us, length us, event | category | flops | bytes accessed | tf_op | source)
XLA Modules:
  0.0 616.6 jit_solution(5746733392723472344)
XLA Ops:
  9.0 9.9 %all_to_all.90 = bf16[4,2,4096]{2,1,0:T(2,128)(2,1)S(1)} all-to-all(bf16[4,2,4096]{2,1,0:T(2,128)(2,1)S(1)} %reshape.624), channel_id=1, replica_groups=mesh['ctx'=64,'head'=4] {'head'}, dimensions={0} | all-to-all | bytes 131072 | tf_op jit(solution)/shard_map/all_to_all | solution.py:135
  21.8 3.3 all-to-all-start.5
  25.1 12.7 %copy.123 = bf16[2,16,16384]{1,0,2:T(2,128)(2,1)} copy(bf16[2,16,16384]{2,1,0:T(8,128)(2,1)S(1)} %copy-done.6) | data formatting | bytes 2097152 | tf_op args[0]
  37.9 10.9 %reshape.620 = bf16[4,2,65536]{2,1,0:T(2,128)(2,1)} reshape(bf16[16384,2,16]{2,1,0:T(2,128)(2,1)} %bitcast.310) | data formatting | bytes 2097152
  48.8 4.8 all-to-all-start.1
  53.7 12.7 %copy.120 = bf16[2,16,16384]{1,0,2:T(2,128)(2,1)} copy(bf16[2,16,16384]{2,1,0:T(8,128)(2,1)S(1)} %copy-done.7) | data formatting | bytes 2097152 | tf_op args[2]
  66.3 10.9 %reshape.622 = bf16[4,2,65536]{2,1,0:T(2,128)(2,1)} reshape(bf16[16384,2,16]{2,1,0:T(2,128)(2,1)} %bitcast.311) | data formatting | bytes 2097152
  77.3 4.9 all-to-all-start
  83.0 7.2 %reshape.621 = bf16[16384,2,16]{2,1,0:T(2,128)(2,1)} reshape(bf16[4,2,65536]{2,1,0:T(2,128)(2,1)S(1)} %all-to-all-done.1) | data formatting | bytes 2097152
  90.1 16.5 %copy.124 = bf16[2,16,4,4096]{3,1,2,0:T(8,128)(2,1)S(1)} copy(bf16[2,16,4,4096]{1,0,3,2:T(2,128)(2,1)} %bitcast.308) | data formatting | bytes 2097152 | tf_op jit(solution)/shard_map/all_to_all | solution.py:131
  107.4 1.9 collective-permute-start
  111.8 7.2 %reshape.623 = bf16[16384,2,16]{2,1,0:T(2,128)(2,1)} reshape(bf16[4,2,65536]{2,1,0:T(2,128)(2,1)S(1)} %all-to-all-done) | data formatting | bytes 2097152
  119.0 19.1 %copy.145 = bf16[2,16,4,4096]{3,2,1,0:T(4,128)(2,1)S(1)} copy(bf16[2,16,4,4096]{1,0,3,2:T(2,128)(2,1)} %bitcast.309) | data formatting | bytes 2097152 | tf_op jit(solution)/shard_map/all_to_all | solution.py:133
  139.4 2.5 multiply_convert_fusion
  141.9 58.9 %while.51 = (s32[]{:T(128)}, f32[2,16,4096]{2,1,0:T(8,128)S(1)}, f32[2,4096]{1,0:T(2,128)S(1)}, f32[8,8,2,4096]{3,1,0,2:T(8,128)}, f32[8,8,2,4096]{3,2,1,0:T(2,1...) while((s32[]{:T(128)}, f32[2,16,4096]{2,1,0:T(8,128)S(1)}, ...), condition=%wide.region_9.10_spmd.clone, body=%wide.region_0.9_spmd.clone.sunk | while | flops 10469385 | bytes 9039950 | solution.py:175
  202.3 6.7 %copy.135 = bf16[2,16,8192]{1,0,2:T(2,128)(2,1)} copy(bf16[2,16,8192]{2,1,0:T(8,128)(2,1)S(1)} %copy-done.9) | data formatting | bytes 1048576 | tf_op args[9]
  209.0 6.5 %reshape.626 = bf16[4,2,32768]{2,1,0:T(2,128)(2,1)} reshape(bf16[8192,2,16]{2,1,0:T(2,128)(2,1)} %bitcast.314) | data formatting | bytes 1048576
  215.5 4.8 all-to-all-start.4
  220.4 12.7 %copy.131 = bf16[2,16,16384]{1,0,2:T(2,128)(2,1)} copy(bf16[2,16,16384]{2,1,0:T(8,128)(2,1)S(1)} %copy-done.8) | data formatting | bytes 2097152 | tf_op args[1]
  233.0 11.0 %reshape.618 = bf16[4,2,65536]{2,1,0:T(2,128)(2,1)} reshape(bf16[16384,2,16]{2,1,0:T(2,128)(2,1)} %bitcast.312) | data formatting | bytes 2097152
  244.0 5.0 all-to-all-start.2
  249.1 4.1 reshape.627
  253.2 9.1 %copy.136 = bf16[2,16,4,2048]{3,1,2,0:T(8,128)(2,1)S(1)} copy(bf16[2,16,4,2048]{1,0,3,2:T(2,128)(2,1)} %bitcast.313) | data formatting | bytes 1048576 | tf_op jit(solution)/shard_map/all_to_all | solution.py:134
  262.6 2.7 all-to-all-done.2
  265.2 7.1 %reshape.619 = bf16[16384,2,16]{2,1,0:T(2,128)(2,1)} reshape(bf16[4,2,65536]{2,1,0:T(2,128)(2,1)S(1)} %all-to-all-done.2) | data formatting | bytes 2097152
  272.4 18.9 %copy.132 = f32[2,16,4,4096]{3,1,2,0:T(8,128)} copy(bf16[2,16,4,4096]{1,0,3,2:T(2,128)(2,1)} %bitcast.307) | data formatting | bytes 3145728 | tf_op jit(solution)/shard_map/convert_element_type | solution.py:192
  291.2 5.1 neg.169
  296.4 5.1 copy.139
  301.5 5.1 copy.141
  306.7 12.4 %while.50 = (s32[]{:T(128)}, f32[2,2,8,64]{3,2,1,0:T(8,128)S(1)}, f32[2,2,8,64]{3,2,1,0:T(8,128)S(1)}, f32[2,2,8,64,128]{4,3,2,1,0:T(8,128)S(1)}, s32[]{:T(128)}...) while((s32[]{:T(128)}, f32[2,2,8,64]{3,2,1,0:T(8,128)S(1)}, ...), condition=%wide.region_18.19_spmd, body=%wide.region_13.18_spmd.sunk | while | flops 551064128 | bytes 16519977 | solution.py:230
  306.7 5.9 conditional.2
  306.8 1.8 fusion
  310.1 2.6 fusion.6
  312.7 5.9 conditional.2
  312.8 1.9 fusion
  316.1 2.6 fusion.6
  320.9 25.2 %all-gather.6.cloned.1.call-done = f32[64,2,16,4096]{3,2,1,0:T(8,128)} async-done(((f32[1,2,16,4096]{3,2,1,0:T(8,128)}), f32[64,2,16,4096]{3,2,1,0:T(8,128)}) %all-gather.6.cloned.1.call-update) | async-done | bytes 33554448 | tf_op jit(solution)/shard_map/all_gather | solution.py:22
  346.2 142.1 %all-gather.12.cloned.1.call-done = f32[128,16,4096]{2,1,0:T(8,128)} async-done(((f32[2,16,4096]{2,1,0:T(8,128)}), f32[128,16,4096]{2,1,0:T(8,128)}) %all-gather.12.cloned.1.call-update) | async-done | bytes 33554448 | tf_op jit(solution)/shard_map/all_gather | solution.py:22
  488.3 105.7 %while.52 = (s32[]{:T(128)}, f32[2,16,4096]{2,1,0:T(8,128)S(1)}, s32[]{:T(128)}, f32[64,2,16,4096]{3,2,1,0:T(8,128)}, f32[64,2,16,4096]{3,2,1,0:T(8,128)}, /*index=5*/s32[]{:T(128)}, s32[]{:T(128)}) while((s32[]{:T(128)}, f32[2,16,4096]{2,1,0:T(8,128)S(1)}, s32[]{:T(128)}, f32[64,2,16,4096]{3,2,1,0:T(8,128)}, ...), condition=%wide.region_11.12_spmd.clone, body=%wide.region_10.11_spmd.clone.sunk | while | flops 524292 | bytes 2097253 | solution.py:31
  490.0 1.7 fusion.132
  491.7 1.7 fusion.132
  493.4 1.7 fusion.132
  495.0 1.7 fusion.132
  496.7 1.7 fusion.132
  498.4 1.7 fusion.132
  501.7 1.7 fusion.132
  503.4 1.7 fusion.132
  505.1 1.7 fusion.132
  508.5 1.7 fusion.132
  510.1 1.7 fusion.132
  511.8 1.7 fusion.132
  515.2 1.7 fusion.132
  516.8 1.7 fusion.132
  518.5 1.7 fusion.132
  521.9 1.7 fusion.132
  523.6 1.7 fusion.132
  525.2 1.7 fusion.132
  526.9 1.7 fusion.132
  528.6 1.7 fusion.132
  530.3 1.7 fusion.132
  533.6 1.7 fusion.132
  535.3 1.7 fusion.132
  594.0 13.4 %multiply_reduce_fusion.8 = f32[64,2,4096]{2,1,0:T(2,128)S(1)} fusion(f32[2,16,4096]{2,1,0:T(8,128)S(1)} %get-tuple-element.472, f32[16,4096]{1,0:T(8,128)S(1)} %get-tuple-element.1256, f32[64,2,4096]{2,1,0:T(2,128)} %bitcast.327, f32[64,2,16]{2,1,0:T(2,128)S(1)} %copy.129), kind=kLoop, calls=%fused_computation.186 | loop fusion | flops 33030144 | bytes 4988928 | tf_op jit(solution)/shard_map/reduce_sum | solution.py:184
  607.4 2.7 bitcast_select_fusion.1
  (443 shorter events, 140.8 us)
Async XLA Ops:
  7.2 13.1 %copy-start.14 = (bf16[2,16,1024]{2,1,0:T(8,128)(2,1)S(1)}, bf16[2,16,1024]{2,1,0:T(8,128)(2,1)}, u32[]{:S(2)}) copy-start(bf16[2,16,1024]{2,1,0:T(8,128)(2,1)} %param.32) | copy-start | bytes 196612
  7.2 18.0 %copy-start.6 = (bf16[2,16,16384]{2,1,0:T(8,128)(2,1)S(1)}, bf16[2,16,16384]{2,1,0:T(8,128)(2,1)}, u32[]{:S(2)}) copy-start(bf16[2,16,16384]{2,1,0:T(8,128)(2,1)} %param.21) | copy-start | bytes 3145732
  7.2 289.2 %all-gather.8.cloned.1.call-start = ((), (), s32[]{:S(2)}) async-start(), calls=%async_computation.7 | async-start | bytes 4259840 | tf_op jit(solution)/shard_map/all_gather | solution.py:204
  21.8 27.0 %all-to-all-start.5 = ((bf16[4,2,4096]{2,1,0:T(2,128)(2,1)}), bf16[4,2,4096]{2,1,0:T(2,128)(2,1)S(1)}, u32[]{:S(2)}, u32[]{:S(2)}) async-start(bf16[4,2,4096]{2,1,0:T(2,128)(2,1)} %reshape.628), calls=%async_computation.5 | async-start | bytes 131072 | tf_op jit(solution)/shard_map/all_to_all | solution.py:136
  48.8 4.9 copy-start.7
  48.8 28.5 %all-to-all-start.1 = ((bf16[4,2,65536]{2,1,0:T(2,128)(2,1)}), bf16[4,2,65536]{2,1,0:T(2,128)(2,1)S(1)}, u32[]{:S(2)}, u32[]{:S(2)}) async-start(bf16[4,2,65536]{2,1,0:T(2,128)(2,1)} %reshape.620), calls=%async_computation.1 | async-start | bytes 2097152 | tf_op jit(solution)/shard_map/all_to_all | solution.py:131
  77.3 4.9 copy-start.15
  77.3 34.5 %all-to-all-start = ((bf16[4,2,65536]{2,1,0:T(2,128)(2,1)}), bf16[4,2,65536]{2,1,0:T(2,128)(2,1)S(1)}, u32[]{:S(2)}, u32[]{:S(2)}) async-start(bf16[4,2,65536]{2,1,0:T(2,128)(2,1)} %reshape.622), calls=%async_computation | async-start | bytes 2097152 | tf_op jit(solution)/shard_map/all_to_all | solution.py:133
  82.2 219.3 %all-gather.10.cloned.1.call-start = ((), (), s32[]{:S(2)}) async-start(), calls=%async_computation.8 | async-start | bytes 4259840 | tf_op jit(solution)/shard_map/all_gather | solution.py:205
  90.1 19.2 %copy-start.17 = (bf16[2,64,32]{1,2,0:T(8,128)(2,1)S(1)}, bf16[2,64,32]{1,2,0:T(8,128)(2,1)}, u32[]{:S(2)}) copy-start(bf16[2,64,32]{1,2,0:T(8,128)(2,1)} %param.24) | copy-start | bytes 24580
  90.1 19.3 %copy-start.10 = (f32[16,4096]{1,0:T(8,128)S(1)}, f32[16,4096]{1,0:T(8,128)}, u32[]{:S(2)}) copy-start(f32[16,4096]{1,0:T(8,128)} %param.28) | copy-start | bytes 786436
  106.7 12.3 %copy-start.3 = (bf16[2,16,4,4096]{3,1,2,0:T(8,128)(2,1)}, bf16[2,16,4,4096]{3,1,2,0:T(8,128)(2,1)S(1)}, u32[]{:S(2)}) copy-start(bf16[2,16,4,4096]{3,1,2,0:T(8,128)(2,1)S(1)} %copy.124) | copy-start | bytes 3145732
  107.4 31.3 %collective-permute-start = (bf16[2,3,4096]{2,1,0:T(4,128)(2,1)}, bf16[2,3,4096]{2,1,0:T(4,128)(2,1)}, u32[]{:S(2)}, u32[]{:S(2)}) collective-permute-start(bf16[2,3,4096]{2,1,0:T(4,128)(2,1)} %slice.220), channel_id=1, source_target_pairs={{0,4},{4,8},{8,12},{12,16},{16,20},{20,24},{24,28},{28,32},{32,36}... | collective-permute-start | bytes 147464 | tf_op jit(solution)/shard_map/ppermute | solution.py:17
  111.6 234.6 %all-gather.6.cloned.1.call-start = ((), (), s32[]{:S(2)}) async-start(), calls=%async_computation.6 | async-start | bytes 34078720 | tf_op jit(solution)/shard_map/all_gather | solution.py:22
  138.1 1.2 copy-start.4
  138.1 1.2 dynamic-slice-start
  138.2 1.2 copy-start.11
  138.2 1.2 copy-start.12
  138.2 1.2 copy-start.13
  138.2 3.7 copy-start.1
  200.8 1.0 copy-start
  200.8 1.5 copy-start.9
  201.7 286.6 %all-gather.12.cloned.1.call-start = ((), (), s32[]{:S(2)}) async-start(), calls=%async_computation.9 | async-start | bytes 34078720 | tf_op jit(solution)/shard_map/all_gather | solution.py:22
  209.0 11.4 %copy-start.8 = (bf16[2,16,16384]{2,1,0:T(8,128)(2,1)S(1)}, bf16[2,16,16384]{2,1,0:T(8,128)(2,1)}, u32[]{:S(2)}) copy-start(bf16[2,16,16384]{2,1,0:T(8,128)(2,1)} %param.22) | copy-start | bytes 3145732
  215.5 28.4 %all-to-all-start.4 = ((bf16[4,2,32768]{2,1,0:T(2,128)(2,1)}), bf16[4,2,32768]{2,1,0:T(2,128)(2,1)S(1)}, u32[]{:S(2)}, u32[]{:S(2)}) async-start(bf16[4,2,32768]{2,1,0:T(2,128)(2,1)} %reshape.626), calls=%async_computation.4 | async-start | bytes 1048576 | tf_op jit(solution)/shard_map/all_to_all | solution.py:134
  244.0 5.1 copy-start.18
  244.0 21.3 %all-to-all-start.2 = ((bf16[4,2,65536]{2,1,0:T(2,128)(2,1)}), bf16[4,2,65536]{2,1,0:T(2,128)(2,1)S(1)}, u32[]{:S(2)}, u32[]{:S(2)}) async-start(bf16[4,2,65536]{2,1,0:T(2,128)(2,1)} %reshape.618), calls=%async_computation.2 | async-start | bytes 2097152 | tf_op jit(solution)/shard_map/all_to_all | solution.py:132
  594.0 13.4 %copy-start.2 = (f32[2,16,4,4096]{3,1,2,0:T(8,128)S(1)}, f32[2,16,4,4096]{3,1,2,0:T(8,128)}, u32[]{:S(2)}) copy-start(f32[2,16,4,4096]{3,1,2,0:T(8,128)} %copy.132) | copy-start | bytes 6291460
  594.0 13.4 %copy-start.5 = (f32[8,8,2,4096]{3,1,0,2:T(8,128)S(1)}, f32[8,8,2,4096]{3,1,0,2:T(8,128)}, u32[]{:S(2)}) copy-start(f32[8,8,2,4096]{3,1,0,2:T(8,128)} %get-tuple-element.468) | copy-start | bytes 6291460
  594.0 13.4 %copy-start.16 = (f32[4096]{0:T(1024)S(1)}, f32[4096]{0:T(1024)}, u32[]{:S(2)}) copy-start(f32[4096]{0:T(1024)} %param.29) | copy-start | bytes 49156
Sparse Core Ops, SparseCore 0:
  20.4 78.7 all-gather.7
  111.7 81.9 all-gather.9
  201.8 144.3 all-gather.5
  348.8 139.4 all-gather.11
where the time goes:
time: 625 us; the launch traced here: 617 us
  local copies, waits for them, and re-layouts  220 us (35%)
  waiting for transfers between devices  171 us (27%)
  other arithmetic  165 us (26%)
  starting transfers between devices  25 us (4%)
  between operations  14.2 us (2%)
  blocking collectives  9.89 us (2%)
  matrix products  8.83 us (1%)
    all_gather x2, waiting for transfers between devices, carried_in(): pieces = jax.tree.map(lambda part: lax.all_gather(part, axis), value)  167 us
    unnamed x57, local copies, waits for them, and re-layouts  114 us
    select_n x63, other arithmetic, step(): jnp.where(position < mine, new, old)  104 us
    reduce_sum x24, other arithmetic, advance(): jnp.sum(proj_row[:, state_count:, None] * state_now, axis=1)  20.5 us
    all_to_all x2, local copies, waits for them, and re-layouts, shards(): lax.all_to_all(step_input, 'head', split_axis=2, concat_axis=1, tiled=True)  19.7 us
    convert_element_type x1, local copies, waits for them, and re-layouts, shards(): jnp.swapaxes(gate_local, 0, 1).astype(jnp.float32)  18.9 us
    all_to_all x1, local copies, waits for them, and re-layouts, shards(): lax.all_to_all(mixer_input, 'head', split_axis=2, concat_axis=1, tiled=True)  16.5 us
    reduce_sum x1, other arithmetic, shards(): jnp.sum(readout_time[:, :, :, None] * jnp.exp(-elapsed_time[:, :, None, :...  13.4 us
  transfers between devices with their start and end apart: 10, of which 3 were waited for; matrix products, arithmetic and copies ran while one was open for 44% of the time, Pallas kernels for 0%

commit v1 on v0

v1 whole, which is shorter than its diff:
```python
import functools
import math

import jax
import jax.numpy as jnp
from jax import lax
from jax.experimental import pallas as pl
from jax.experimental.pallas import tpu as pltpu
from jax.sharding import Mesh, PartitionSpec as P

HD = 128
LANES = 128
PIECES = 8
ROWS = 16
SPAN = PIECES * ROWS
WIDE = 1024
NST = 16
MSG = 24
LOG2E = math.log2(math.e)
neg_large = -1e30

F32 = jnp.float32
BF16 = jnp.bfloat16


def silu(v):
    return v / (1.0 + jnp.exp(-v))


def softplus(v):
    z = jnp.exp(-jnp.abs(v))
    u = 1.0 + z
    small = jnp.where(u == 1.0, z, jnp.log(u) * (z / jnp.where(u == 1.0, 1.0, u - 1.0)))
    return jnp.maximum(v, 0.0) + small


def row_of(ref, row):
    return jnp.broadcast_to(ref[0, pl.ds(row, 1), :], (8, LANES))


def first_pass(order, *refs):
    pieces = refs[:PIECES]
    tail, params, rate, inflow, dt_out, conv_out, msg_out, xf, sf, tmp = refs[PIECES:]
    for d in range(PIECES):
        at = pl.multiple_of(order[d] * ROWS, ROWS)
        xf[pl.ds(8 + at, ROWS), :] = pieces[d][0, 0].astype(F32)
        sf[pl.ds(at, ROWS), :] = pieces[d][1, 0].astype(F32)
    xf[5:8, :] = tail[0].astype(F32)
    for j in range(8):
        cols = slice(j * LANES, (j + 1) * LANES)
        acc = jnp.broadcast_to(params[4:5, cols], (SPAN, LANES))
        for k in range(4):
            acc = acc + xf[5 + k : 5 + k + SPAN, cols] * params[k : k + 1, cols]
        conv_out[0, 0, pl.ds(j, SPAN, stride=8), :] = silu(acc).astype(BF16).astype(F32)
        dt_out[0, 0, pl.ds(j, SPAN, stride=8), :] = softplus(sf[:, cols] + params[5:6, cols])
    rates = [rate[0, n] for n in range(NST)]

    def step(t, carry):
        states, elapsed = carry
        dt = dt_out[0, 0, pl.ds(pl.multiple_of(t * 8, 8), 8), :]
        u = dt * conv_out[0, 0, pl.ds(pl.multiple_of(t * 8, 8), 8), :]
        new = []
        for n in range(NST):
            new.append(jnp.exp2(dt * rates[n]) * states[n] + u * row_of(inflow, t * NST + n))
        return tuple(new), elapsed + dt

    zero = jnp.zeros((8, LANES), F32)
    states, elapsed = lax.fori_loop(0, SPAN, step, ((zero,) * NST, zero), unroll=2)
    for n in range(NST):
        tmp[pl.ds(n, 8, stride=MSG), :] = states[n]
    high = elapsed.astype(BF16).astype(F32)
    rest = elapsed - high
    middle = rest.astype(BF16).astype(F32)
    for n, part in enumerate((high, middle, rest - middle, zero, zero, zero, zero, zero)):
        tmp[pl.ds(NST + n, 8, stride=MSG), :] = part
    for j in range(8):
        msg_out[j] = tmp[j * MSG : (j + 1) * MSG, :].astype(BF16)


def prefix_pass(msg, rate, out):
    rates = rate[...]
    state = jnp.zeros((NST, LANES), F32)
    for s in range(msg.shape[0]):
        out[s] = state.astype(BF16)
        part = msg[s].astype(F32)
        elapsed = part[NST : NST + 1] + part[NST + 1 : NST + 2] + part[NST + 2 : NST + 3]
        state = jnp.exp2(rates * elapsed) * state + part[:NST]


def second_pass(order, *refs):
    gates = refs[:PIECES]
    dt_in, conv_in, params, rate, inflow, readout, entering, live, out, gf, ys, tmp = refs[PIECES:]
    for d in range(PIECES):
        at = pl.multiple_of(order[d] * ROWS, ROWS)
        gf[pl.ds(at, ROWS), :] = gates[d][0, 0].astype(F32)
    for j in range(8):
        tmp[j * NST : (j + 1) * NST, :] = entering[j].astype(F32)
    rates = [rate[0, n] for n in range(NST)]

    def step(t, states):
        dt = dt_in[0, 0, pl.ds(pl.multiple_of(t * 8, 8), 8), :]
        u = dt * conv_in[0, 0, pl.ds(pl.multiple_of(t * 8, 8), 8), :]
        new = []
        total = [None] * 4
        for n in range(NST):
            s = jnp.exp2(dt * rates[n]) * states[n] + u * row_of(inflow, t * NST + n)
            new.append(s)
            term = s * row_of(readout, t * NST + n)
            total[n % 4] = term if total[n % 4] is None else total[n % 4] + term
        ys[pl.ds(pl.multiple_of(t * 8, 8), 8), :] = (total[0] + total[1]) + (total[2] + total[3])
        return tuple(new)

    start = tuple(tmp[pl.ds(n, 8, stride=NST), :] for n in range(NST))
    lax.fori_loop(0, SPAN, step, start, unroll=2)
    rows = order[PIECES] + lax.broadcasted_iota(jnp.int32, (SPAN, LANES), 0)
    keep = rows < live[pl.program_id(1)]
    for j in range(8):
        cols = slice(j * LANES, (j + 1) * LANES)
        conv = conv_in[0, 0, pl.ds(j, SPAN, stride=8), :]
        mixed = ys[pl.ds(j, SPAN, stride=8), :] + params[6:7, cols] * conv
        gated = mixed * silu(gf[:, cols])
        out[0, :, cols] = jnp.where(keep, gated, 0.0).astype(BF16)


def pack_pass(q, k, v, out):
    for i in range(16):
        b, kvl, y = i // 8, (i // 4) % 2, i % 4
        g = 2 * y + kvl
        out[i, :, :1024] = q[b, :, g * 1024 : (g + 1) * 1024]
        out[i, :, 1024:1152] = k[b, :, g * HD : (g + 1) * HD]
        out[i, :, 1152:1280] = v[b, :, g * HD : (g + 1) * HD]


def attend_pass(info, q_ref, kv_ref, out):
    z, core, live = info[0], info[1], info[2]
    qs = q_ref[...].reshape(256, HD)
    factor = LOG2E / math.sqrt(HD)

    def block(zz, carry, masked):
        peak, divisor, acc = carry
        kv = kv_ref[pl.ds(zz * 2, 2)].reshape(512, 256)
        keys, values = kv[:, :HD], kv[:, HD:]
        scores = lax.dot_general(keys, qs, (((1,), (1,)), ((), ())), preferred_element_type=F32) * factor
        if masked:
            kr = lax.broadcasted_iota(jnp.int32, (512, 256), 0)
            qr = lax.broadcasted_iota(jnp.int32, (512, 256), 1)
            kp = ((kr // 64) % 4) * 128 + (kr // 256) * 64 + kr % 64
            qp = (qr // 64) * 128 + core * 64 + qr % 64
            scores = jnp.where(kp <= qp, scores, neg_large)
        new_peak = jnp.maximum(peak, jnp.max(scores, axis=0, keepdims=True))
        weights = jnp.exp2(scores - new_peak)
        fade = jnp.exp2(peak - new_peak)
        divisor = divisor * fade + jnp.sum(weights, axis=0, keepdims=True)
        update = lax.dot_general(
            values, weights.astype(BF16), (((0,), (0,)), ((), ())), preferred_element_type=F32
        )
        return new_peak, divisor, acc * fade + update

    start = (jnp.full((1, 256), neg_large, F32), jnp.zeros((1, 256), F32), jnp.zeros((HD, 256), F32))
    carry = lax.fori_loop(0, z, lambda zz, c: block(zz, c, False), start)
    _, divisor, acc = block(z, carry, True)
    result = jnp.transpose(acc / divisor)
    r = lax.broadcasted_iota(jnp.int32, (256, HD), 0)
    pos = z * 512 + (r // 64) * 128 + core * 64 + r % 64
    out[...] = jnp.where(pos < live, result, 0.0).astype(BF16).reshape(4, 64, HD)


def shards(
    mixer_input,
    gate_input,
    step_input,
    state_proj,
    conv_weight,
    conv_bias,
    step_bias,
    decay_log,
    skip_gain,
    query_states,
    key_states,
    value_states,
    lengths,
):
    z, x, core, head = (lax.axis_index(name) for name in ("z", "x", "core", "head"))
    nz, nx = lax.axis_size("z"), lax.axis_size("x")
    group = ("core", "head")
    half = decay_log.shape[1] // 2
    quarter = decay_log.shape[1]
    vmem = pl.BlockSpec(memory_space=pltpu.VMEM)

    packed = pl.pallas_call(
        pack_pass,
        out_shape=jax.ShapeDtypeStruct((16, ROWS, 1280), BF16),
        in_specs=[vmem] * 3,
        out_specs=vmem,
    )(query_states, key_states, value_states)

    def piece_for(to_core, to_head):
        at = to_head * quarter + to_core * half
        return jnp.stack(
            [
                lax.dynamic_slice_in_dim(part, at, half, 2)
                for part in (mixer_input, step_input, gate_input)
            ]
        )

    pieces, order = [], []
    for dc in range(2):
        for dh in range(4):
            block = piece_for(core ^ dc, (head + dh) % 4)
            route = [
                (c * 4 + h, (c ^ dc) * 4 + (h + dh) % 4) for c in range(2) for h in range(4)
            ]
            pieces.append(block if dc + dh == 0 else lax.ppermute(block, group, route))
            order.append((core ^ dc) * 4 + (head - dh) % 4)
    last = sum(
        jnp.where(order[d] == PIECES - 1, pieces[d][0, :, ROWS - 3 :, :], jnp.zeros((), BF16))
        for d in range(PIECES)
    )
    chips = nz * nx
    tail = lax.ppermute(last, ("z", "x"), [(i, i + 1) for i in range(chips - 1)])

    received = lax.all_to_all(packed, ("x", "head"), 0, 0, tiled=True)
    received = received.reshape(4, 64, 1280)
    kv_own = received[:, :, 1024:].reshape(1, 256, 256)
    kv_all = lax.all_gather(kv_own, ("z", "core"), axis=0, tiled=True)

    other = lax.ppermute(state_proj, "core", [(0, 1), (1, 0)])
    first = jnp.where(core == 0, state_proj, other)
    second = jnp.where(core == 0, other, state_proj)
    proj = jnp.concatenate([first, second], axis=1).astype(F32)
    inflow = jnp.broadcast_to(proj[:, :, :NST, None], (2, SPAN, NST, LANES)).reshape(2, SPAN * NST, LANES)
    readout = jnp.broadcast_to(proj[:, :, NST:, None], (2, SPAN, NST, LANES)).reshape(2, SPAN * NST, LANES)
    mine = lambda part, dim: lax.dynamic_slice_in_dim(part, core * half, half, dim)
    whole = lambda part, dim: lax.dynamic_slice_in_dim(part, head * quarter + core * half, half, dim)
    params = jnp.concatenate(
        [
            whole(conv_weight, 1).astype(F32),
            whole(conv_bias, 0)[None],
            mine(step_bias, 0)[None],
            mine(skip_gain, 0)[None],
            jnp.zeros((1, half), F32),
        ]
    )
    rate_rows = -LOG2E * jnp.exp(mine(decay_log, 1))
    rate = jnp.transpose(rate_rows.reshape(NST, 2, 8, LANES), (1, 0, 2, 3))
    start_row = (z * nx + x) * SPAN
    order = jnp.stack(order + [start_row]).astype(jnp.int32)

    blk = lambda arrays, which: pl.BlockSpec(
        (arrays, 1, ROWS, WIDE), lambda c, b, o: (which, b, 0, c)
    )
    slab = pl.BlockSpec((1, 1, SPAN * 8, LANES), lambda c, b, o: (b, c, 0, 0))
    params_spec = pl.BlockSpec((8, WIDE), lambda c, b, o: (0, c))
    rate_spec = pl.BlockSpec((1, NST, 8, LANES), lambda c, b, o: (c, 0, 0, 0))
    flow_spec = pl.BlockSpec((1, SPAN * NST, LANES), lambda c, b, o: (b, 0, 0))
    slab_shape = jax.ShapeDtypeStruct((2, 2, SPAN * 8, LANES), F32)
    dt, conv, message = pl.pallas_call(
        first_pass,
        grid_spec=pltpu.PrefetchScalarGridSpec(
            num_scalar_prefetch=1,
            grid=(2, 2),
            in_specs=[blk(2, 0)] * PIECES
            + [
                pl.BlockSpec((1, 3, WIDE), lambda c, b, o: (b, 0, c)),
                params_spec,
                rate_spec,
                flow_spec,
            ],
            out_specs=[
                slab,
                slab,
                pl.BlockSpec((8, MSG, LANES), lambda c, b, o: (b * 2 + c, 0, 0)),
            ],
            scratch_shapes=[
                pltpu.VMEM((SPAN + 8, WIDE), F32),
                pltpu.VMEM((SPAN, WIDE), F32),
                pltpu.VMEM((8 * MSG, LANES), F32),
            ],
        ),
        out_shape=[slab_shape, slab_shape, jax.ShapeDtypeStruct((32, MSG, LANES), BF16)],
        name="first_pass",
    )(order, *pieces, tail, params, rate, inflow)

    sections = lax.all_to_all(message, ("z", "x"), 0, 0, tiled=True)
    chunk = (z * nx + x) % 16
    rate_chunk = lax.dynamic_slice_in_dim(rate_rows, chunk * LANES, LANES, 1)
    prefix = pl.pallas_call(
        prefix_pass,
        out_shape=jax.ShapeDtypeStruct((32, NST, LANES), BF16),
        in_specs=[vmem] * 2,
        out_specs=vmem,
        name="prefix_pass",
    )(sections, rate_chunk)
    entering = lax.all_to_all(prefix, ("z", "x"), 0, 0, tiled=True)

    mixed = pl.pallas_call(
        second_pass,
        grid_spec=pltpu.PrefetchScalarGridSpec(
            num_scalar_prefetch=1,
            grid=(2, 2),
            in_specs=[blk(1, 2)] * PIECES
            + [
                slab,
                slab,
                params_spec,
                rate_spec,
                flow_spec,
                flow_spec,
                pl.BlockSpec((8, NST, LANES), lambda c, b, o: (b * 2 + c, 0, 0)),
                pl.BlockSpec(memory_space=pltpu.SMEM),
            ],
            out_specs=pl.BlockSpec((1, SPAN, WIDE), lambda c, b, o: (b, 0, c)),
            scratch_shapes=[
                pltpu.VMEM((SPAN, WIDE), F32),
                pltpu.VMEM((SPAN * 8, LANES), F32),
                pltpu.VMEM((8 * NST, LANES), F32),
            ],
        ),
        out_shape=jax.ShapeDtypeStruct((2, SPAN, half), BF16),
        name="second_pass",
    )(order, *pieces, dt, conv, params, rate, inflow, readout, entering, lengths)

    rows = SPAN // 2
    own = lax.dynamic_slice_in_dim(mixed, core * rows, rows, 1)
    away = lax.dynamic_slice_in_dim(mixed, (1 - core) * rows, rows, 1)
    back = lax.ppermute(away, "core", [(0, 1), (1, 0)])
    mixer_output = jnp.concatenate(
        [jnp.where(core == 0, own, back), jnp.where(core == 0, back, own)], axis=2
    )

    info = jnp.stack([z, core, lax.dynamic_index_in_dim(lengths, x // 2, 0, keepdims=False)])
    attended = pl.pallas_call(
        attend_pass,
        grid_spec=pltpu.PrefetchScalarGridSpec(
            num_scalar_prefetch=1,
            grid=(8,),
            in_specs=[
                pl.BlockSpec((4, 64, HD), lambda h, i: (0, 0, h)),
                pl.BlockSpec((16, 256, 256), lambda h, i: (0, 0, 0)),
            ],
            out_specs=pl.BlockSpec((4, 64, HD), lambda h, i: (0, 0, h)),
        ),
        out_shape=jax.ShapeDtypeStruct((4, 64, 1024), BF16),
        name="attend_pass",
    )(info.astype(jnp.int32), received, kv_all)
    home = lax.all_to_all(attended, "x", 0, 0, tiled=True)
    attention_output = jnp.stack(
        [
            jnp.concatenate([home[0], home[1]], axis=1),
            jnp.concatenate([home[2], home[3]], axis=1),
        ]
    )
    return (mixer_output, attention_output)


def solution(mesh):
    ctx = ("z", "x", "core")
    split = Mesh(mesh.devices.reshape(8, 4, 2, 4), ctx + ("head",))
    rows = P(None, ctx + ("head",), None)
    in_specs = (
        rows,
        rows,
        rows,
        P(None, ctx, None),
        P(),
        P(),
        P("head"),
        P(None, "head"),
        P("head"),
        rows,
        rows,
        rows,
        P(),
    )
    out_specs = (P(None, ctx, "head"), P(None, ctx, "head"))
    return jax.shard_map(shards, mesh=split, in_specs=in_specs, out_specs=out_specs, check_vma=False)
```

time: 625 us -> 207 us (0.33)
  the two profiles are of different devices: /device:TPU:32 before, /device:TPU:224 now
where the time goes in v1:
time: 207 us; the launch traced here: 206 us
  Pallas kernels  71.9 us (35%)
  waiting for transfers between devices  47.3 us (23%)
  starting transfers between devices  37.4 us (18%)
  local copies, waits for them, and re-layouts  17.6 us (9%)
  other arithmetic  17.5 us (8%)
  between operations  14.5 us (7%)
    pallas_call x1, Pallas kernels, shards(): pl.pallas_call(attend_pass, grid_spec=pltpu.PrefetchScalarGridSpec(num_sc...  38.4 us
    pallas_call x1, Pallas kernels, shards(): pl.pallas_call(second_pass, grid_spec=pltpu.PrefetchScalarGridSpec(num_sc...  15 us
    pallas_call x1, Pallas kernels, shards(): pl.pallas_call(first_pass, grid_spec=pltpu.PrefetchScalarGridSpec(num_sca...  14.9 us
    ppermute x7, starting transfers between devices, shards(): pieces.append(block if dc + dh == 0 else lax.ppermute(block, group, route))  10.7 us
    all_to_all x1, waiting for transfers between devices, shards(): home = lax.all_to_all(attended, 'x', 0, 0, tiled=True)  9.31 us
    ppermute x7, waiting for transfers between devices, shards(): pieces.append(block if dc + dh == 0 else lax.ppermute(block, group, route))  8.96 us
    all_to_all x1, waiting for transfers between devices, shards(): received = lax.all_to_all(packed, ('x', 'head'), 0, 0, tiled=True)  8.39 us
    another operation x8, other arithmetic, piece_for(): jnp.stack([lax.dynamic_slice_in_dim(part, at, half, 2) for part in (mixer...  8.23 us
  transfers between devices with their start and end apart: 15, of which 6 were waited for; matrix products, arithmetic and copies ran while one was open for 14% of the time, Pallas kernels for 16%

profile of v1, /device:TPU:224, one launch (start us, length us, event | category | flops | bytes accessed | tf_op | source)
XLA Modules:
  0.0 206.1 jit_solution(14147491728101037681)
XLA Ops:
  7.3 2.2 %dynamic-slice_bitcast_fusion.2 = (bf16[1,2,16,2048]{3,2,1,0:T(8,128)(2,1)S(1)}, bf16[1,2,16,2048]{3,2,1,0:T(8,128)(2,1)S(1)}, bf16[1,2,16,2048]{3,2,1,0:T(8,128...) fusion(bf16[2,16,16384]{2,1,0:T(8,128)(2,1)} %param.13, ...), kind=kLoop, calls=%fused_computation.22 | loop fusion | bytes 2097184 | tf_op jit(solution)/shard_map/stack | solution.py:199
  9.5 1.1 dynamic-slice_bitcast_fusion
  10.5 0.8 pad_maximum_fusion.3
  11.3 1.6 collective-permute-start
  12.9 0.8 pad_maximum_fusion.4
  13.7 2.9 %collective-permute-start.1 = (bf16[3,2,16,2048]{3,2,1,0:T(8,128)(2,1)}, bf16[3,2,16,2048]{3,2,1,0:T(8,128)(2,1)S(1)}, u32[]{:S(2)}, u32[]{:S(2)}) collective-permute-start(bf16[3,2,16,2048]{3,2,1,0:T(8,128)(2,1)} %pad_maximum_fusion.4), channel_id=1, source_target_pairs={{0,2},{1,3},{2,0},{3,1},{4,6},{5,7},{6,4},{7,5},{8,10},{9,11},{10,... | collective-permute-start | bytes 1179656 | tf_op jit(solution)/shard_map/ppermute | solution.py:213
  16.6 2.0 shard_map.140
  18.6 5.3 %all-to-all-start.2 = ((bf16[16,16,1280]{2,1,0:T(8,128)(2,1)}), bf16[16,16,1280]{2,1,0:T(8,128)(2,1)S(1)}, u32[]{:S(2)}, u32[]{:S(2)}) async-start(bf16[16,16,1280]{2,1,0:T(8,128)(2,1)} %shard_map.140), calls=%async_computation.2 | async-start | bytes 1310720 | tf_op jit(solution)/shard_map/all_to_all | solution.py:222
  23.9 0.0 all-gather.2.cloned.1.call-start
  24.0 0.8 pad_maximum_fusion.5
  24.8 3.1 %collective-permute-start.2 = (bf16[3,2,16,2048]{3,2,1,0:T(8,128)(2,1)}, bf16[3,2,16,2048]{3,2,1,0:T(8,128)(2,1)S(1)}, u32[]{:S(2)}, u32[]{:S(2)}) collective-permute-start(bf16[3,2,16,2048]{3,2,1,0:T(8,128)(2,1)} %pad_maximum_fusion.5), channel_id=1, source_target_pairs={{0,3},{1,0},{2,1},{3,2},{4,7},{5,4},{6,5},{7,6},{8,11},{9,8},{10,9... | collective-permute-start | bytes 1179656 | tf_op jit(solution)/shard_map/ppermute | solution.py:213
  27.9 1.7 pad_maximum_fusion.6
  29.6 0.5 collective-permute-start.8
  30.2 1.8 pad_maximum_fusion.2.refs_0_
  31.9 8.4 %all-to-all-done.2 = bf16[16,16,1280]{2,1,0:T(8,128)(2,1)S(1)} async-done(((bf16[16,16,1280]{2,1,0:T(8,128)(2,1)}), bf16[16,16,1280]{2,1,0:T(8,128)(2,1)S(1)}, u32[]{:S(2)}, u32[]{:S(2)}) %all-to-all-start.2) | async-done | bytes 655392 | tf_op jit(solution)/shard_map/all_to_all | solution.py:222
  40.3 0.7 slice.70
  41.0 0.0 all-gather.2.cloned.1.call-update
  41.1 0.8 pad_maximum_fusion.7
  41.9 0.8 pad_maximum_fusion.8
  42.6 0.8 pad_maximum_fusion.9
  43.4 1.3 dynamic-slice_convert_fusion
  44.8 2.1 %collective-permute-start.5 = (bf16[3,2,16,2048]{3,2,1,0:T(8,128)(2,1)}, bf16[3,2,16,2048]{3,2,1,0:T(8,128)(2,1)S(1)}, u32[]{:S(2)}, u32[]{:S(2)}) collective-permute-start(bf16[3,2,16,2048]{3,2,1,0:T(8,128)(2,1)} %pad_maximum_fusion.8), channel_id=1, source_target_pairs={{0,6},{1,7},{2,4},{3,5},{4,2},{5,3},{6,0},{7,1},{8,14},{9,15},{10,... | collective-permute-start | bytes 1179656 | tf_op jit(solution)/shard_map/ppermute | solution.py:213
  46.9 0.9 collective-permute-start.6
  47.8 1.6 fusion.9
  49.4 0.7 dynamic_slice.126
  50.1 1.3 dynamic_slice.127
  51.4 0.9 copy.21
  52.3 0.7 copy.23
  53.0 0.6 broadcast_in_dim.43
  53.6 1.5 concatenate.15.refs_9_.refs_10_
  55.1 0.6 stack.154.order
  55.7 0.7 broadcast_select_fusion.3
  56.4 0.1 maximum_convert_fusion
  56.5 8.9 %collective-permute-done.4.refs_5_ = bf16[3,2,16,2048]{3,2,1,0:T(8,128)(2,1)S(1)} collective-permute-done((bf16[3,2,16,2048]{3,2,1,0:T(8,128)(2,1)}, bf16[3,2,16,2048]{3,2,1,0:T(8,128)(2,1)S(1)}, u32[]{:S(2)}, u32[]{:S(2)}) %collective-permute-start.4) | collective-permute-done | bytes 393248 | tf_op jit(solution)/shard_map/ppermute | solution.py:213
  65.5 1.0 fusion.1
  66.5 3.4 %collective-permute-start.7 = (bf16[2,3,2048]{2,1,0:T(4,128)(2,1)}, bf16[2,3,2048]{2,1,0:T(4,128)(2,1)}, u32[]{:S(2)}, u32[]{:S(2)}) collective-permute-start(bf16[2,3,2048]{2,1,0:T(4,128)(2,1)} %fusion.1), channel_id=1, source_target_pairs={{0,8},{8,16},{16,24},{24,32},{32,40},{40,48},{48,56},{56,64},{64,7... | collective-permute-start | bytes 73736 | tf_op jit(solution)/shard_map/ppermute | solution.py:220
  69.9 0.1 copy.19
  70.0 0.1 broadcast_in_dim.44
  70.1 4.6 %collective-permute-done.7.refs_8_ = bf16[2,3,2048]{2,1,0:T(4,128)(2,1)} collective-permute-done((bf16[2,3,2048]{2,1,0:T(4,128)(2,1)}, bf16[2,3,2048]{2,1,0:T(4,128)(2,1)}, u32[]{:S(2)}, u32[]{:S(2)}) %collective-permute-start.7) | collective-permute-done | bytes 24608 | tf_op jit(solution)/shard_map/ppermute | solution.py:220
  74.7 1.9 broadcast_in_dim.45.refs_11_.refs_12_
  76.7 0.0 copy-start.19
  76.7 14.9 %first_pass.1 = (f32[2,2,1024,128]{3,2,1,0:T(8,128)}, f32[2,2,1024,128]{3,2,1,0:T(8,128)}, bf16[32,24,128]{2,1,0:T(8,128)(2,1)}) custom-call(s32[9]{0:T(128)} %stack.154.order, bf16[3,2,16,2048]{3,2,1,0:T(8,128)(2,1)} %pad_maximum_fusion.2.refs_0_, bf16[3,2,16,2048]{3,2,1,0:T(8,128)(2,1)} %copy-done.1, bf16[3,2,16,2048]{3,2,1,0:T(8,128)(2,1)} %copy-done.2, ...), custom_call_target="tpu_custom_call" | custom-call | tf_op jit(solution)/shard_map/first_pass/pallas_call | solution.py:257
  91.7 7.6 %all-to-all-start = ((bf16[32,24,128]{2,1,0:T(8,128)(2,1)}), bf16[32,24,128]{2,1,0:T(8,128)(2,1)S(1)}, u32[]{:S(2)}, u32[]{:S(2)}) async-start(bf16[32,24,128]{2,1,0:T(8,128)(2,1)} %get-tuple-element.7), calls=%async_computation | async-start | bytes 393216 | tf_op jit(solution)/shard_map/all_to_all | solution.py:284
  99.3 0.6 constant_dynamic-slice_fusion.1.rate
  99.9 8.1 %all-to-all-done.msg = bf16[32,24,128]{2,1,0:T(8,128)(2,1)S(1)} async-done(((bf16[32,24,128]{2,1,0:T(8,128)(2,1)}), bf16[32,24,128]{2,1,0:T(8,128)(2,1)S(1)}, u32[]{:S(2)}, u32[]{:S(2)}) %all-to-all-start) | async-done | bytes 196640 | tf_op jit(solution)/shard_map/all_to_all | solution.py:284
  108.0 0.7 copy-done.10
  108.7 1.7 prefix_pass.1
  110.3 6.4 %all-to-all-start.1 = ((bf16[32,16,128]{2,1,0:T(8,128)(2,1)}), bf16[32,16,128]{2,1,0:T(8,128)(2,1)S(1)}, u32[]{:S(2)}, u32[]{:S(2)}) async-start(bf16[32,16,128]{2,1,0:T(8,128)(2,1)} %prefix_pass.1), calls=%async_computation.1 | async-start | bytes 262144 | tf_op jit(solution)/shard_map/all_to_all | solution.py:294
  116.7 0.1 copy.20
  116.8 0.1 broadcast_in_dim.46
  116.9 7.9 %all-to-all-done.1.refs_14_ = bf16[32,16,128]{2,1,0:T(8,128)(2,1)S(1)} async-done(((bf16[32,16,128]{2,1,0:T(8,128)(2,1)}), bf16[32,16,128]{2,1,0:T(8,128)(2,1)S(1)}, u32[]{:S(2)}, u32[]{:S(2)}) %all-to-all-start.1) | async-done | bytes 131104 | tf_op jit(solution)/shard_map/all_to_all | solution.py:294
  124.8 1.9 broadcast_in_dim.47.refs_13_
  126.7 15.0 %second_pass.1 = bf16[2,128,2048]{2,1,0:T(8,128)(2,1)} custom-call(s32[9]{0:T(128)} %stack.154.order, bf16[3,2,16,2048]{3,2,1,0:T(8,128)(2,1)} %pad_maximum_fusion.2.refs_0_, bf16[3,2,16,2048]{3,2,1,0:T(8,128)(2,1)} %copy-done.1, bf16[3,2,16,2048]{3,2,1,0:T(8,128)(2,1)} %copy-done.2, bf16[3,2,16,2048]{3,2,1,0:T(8,128)(2,1)} %copy-done.3, ...), custom_call_target="tpu_custom_call" | custom-call | tf_op jit(solution)/shard_map/second_pass/pallas_call | solution.py:296
  141.7 1.1 constant_dynamic-slice_fusion
  142.8 0.1 collective-permute-start.9
  142.9 0.6 dynamic_slice.132
  143.5 1.3 pad_add_fusion.info
  144.8 1.3 broadcast_select_fusion.1
  146.1 0.0 all-gather.2.cloned.1.call-done.kv_ref
  146.1 38.4 %attend_pass.1 = bf16[4,64,1024]{2,1,0:T(8,128)(2,1)} custom-call(s32[3]{0:T(128)} %pad_add_fusion.info, bf16[4,64,1280]{2,1,0:T(8,128)(2,1)} %bitcast.86, bf16[16,256,256]{2,1,0:T(8,128)(2,1)} %all-gather.2.cloned.1.call-done.kv_ref), custom_call_target="tpu_custom_call" | custom-call | tf_op jit(solution)/shard_map/attend_pass/pallas_call | solution.py:332
  184.4 3.5 %all-to-all-start.3 = ((bf16[4,64,1024]{2,1,0:T(8,128)(2,1)}), bf16[4,64,1024]{2,1,0:T(8,128)(2,1)S(1)}, u32[]{:S(2)}, u32[]{:S(2)}) async-start(bf16[4,64,1024]{2,1,0:T(8,128)(2,1)} %attend_pass.1), calls=%async_computation.3 | async-start | bytes 1048576 | tf_op jit(solution)/shard_map/all_to_all | solution.py:346
  187.9 1.0 pad_maximum_fusion
  189.0 9.3 %all-to-all-done.3 = bf16[4,64,1024]{2,1,0:T(8,128)(2,1)S(1)} async-done(((bf16[4,64,1024]{2,1,0:T(8,128)(2,1)}), bf16[4,64,1024]{2,1,0:T(8,128)(2,1)S(1)}, u32[]{:S(2)}, u32[]{:S(2)}) %all-to-all-start.3) | async-done | bytes 524320 | tf_op jit(solution)/shard_map/all_to_all | solution.py:346
  198.4 0.8 pad_maximum_fusion.1
  (56 shorter events, 0.2 us)
Async XLA Ops:
  7.2 2.3 %copy-start.8 = (bf16[2,16,16384]{2,1,0:T(8,128)(2,1)S(1)}, bf16[2,16,16384]{2,1,0:T(8,128)(2,1)}, u32[]{:S(2)}) copy-start(bf16[2,16,16384]{2,1,0:T(8,128)(2,1)} %param.14) | copy-start | bytes 3145732
  7.2 2.3 %copy-start.9 = (bf16[2,16,16384]{2,1,0:T(8,128)(2,1)S(1)}, bf16[2,16,16384]{2,1,0:T(8,128)(2,1)}, u32[]{:S(2)}) copy-start(bf16[2,16,16384]{2,1,0:T(8,128)(2,1)} %param.15) | copy-start | bytes 3145732
  10.5 13.4 %copy-start.15 = (bf16[1,2,16,2048]{3,2,1,0:T(8,128)(2,1)S(1)}, bf16[1,2,16,2048]{3,2,1,0:T(8,128)(2,1)}, u32[]{:S(2)}) copy-start(bf16[1,2,16,2048]{3,2,1,0:T(8,128)(2,1)} %get-tuple-element.13) | copy-start | bytes 393220
  10.5 13.5 %copy-start.17 = (bf16[1,2,16,2048]{3,2,1,0:T(8,128)(2,1)S(1)}, bf16[1,2,16,2048]{3,2,1,0:T(8,128)(2,1)}, u32[]{:S(2)}) copy-start(bf16[1,2,16,2048]{3,2,1,0:T(8,128)(2,1)} %get-tuple-element.29) | copy-start | bytes 393220
  10.5 13.5 %copy-start.18 = (bf16[1,2,16,2048]{3,2,1,0:T(8,128)(2,1)S(1)}, bf16[1,2,16,2048]{3,2,1,0:T(8,128)(2,1)}, u32[]{:S(2)}) copy-start(bf16[1,2,16,2048]{3,2,1,0:T(8,128)(2,1)} %get-tuple-element.46) | copy-start | bytes 393220
  11.3 33.4 %collective-permute-start = (bf16[3,2,16,2048]{3,2,1,0:T(8,128)(2,1)}, bf16[3,2,16,2048]{3,2,1,0:T(8,128)(2,1)S(1)}, u32[]{:S(2)}, u32[]{:S(2)}) collective-permute-start(bf16[3,2,16,2048]{3,2,1,0:T(8,128)(2,1)} %pad_maximum_fusion.3), channel_id=1, source_target_pairs={{0,1},{1,2},{2,3},{3,0},{4,5},{5,6},{6,7},{7,4},{8,9},{9,10},{10,1... | collective-permute-start | bytes 1179656 | tf_op jit(solution)/shard_map/ppermute | solution.py:213
  12.9 15.0 %copy-start.14 = (bf16[1,2,16,2048]{3,2,1,0:T(8,128)(2,1)S(1)}, bf16[1,2,16,2048]{3,2,1,0:T(8,128)(2,1)}, u32[]{:S(2)}) copy-start(bf16[1,2,16,2048]{3,2,1,0:T(8,128)(2,1)} %get-tuple-element.12) | copy-start | bytes 393220
  12.9 15.0 %copy-start.16 = (bf16[1,2,16,2048]{3,2,1,0:T(8,128)(2,1)S(1)}, bf16[1,2,16,2048]{3,2,1,0:T(8,128)(2,1)}, u32[]{:S(2)}) copy-start(bf16[1,2,16,2048]{3,2,1,0:T(8,128)(2,1)} %get-tuple-element.28) | copy-start | bytes 393220
  13.7 33.2 %collective-permute-start.1 = (bf16[3,2,16,2048]{3,2,1,0:T(8,128)(2,1)}, bf16[3,2,16,2048]{3,2,1,0:T(8,128)(2,1)S(1)}, u32[]{:S(2)}, u32[]{:S(2)}) collective-permute-start(bf16[3,2,16,2048]{3,2,1,0:T(8,128)(2,1)} %pad_maximum_fusion.4), channel_id=1, source_target_pairs={{0,2},{1,3},{2,0},{3,1},{4,6},{5,7},{6,4},{7,5},{8,10},{9,11},{10,... | collective-permute-start | bytes 1179656 | tf_op jit(solution)/shard_map/ppermute | solution.py:213
  18.6 22.5 %copy-start.12 = (bf16[1,2,16,2048]{3,2,1,0:T(8,128)(2,1)S(1)}, bf16[1,2,16,2048]{3,2,1,0:T(8,128)(2,1)}, u32[]{:S(2)}) copy-start(bf16[1,2,16,2048]{3,2,1,0:T(8,128)(2,1)} %get-tuple-element.27) | copy-start | bytes 393220
  18.6 22.5 %copy-start.13 = (bf16[1,2,16,2048]{3,2,1,0:T(8,128)(2,1)S(1)}, bf16[1,2,16,2048]{3,2,1,0:T(8,128)(2,1)}, u32[]{:S(2)}) copy-start(bf16[1,2,16,2048]{3,2,1,0:T(8,128)(2,1)} %get-tuple-element.48) | copy-start | bytes 393220
  18.6 21.7 %all-to-all-start.2 = ((bf16[16,16,1280]{2,1,0:T(8,128)(2,1)}), bf16[16,16,1280]{2,1,0:T(8,128)(2,1)S(1)}, u32[]{:S(2)}, u32[]{:S(2)}) async-start(bf16[16,16,1280]{2,1,0:T(8,128)(2,1)} %shard_map.140), calls=%async_computation.2 | async-start | bytes 1310720 | tf_op jit(solution)/shard_map/all_to_all | solution.py:222
  23.9 122.2 %all-gather.2.cloned.1.call-start = ((), (), s32[]{:S(2)}) async-start(), calls=%async_computation.4 | async-start | bytes 2228224 | tf_op jit(solution)/shard_map/all_gather | solution.py:225
  24.8 31.7 %collective-permute-start.2 = (bf16[3,2,16,2048]{3,2,1,0:T(8,128)(2,1)}, bf16[3,2,16,2048]{3,2,1,0:T(8,128)(2,1)S(1)}, u32[]{:S(2)}, u32[]{:S(2)}) collective-permute-start(bf16[3,2,16,2048]{3,2,1,0:T(8,128)(2,1)} %pad_maximum_fusion.5), channel_id=1, source_target_pairs={{0,3},{1,0},{2,1},{3,2},{4,7},{5,4},{6,5},{7,6},{8,11},{9,8},{10,9... | collective-permute-start | bytes 1179656 | tf_op jit(solution)/shard_map/ppermute | solution.py:213
  29.6 26.9 %collective-permute-start.3 = (bf16[3,2,16,2048]{3,2,1,0:T(8,128)(2,1)}, bf16[3,2,16,2048]{3,2,1,0:T(8,128)(2,1)S(1)}, u32[]{:S(2)}, u32[]{:S(2)}) collective-permute-start(bf16[3,2,16,2048]{3,2,1,0:T(8,128)(2,1)} %pad_maximum_fusion.6), channel_id=1, source_target_pairs={{0,4},{1,5},{2,6},{3,7},{4,0},{5,1},{6,2},{7,3},{8,12},{9,13},{10,... | collective-permute-start | bytes 1179656 | tf_op jit(solution)/shard_map/ppermute | solution.py:213
  29.6 15.1 %collective-permute-start.8 = (bf16[2,64,32]{1,2,0:T(8,128)(2,1)}, bf16[2,64,32]{1,2,0:T(8,128)(2,1)}, u32[]{:S(2)}, u32[]{:S(2)}) collective-permute-start(bf16[2,64,32]{1,2,0:T(8,128)(2,1)} %param.16), channel_id=1, source_target_pairs={{0,4},{4,0},{1,5},{5,1},{2,6},{6,2},{3,7},{7,3},{8,12},{12,8},{9,1... | collective-permute-start | bytes 24584 | tf_op jit(solution)/shard_map/ppermute | solution.py:227
  31.9 21.7 %dynamic-slice-start = ((f32[16384]{0:T(1024)}, s32[]{:T(128)}), f32[2048]{0:T(1024)S(1)}, s32[]{:S(2)}) async-start(f32[16384]{0:T(1024)} %param.18, s32[]{:T(128)} %select_n.245), calls=%async_computation.5 | async-start | bytes 16896 | tf_op jit(solution)/shard_map/dynamic_slice | solution.py:234
  40.3 26.2 %copy-start = (bf16[16,16,1280]{2,1,0:T(8,128)(2,1)}, bf16[16,16,1280]{2,1,0:T(8,128)(2,1)S(1)}, u32[]{:S(2)}) copy-start(bf16[16,16,1280]{2,1,0:T(8,128)(2,1)S(1)} %all-to-all-done.2) | copy-start | bytes 1966084
  44.8 20.7 %collective-permute-start.4 = (bf16[3,2,16,2048]{3,2,1,0:T(8,128)(2,1)}, bf16[3,2,16,2048]{3,2,1,0:T(8,128)(2,1)S(1)}, u32[]{:S(2)}, u32[]{:S(2)}) collective-permute-start(bf16[3,2,16,2048]{3,2,1,0:T(8,128)(2,1)} %pad_maximum_fusion.7), channel_id=1, source_target_pairs={{0,5},{1,6},{2,7},{3,4},{4,1},{5,2},{6,3},{7,0},{8,13},{9,14},{10,... | collective-permute-start | bytes 1179656 | tf_op jit(solution)/shard_map/ppermute | solution.py:213
  44.8 31.9 %copy-start.1 = (bf16[3,2,16,2048]{3,2,1,0:T(8,128)(2,1)}, bf16[3,2,16,2048]{3,2,1,0:T(8,128)(2,1)S(1)}, u32[]{:S(2)}) copy-start(bf16[3,2,16,2048]{3,2,1,0:T(8,128)(2,1)S(1)} %collective-permute-done.refs_1_) | copy-start | bytes 1179652
  44.8 20.7 %collective-permute-start.5 = (bf16[3,2,16,2048]{3,2,1,0:T(8,128)(2,1)}, bf16[3,2,16,2048]{3,2,1,0:T(8,128)(2,1)S(1)}, u32[]{:S(2)}, u32[]{:S(2)}) collective-permute-start(bf16[3,2,16,2048]{3,2,1,0:T(8,128)(2,1)} %pad_maximum_fusion.8), channel_id=1, source_target_pairs={{0,6},{1,7},{2,4},{3,5},{4,2},{5,3},{6,0},{7,1},{8,14},{9,15},{10,... | collective-permute-start | bytes 1179656 | tf_op jit(solution)/shard_map/ppermute | solution.py:213
  46.9 29.8 %copy-start.2 = (bf16[3,2,16,2048]{3,2,1,0:T(8,128)(2,1)}, bf16[3,2,16,2048]{3,2,1,0:T(8,128)(2,1)S(1)}, u32[]{:S(2)}) copy-start(bf16[3,2,16,2048]{3,2,1,0:T(8,128)(2,1)S(1)} %collective-permute-done.1.refs_2_) | copy-start | bytes 1179652
  46.9 18.6 %collective-permute-start.6 = (bf16[3,2,16,2048]{3,2,1,0:T(8,128)(2,1)}, bf16[3,2,16,2048]{3,2,1,0:T(8,128)(2,1)S(1)}, u32[]{:S(2)}, u32[]{:S(2)}) collective-permute-start(bf16[3,2,16,2048]{3,2,1,0:T(8,128)(2,1)} %pad_maximum_fusion.9), channel_id=1, source_target_pairs={{0,7},{1,4},{2,5},{3,6},{4,3},{5,0},{6,1},{7,2},{8,15},{9,12},{10,... | collective-permute-start | bytes 1179656 | tf_op jit(solution)/shard_map/ppermute | solution.py:213
  56.5 20.2 %copy-start.3 = (bf16[3,2,16,2048]{3,2,1,0:T(8,128)(2,1)}, bf16[3,2,16,2048]{3,2,1,0:T(8,128)(2,1)S(1)}, u32[]{:S(2)}) copy-start(bf16[3,2,16,2048]{3,2,1,0:T(8,128)(2,1)S(1)} %collective-permute-done.2.refs_3_) | copy-start | bytes 1179652
  56.5 20.1 %copy-start.4 = (bf16[3,2,16,2048]{3,2,1,0:T(8,128)(2,1)}, bf16[3,2,16,2048]{3,2,1,0:T(8,128)(2,1)S(1)}, u32[]{:S(2)}) copy-start(bf16[3,2,16,2048]{3,2,1,0:T(8,128)(2,1)S(1)} %collective-permute-done.3.refs_4_) | copy-start | bytes 1179652
  65.5 11.2 %copy-start.5 = (bf16[3,2,16,2048]{3,2,1,0:T(8,128)(2,1)}, bf16[3,2,16,2048]{3,2,1,0:T(8,128)(2,1)S(1)}, u32[]{:S(2)}) copy-start(bf16[3,2,16,2048]{3,2,1,0:T(8,128)(2,1)S(1)} %collective-permute-done.4.refs_5_) | copy-start | bytes 1179652
  65.5 11.2 %copy-start.6 = (bf16[3,2,16,2048]{3,2,1,0:T(8,128)(2,1)}, bf16[3,2,16,2048]{3,2,1,0:T(8,128)(2,1)S(1)}, u32[]{:S(2)}) copy-start(bf16[3,2,16,2048]{3,2,1,0:T(8,128)(2,1)S(1)} %collective-permute-done.5.refs_6_) | copy-start | bytes 1179652
  65.5 11.2 %copy-start.7 = (bf16[3,2,16,2048]{3,2,1,0:T(8,128)(2,1)}, bf16[3,2,16,2048]{3,2,1,0:T(8,128)(2,1)S(1)}, u32[]{:S(2)}) copy-start(bf16[3,2,16,2048]{3,2,1,0:T(8,128)(2,1)S(1)} %collective-permute-done.6.refs_7_) | copy-start | bytes 1179652
  66.5 8.2 %collective-permute-start.7 = (bf16[2,3,2048]{2,1,0:T(4,128)(2,1)}, bf16[2,3,2048]{2,1,0:T(4,128)(2,1)}, u32[]{:S(2)}, u32[]{:S(2)}) collective-permute-start(bf16[2,3,2048]{2,1,0:T(4,128)(2,1)} %fusion.1), channel_id=1, source_target_pairs={{0,8},{8,16},{16,24},{24,32},{32,40},{40,48},{48,56},{56,64},{64,7... | collective-permute-start | bytes 73736 | tf_op jit(solution)/shard_map/ppermute | solution.py:220
  76.7 22.5 %copy-start.19 = (f32[16,4096]{1,0:T(8,128)S(1)}, f32[16,4096]{1,0:T(8,128)}, u32[]{:S(2)}) copy-start(f32[16,4096]{1,0:T(8,128)} %param.20) | copy-start | bytes 786436
  91.7 16.3 %all-to-all-start = ((bf16[32,24,128]{2,1,0:T(8,128)(2,1)}), bf16[32,24,128]{2,1,0:T(8,128)(2,1)S(1)}, u32[]{:S(2)}, u32[]{:S(2)}) async-start(bf16[32,24,128]{2,1,0:T(8,128)(2,1)} %get-tuple-element.7), calls=%async_computation | async-start | bytes 393216 | tf_op jit(solution)/shard_map/all_to_all | solution.py:284
  108.0 0.7 copy-start.10
  110.3 14.5 %all-to-all-start.1 = ((bf16[32,16,128]{2,1,0:T(8,128)(2,1)}), bf16[32,16,128]{2,1,0:T(8,128)(2,1)S(1)}, u32[]{:S(2)}, u32[]{:S(2)}) async-start(bf16[32,16,128]{2,1,0:T(8,128)(2,1)} %prefix_pass.1), calls=%async_computation.1 | async-start | bytes 262144 | tf_op jit(solution)/shard_map/all_to_all | solution.py:294
  124.8 1.9 copy-start.11
  126.7 16.2 %copy-start.20 = (s32[2]{0:T(128)S(1)}, s32[2]{0:T(128)}, u32[]{:S(2)}) copy-start(s32[2]{0:T(128)} %refs_15_.1) | copy-start | bytes 28
  142.8 2.0 collective-permute-start.9
  184.4 13.8 %all-to-all-start.3 = ((bf16[4,64,1024]{2,1,0:T(8,128)(2,1)}), bf16[4,64,1024]{2,1,0:T(8,128)(2,1)S(1)}, u32[]{:S(2)}, u32[]{:S(2)}) async-start(bf16[4,64,1024]{2,1,0:T(8,128)(2,1)} %attend_pass.1), calls=%async_computation.3 | async-start | bytes 1048576 | tf_op jit(solution)/shard_map/all_to_all | solution.py:346
Sparse Core Ops, SparseCore 0:
  41.2 36.3 all-gather.1

commit v2 on v1

--- a/solution.py
+++ b/solution.py
@@ -131,9 +131,10 @@
         out[i, :, 1152:1280] = v[b, :, g * HD : (g + 1) * HD]
 
 
-def attend_pass(info, q_ref, kv_ref, out):
-    z, core, live = info[0], info[1], info[2]
-    qs = q_ref[...].reshape(256, HD)
+def attend_pass(info, own_ref, far_ref, kv_ref, own_out, far_out):
+    own = pl.program_id(0) < 2
+    z, core, live = jnp.where(own, info[0], info[1]), info[2], info[3]
+    qs = jnp.where(own, own_ref[...], far_ref[...]).reshape(256, HD)
     factor = LOG2E / math.sqrt(HD)
 
     def block(zz, carry, masked):
@@ -162,7 +163,37 @@
     result = jnp.transpose(acc / divisor)
     r = lax.broadcasted_iota(jnp.int32, (256, HD), 0)
     pos = z * 512 + (r // 64) * 128 + core * 64 + r % 64
-    out[...] = jnp.where(pos < live, result, 0.0).astype(BF16).reshape(4, 64, HD)
+    kept = jnp.where(pos < live, result, 0.0).astype(BF16).reshape(4, 64, HD)
+
+    @pl.when(own)
+    def _():
+        own_out[...] = kept
+
+    @pl.when(jnp.logical_not(own))
+    def _():
+        far_out[...] = kept
+
+
+def attend(part, info, own, far, kv):
+    own_at = lambda i: jnp.minimum(i, 1)
+    far_at = lambda i: jnp.maximum(i - 2, 0)
+    block = lambda at, base: pl.BlockSpec((4, 64, HD), lambda i, o: (0, 0, base + at(i)))
+    shape = jax.ShapeDtypeStruct((4, 64, 256), BF16)
+    return pl.pallas_call(
+        attend_pass,
+        grid_spec=pltpu.PrefetchScalarGridSpec(
+            num_scalar_prefetch=1,
+            grid=(4,),
+            in_specs=[
+                block(own_at, 2 * part),
+                block(far_at, 2 * part),
+                pl.BlockSpec((16, 256, 256), lambda i, o: (0, 0, 0)),
+            ],
+            out_specs=[block(own_at, 0), block(far_at, 0)],
+        ),
+        out_shape=[shape, shape],
+        name="attend_pass",
+    )(info, own, far, kv)
 
 
 def shards(
@@ -223,6 +254,11 @@
     received = received.reshape(4, 64, 1280)
     kv_own = received[:, :, 1024:].reshape(1, 256, 256)
     kv_all = lax.all_gather(kv_own, ("z", "core"), axis=0, tiled=True)
+    mirror = [(i, nz - 1 - i) for i in range(nz)]
+    far = lax.ppermute(received[:, :, 512:1024], "z", mirror)
+    info = jnp.stack(
+        [z, nz - 1 - z, core, lax.dynamic_index_in_dim(lengths, x // 2, 0, keepdims=False)]
+    ).astype(jnp.int32)
 
     other = lax.ppermute(state_proj, "core", [(0, 1), (1, 0)])
     first = jnp.where(core == 0, state_proj, other)
@@ -281,7 +317,11 @@
         name="first_pass",
     )(order, *pieces, tail, params, rate, inflow)
 
+    message, far = lax.optimization_barrier((message, far))
     sections = lax.all_to_all(message, ("z", "x"), 0, 0, tiled=True)
+    own_0, far_0 = attend(0, info, received, far, kv_all)
+    sections, own_0, far_0 = lax.optimization_barrier((sections, own_0, far_0))
+    back_0 = lax.ppermute(far_0, "z", mirror)
     chunk = (z * nx + x) % 16
     rate_chunk = lax.dynamic_slice_in_dim(rate_rows, chunk * LANES, LANES, 1)
     prefix = pl.pallas_call(
@@ -291,7 +331,11 @@
         out_specs=vmem,
         name="prefix_pass",
     )(sections, rate_chunk)
+    prefix, far = lax.optimization_barrier((prefix, far))
     entering = lax.all_to_all(prefix, ("z", "x"), 0, 0, tiled=True)
+    own_1, far_1 = attend(1, info, received, far, kv_all)
+    entering, own_1, far_1, back_0 = lax.optimization_barrier((entering, own_1, far_1, back_0))
+    back_1 = lax.ppermute(far_1, "z", mirror)
 
     mixed = pl.pallas_call(
         second_pass,
@@ -328,21 +372,7 @@
         [jnp.where(core == 0, own, back), jnp.where(core == 0, back, own)], axis=2
     )
 
-    info = jnp.stack([z, core, lax.dynamic_index_in_dim(lengths, x // 2, 0, keepdims=False)])
-    attended = pl.pallas_call(
-        attend_pass,
-        grid_spec=pltpu.PrefetchScalarGridSpec(
-            num_scalar_prefetch=1,
-            grid=(8,),
-            in_specs=[
-                pl.BlockSpec((4, 64, HD), lambda h, i: (0, 0, h)),
-                pl.BlockSpec((16, 256, 256), lambda h, i: (0, 0, 0)),
-            ],
-            out_specs=pl.BlockSpec((4, 64, HD), lambda h, i: (0, 0, h)),
-        ),
-        out_shape=jax.ShapeDtypeStruct((4, 64, 1024), BF16),
-        name="attend_pass",
-    )(info.astype(jnp.int32), received, kv_all)
+    attended = jnp.concatenate([own_0, own_1, back_0, back_1], axis=2)
     home = lax.all_to_all(attended, "x", 0, 0, tiled=True)
     attention_output = jnp.stack(
         [

time: 207 us -> 212 us (1.024)
  the two profiles are of different devices: /device:TPU:224 before, /device:TPU:32 now
where the time goes in v2:
time: 212 us; the launch traced here: 211 us
  Pallas kernels  60.2 us (28%)
  starting transfers between devices  52.1 us (25%)
  waiting for transfers between devices  47.8 us (23%)
  local copies, waits for them, and re-layouts  19.2 us (9%)
  other arithmetic  17.4 us (8%)
  between operations  14.5 us (7%)
    pallas_call x2, Pallas kernels, attend(): pl.pallas_call(attend_pass, grid_spec=pltpu.PrefetchScalarGridSpec(num_sc...  26.6 us
    pallas_call x1, Pallas kernels, shards(): pl.pallas_call(second_pass, grid_spec=pltpu.PrefetchScalarGridSpec(num_sc...  15 us
    pallas_call x1, Pallas kernels, shards(): pl.pallas_call(first_pass, grid_spec=pltpu.PrefetchScalarGridSpec(num_sca...  14.9 us
    ppermute x7, waiting for transfers between devices, shards(): pieces.append(block if dc + dh == 0 else lax.ppermute(block, group, route))  14.7 us
    all_to_all x1, waiting for transfers between devices, shards(): received = lax.all_to_all(packed, ('x', 'head'), 0, 0, tiled=True)  11.6 us
    all_to_all x1, starting transfers between devices, shards(): sections = lax.all_to_all(message, ('z', 'x'), 0, 0, tiled=True)  11.4 us
    all_to_all x1, starting transfers between devices, shards(): entering = lax.all_to_all(prefix, ('z', 'x'), 0, 0, tiled=True)  9.77 us
    another operation x8, other arithmetic, piece_for(): jnp.stack([lax.dynamic_slice_in_dim(part, at, half, 2) for part in (mixer...  8.21 us
  transfers between devices with their start and end apart: 18, of which 5 were waited for; matrix products, arithmetic and copies ran while one was open for 15% of the time, Pallas kernels for 20%

profile of v2, /device:TPU:32, one launch (start us, length us, event | category | flops | bytes accessed | tf_op | source)
XLA Modules:
  0.0 211.1 jit_solution(4831747078047946568)
XLA Ops:
  7.2 2.1 shard_map.140
  9.3 7.0 %all-to-all-start = ((bf16[16,16,1280]{2,1,0:T(8,128)(2,1)}), bf16[16,16,1280]{2,1,0:T(8,128)(2,1)S(1)}, u32[]{:S(2)}, u32[]{:S(2)}) async-start(bf16[16,16,1280]{2,1,0:T(8,128)(2,1)} %shard_map.140), calls=%async_computation | async-start | bytes 1310720 | tf_op jit(solution)/shard_map/all_to_all | solution.py:253
  16.5 1.1 dynamic-slice_bitcast_fusion
  17.6 11.6 %all-to-all-done = bf16[16,16,1280]{2,1,0:T(8,128)(2,1)S(1)} async-done(((bf16[16,16,1280]{2,1,0:T(8,128)(2,1)}), bf16[16,16,1280]{2,1,0:T(8,128)(2,1)S(1)}, u32[]{:S(2)}, u32[]{:S(2)}) %all-to-all-start) | async-done | bytes 655392 | tf_op jit(solution)/shard_map/all_to_all | solution.py:253
  29.2 0.7 slice.75
  30.0 2.1 %dynamic-slice_bitcast_fusion.2 = (bf16[1,2,16,2048]{3,2,1,0:T(8,128)(2,1)S(1)}, bf16[1,2,16,2048]{3,2,1,0:T(8,128)(2,1)S(1)}, bf16[1,2,16,2048]{3,2,1,0:T(8,128...) fusion(bf16[2,16,16384]{2,1,0:T(8,128)(2,1)} %param.13, ...), kind=kLoop, calls=%fused_computation.23 | loop fusion | bytes 2097184 | tf_op jit(solution)/shard_map/stack | solution.py:230
  32.1 0.8 pad_maximum_fusion.7
  33.0 0.8 pad_maximum_fusion.8
  33.8 0.7 collective-permute-start.4
  34.4 0.8 pad_maximum_fusion.9
  35.2 1.2 collective-permute-start.5
  36.4 0.8 pad_maximum_fusion.10
  37.2 1.6 collective-permute-start.6
  38.9 1.7 pad_maximum_fusion.6
  40.6 1.7 pad_maximum_fusion.5
  42.3 0.8 pad_maximum_fusion.4
  43.1 0.8 pad_maximum_fusion.3.refs_0_
  43.9 1.3 dynamic-slice_convert_fusion
  45.2 1.0 collective-permute-start.2
  46.2 1.9 collective-permute-start.1
  48.1 14.7 %collective-permute-done.4.refs_5_ = bf16[3,2,16,2048]{3,2,1,0:T(8,128)(2,1)S(1)} collective-permute-done((bf16[3,2,16,2048]{3,2,1,0:T(8,128)(2,1)}, bf16[3,2,16,2048]{3,2,1,0:T(8,128)(2,1)S(1)}, u32[]{:S(2)}, u32[]{:S(2)}) %collective-permute-start.4) | collective-permute-done | bytes 393248 | tf_op jit(solution)/shard_map/ppermute | solution.py:244
  62.8 1.7 fusion.9
  64.5 0.7 dynamic_slice.126
  65.2 1.3 dynamic_slice.127
  66.5 0.9 copy.21
  67.5 0.7 copy.23
  68.1 1.2 dynamic_slice.129
  69.4 0.6 broadcast_in_dim.43
  70.0 1.5 concatenate.18.refs_9_.refs_10_
  71.4 0.7 stack.157.order
  72.1 0.7 broadcast_select_fusion.3
  72.9 0.7 slice.74
  73.6 5.8 %collective-permute-start.9 = (bf16[4,64,512]{2,1,0:T(8,128)(2,1)}, bf16[4,64,512]{2,1,0:T(8,128)(2,1)S(1)}, u32[]{:S(2)}, u32[]{:S(2)}) collective-permute-start(bf16[4,64,512]{2,1,0:T(8,128)(2,1)} %slice.74), channel_id=1, source_target_pairs={{0,224},{32,192},{64,160},{96,128},{128,96},{160,64},{192,32},{224... | collective-permute-start | bytes 786440 | tf_op jit(solution)/shard_map/ppermute | solution.py:258
  79.5 0.2 fusion.1
  79.7 1.9 collective-permute-start.7
  81.6 0.1 copy.19
  81.7 0.1 broadcast_in_dim.44
  81.9 6.0 %collective-permute-done.7.refs_8_ = bf16[2,3,2048]{2,1,0:T(4,128)(2,1)S(1)} collective-permute-done((bf16[2,3,2048]{2,1,0:T(4,128)(2,1)S(1)}, bf16[2,3,2048]{2,1,0:T(4,128)(2,1)S(1)}, u32[]{:S(2)}, u32[]{:S(2)}) %collective-permute-start.7) | collective-permute-done | bytes 24608 | tf_op jit(solution)/shard_map/ppermute | solution.py:251
  87.8 2.0 broadcast_in_dim.45.refs_11_.refs_12_
  89.9 14.9 %first_pass.1 = (f32[2,2,1024,128]{3,2,1,0:T(8,128)}, f32[2,2,1024,128]{3,2,1,0:T(8,128)}, bf16[32,24,128]{2,1,0:T(8,128)(2,1)}) custom-call(s32[9]{0:T(128)} %stack.157.order, bf16[3,2,16,2048]{3,2,1,0:T(8,128)(2,1)} %pad_maximum_fusion.3.refs_0_, bf16[3,2,16,2048]{3,2,1,0:T(8,128)(2,1)} %copy-done.8, bf16[3,2,16,2048]{3,2,1,0:T(8,128)(2,1)} %copy-done.7, ...), custom_call_target="tpu_custom_call" | custom-call | tf_op jit(solution)/shard_map/first_pass/pallas_call | solution.py:293
  104.7 11.4 %all-to-all-start.1 = ((bf16[32,24,128]{2,1,0:T(8,128)(2,1)}), bf16[32,24,128]{2,1,0:T(8,128)(2,1)S(1)}, u32[]{:S(2)}, u32[]{:S(2)}) async-start(bf16[32,24,128]{2,1,0:T(8,128)(2,1)} %get-tuple-element.23), calls=%async_computation.1 | async-start | bytes 393216 | tf_op jit(solution)/shard_map/all_to_all | solution.py:321
  116.2 1.1 pad_add_fusion.info
  117.3 0.9 exponential_multiply_fusion
  118.2 0.6 constant_dynamic-slice_fusion.1.rate
  118.9 13.3 %attend_pass.2 = (bf16[4,64,256]{2,1,0:T(8,128)(2,1)}, bf16[4,64,256]{2,1,0:T(8,128)(2,1)}) custom-call(s32[4]{0:T(128)} %pad_add_fusion.info, bf16[4,64,1280]{2,1,0:T(8,128)(2,1)} %bitcast.88, bf16[4,64,512]{2,1,0:T(8,128)(2,1)} %copy-done.11, bf16[16,256,256]{2,1,0:T(8,128)(2,1)} %all-gather.2.cloned.1.call-done.kv_ref), custom_call_target="tpu_custom_call" | custom-call | tf_op jit(solution)/shard_map/attend_pass/pallas_call | solution.py:182
  132.2 0.7 copy-done.12
  132.8 1.7 prefix_pass.1
  134.5 9.8 %all-to-all-start.2 = ((bf16[32,16,128]{2,1,0:T(8,128)(2,1)}), bf16[32,16,128]{2,1,0:T(8,128)(2,1)S(1)}, u32[]{:S(2)}, u32[]{:S(2)}) async-start(bf16[32,16,128]{2,1,0:T(8,128)(2,1)} %prefix_pass.1), calls=%async_computation.2 | async-start | bytes 262144 | tf_op jit(solution)/shard_map/all_to_all | solution.py:335
  144.3 3.9 %collective-permute-start.10 = (bf16[4,64,256]{2,1,0:T(8,128)(2,1)}, bf16[4,64,256]{2,1,0:T(8,128)(2,1)S(1)}, u32[]{:S(2)}, u32[]{:S(2)}) collective-permute-start(bf16[4,64,256]{2,1,0:T(8,128)(2,1)} %get-tuple-element.32), channel_id=1, source_target_pairs={{0,224},{32,192},{64,160},{96,128},{128,96},{160,64},{192,32},{224... | collective-permute-start | bytes 393224 | tf_op jit(solution)/shard_map/ppermute | solution.py:324
  148.1 0.1 copy.20
  148.2 0.1 broadcast_in_dim.46
  148.4 13.3 %attend_pass.3 = (bf16[4,64,256]{2,1,0:T(8,128)(2,1)}, bf16[4,64,256]{2,1,0:T(8,128)(2,1)}) custom-call(s32[4]{0:T(128)} %pad_add_fusion.info, bf16[4,64,1280]{2,1,0:T(8,128)(2,1)} %bitcast.89, bf16[4,64,512]{2,1,0:T(8,128)(2,1)} %copy-done.11, bf16[16,256,256]{2,1,0:T(8,128)(2,1)} %all-gather.2.cloned.1.call-done.kv_ref), custom_call_target="tpu_custom_call" | custom-call | tf_op jit(solution)/shard_map/attend_pass/pallas_call | solution.py:182
  161.7 2.0 broadcast_in_dim.47.refs_13_
  163.7 15.0 %second_pass.1 = bf16[2,128,2048]{2,1,0:T(8,128)(2,1)} custom-call(s32[9]{0:T(128)} %stack.157.order, bf16[3,2,16,2048]{3,2,1,0:T(8,128)(2,1)} %pad_maximum_fusion.3.refs_0_, bf16[3,2,16,2048]{3,2,1,0:T(8,128)(2,1)} %copy-done.8, bf16[3,2,16,2048]{3,2,1,0:T(8,128)(2,1)} %copy-done.7, bf16[3,2,16,2048]{3,2,1,0:T(8,128)(2,1)} %copy-done.6, ...), custom_call_target="tpu_custom_call" | custom-call | tf_op jit(solution)/shard_map/second_pass/pallas_call | solution.py:340
  178.7 1.2 constant_dynamic-slice_fusion
  179.9 0.1 collective-permute-start.11
  180.0 1.5 collective-permute-start.12
  181.5 7.5 %collective-permute-done.12 = bf16[4,64,256]{2,1,0:T(8,128)(2,1)S(1)} collective-permute-done((bf16[4,64,256]{2,1,0:T(8,128)(2,1)S(1)}, bf16[4,64,256]{2,1,0:T(8,128)(2,1)S(1)}, u32[]{:S(2)}, u32[]{:S(2)}) %collective-permute-start.12) | collective-permute-done | bytes 131104 | tf_op jit(solution)/shard_map/ppermute | solution.py:338
  189.0 0.9 pad_maximum_fusion.1
  189.9 4.3 %all-to-all-start.3 = ((bf16[4,64,1024]{2,1,0:T(8,128)(2,1)}), bf16[4,64,1024]{2,1,0:T(8,128)(2,1)S(1)}, u32[]{:S(2)}, u32[]{:S(2)}) async-start(bf16[4,64,1024]{2,1,0:T(8,128)(2,1)} %pad_maximum_fusion.1), calls=%async_computation.3 | async-start | bytes 1048576 | tf_op jit(solution)/shard_map/all_to_all | solution.py:376
  194.1 0.2 broadcast_select_fusion.1
  194.4 1.1 pad_maximum_fusion
  195.4 7.9 %all-to-all-done.3 = bf16[4,64,1024]{2,1,0:T(8,128)(2,1)S(1)} async-done(((bf16[4,64,1024]{2,1,0:T(8,128)(2,1)}), bf16[4,64,1024]{2,1,0:T(8,128)(2,1)S(1)}, u32[]{:S(2)}, u32[]{:S(2)}) %all-to-all-start.3) | async-done | bytes 524320 | tf_op jit(solution)/shard_map/all_to_all | solution.py:376
  203.4 0.8 pad_maximum_fusion.2
  (80 shorter events, 0.4 us)
Async XLA Ops:
  7.2 9.3 %copy-start.9 = (bf16[2,16,16384]{2,1,0:T(8,128)(2,1)S(1)}, bf16[2,16,16384]{2,1,0:T(8,128)(2,1)}, u32[]{:S(2)}) copy-start(bf16[2,16,16384]{2,1,0:T(8,128)(2,1)} %param.14) | copy-start | bytes 3145732
  7.2 9.3 %copy-start.10 = (bf16[2,16,16384]{2,1,0:T(8,128)(2,1)S(1)}, bf16[2,16,16384]{2,1,0:T(8,128)(2,1)}, u32[]{:S(2)}) copy-start(bf16[2,16,16384]{2,1,0:T(8,128)(2,1)} %param.15) | copy-start | bytes 3145732
  9.3 19.9 %all-to-all-start = ((bf16[16,16,1280]{2,1,0:T(8,128)(2,1)}), bf16[16,16,1280]{2,1,0:T(8,128)(2,1)S(1)}, u32[]{:S(2)}, u32[]{:S(2)}) async-start(bf16[16,16,1280]{2,1,0:T(8,128)(2,1)} %shard_map.140), calls=%async_computation | async-start | bytes 1310720 | tf_op jit(solution)/shard_map/all_to_all | solution.py:253
  16.3 102.5 %all-gather.2.cloned.1.call-start = ((), (), s32[]{:S(2)}) async-start(), calls=%async_computation.4 | async-start | bytes 2228224 | tf_op jit(solution)/shard_map/all_gather | solution.py:256
  17.6 14.6 %copy-start.22 = (bf16[1,2,16,2048]{3,2,1,0:T(8,128)(2,1)S(1)}, bf16[1,2,16,2048]{3,2,1,0:T(8,128)(2,1)}, u32[]{:S(2)}) copy-start(bf16[1,2,16,2048]{3,2,1,0:T(8,128)(2,1)} %get-tuple-element.58) | copy-start | bytes 393220
  17.6 14.6 %copy-start.23 = (bf16[1,2,16,2048]{3,2,1,0:T(8,128)(2,1)S(1)}, bf16[1,2,16,2048]{3,2,1,0:T(8,128)(2,1)}, u32[]{:S(2)}) copy-start(bf16[1,2,16,2048]{3,2,1,0:T(8,128)(2,1)} %get-tuple-element.77) | copy-start | bytes 393220
  17.6 15.4 %copy-start.20 = (bf16[1,2,16,2048]{3,2,1,0:T(8,128)(2,1)S(1)}, bf16[1,2,16,2048]{3,2,1,0:T(8,128)(2,1)}, u32[]{:S(2)}) copy-start(bf16[1,2,16,2048]{3,2,1,0:T(8,128)(2,1)} %get-tuple-element.57) | copy-start | bytes 393220
  17.6 15.4 %copy-start.21 = (bf16[1,2,16,2048]{3,2,1,0:T(8,128)(2,1)S(1)}, bf16[1,2,16,2048]{3,2,1,0:T(8,128)(2,1)}, u32[]{:S(2)}) copy-start(bf16[1,2,16,2048]{3,2,1,0:T(8,128)(2,1)} %get-tuple-element.78) | copy-start | bytes 393220
  17.6 16.9 %copy-start.18 = (bf16[1,2,16,2048]{3,2,1,0:T(8,128)(2,1)S(1)}, bf16[1,2,16,2048]{3,2,1,0:T(8,128)(2,1)}, u32[]{:S(2)}) copy-start(bf16[1,2,16,2048]{3,2,1,0:T(8,128)(2,1)} %get-tuple-element.63) | copy-start | bytes 393220
  17.6 16.8 %copy-start.19 = (bf16[1,2,16,2048]{3,2,1,0:T(8,128)(2,1)S(1)}, bf16[1,2,16,2048]{3,2,1,0:T(8,128)(2,1)}, u32[]{:S(2)}) copy-start(bf16[1,2,16,2048]{3,2,1,0:T(8,128)(2,1)} %get-tuple-element.72) | copy-start | bytes 393220
  29.2 43.7 %copy-start = (bf16[16,16,1280]{2,1,0:T(8,128)(2,1)}, bf16[16,16,1280]{2,1,0:T(8,128)(2,1)S(1)}, u32[]{:S(2)}) copy-start(bf16[16,16,1280]{2,1,0:T(8,128)(2,1)S(1)} %all-to-all-done) | copy-start | bytes 1966084
  30.0 6.4 %copy-start.16 = (bf16[1,2,16,2048]{3,2,1,0:T(8,128)(2,1)S(1)}, bf16[1,2,16,2048]{3,2,1,0:T(8,128)(2,1)}, u32[]{:S(2)}) copy-start(bf16[1,2,16,2048]{3,2,1,0:T(8,128)(2,1)} %get-tuple-element.56) | copy-start | bytes 393220
  30.0 6.4 %copy-start.17 = (bf16[1,2,16,2048]{3,2,1,0:T(8,128)(2,1)S(1)}, bf16[1,2,16,2048]{3,2,1,0:T(8,128)(2,1)}, u32[]{:S(2)}) copy-start(bf16[1,2,16,2048]{3,2,1,0:T(8,128)(2,1)} %get-tuple-element.79) | copy-start | bytes 393220
  32.1 6.7 %copy-start.14 = (bf16[1,2,16,2048]{3,2,1,0:T(8,128)(2,1)S(1)}, bf16[1,2,16,2048]{3,2,1,0:T(8,128)(2,1)}, u32[]{:S(2)}) copy-start(bf16[1,2,16,2048]{3,2,1,0:T(8,128)(2,1)} %get-tuple-element.59) | copy-start | bytes 393220
  32.1 6.7 %copy-start.15 = (bf16[1,2,16,2048]{3,2,1,0:T(8,128)(2,1)S(1)}, bf16[1,2,16,2048]{3,2,1,0:T(8,128)(2,1)}, u32[]{:S(2)}) copy-start(bf16[1,2,16,2048]{3,2,1,0:T(8,128)(2,1)} %get-tuple-element.76) | copy-start | bytes 393220
  32.9 13.3 %collective-permute-start.3 = (bf16[3,2,16,2048]{3,2,1,0:T(8,128)(2,1)}, bf16[3,2,16,2048]{3,2,1,0:T(8,128)(2,1)S(1)}, u32[]{:S(2)}, u32[]{:S(2)}) collective-permute-start(bf16[3,2,16,2048]{3,2,1,0:T(8,128)(2,1)} %pad_maximum_fusion.7), channel_id=1, source_target_pairs={{0,4},{1,5},{2,6},{3,7},{4,0},{5,1},{6,2},{7,3},{8,12},{9,13},{10,... | collective-permute-start | bytes 1179656 | tf_op jit(solution)/shard_map/ppermute | solution.py:244
  33.8 29.0 %collective-permute-start.4 = (bf16[3,2,16,2048]{3,2,1,0:T(8,128)(2,1)}, bf16[3,2,16,2048]{3,2,1,0:T(8,128)(2,1)S(1)}, u32[]{:S(2)}, u32[]{:S(2)}) collective-permute-start(bf16[3,2,16,2048]{3,2,1,0:T(8,128)(2,1)} %pad_maximum_fusion.8), channel_id=1, source_target_pairs={{0,5},{1,6},{2,7},{3,4},{4,1},{5,2},{6,3},{7,0},{8,13},{9,14},{10,... | collective-permute-start | bytes 1179656 | tf_op jit(solution)/shard_map/ppermute | solution.py:244
  35.2 38.4 %collective-permute-start.5 = (bf16[3,2,16,2048]{3,2,1,0:T(8,128)(2,1)}, bf16[3,2,16,2048]{3,2,1,0:T(8,128)(2,1)S(1)}, u32[]{:S(2)}, u32[]{:S(2)}) collective-permute-start(bf16[3,2,16,2048]{3,2,1,0:T(8,128)(2,1)} %pad_maximum_fusion.9), channel_id=1, source_target_pairs={{0,6},{1,7},{2,4},{3,5},{4,2},{5,3},{6,0},{7,1},{8,14},{9,15},{10,... | collective-permute-start | bytes 1179656 | tf_op jit(solution)/shard_map/ppermute | solution.py:244
  37.2 42.2 %collective-permute-start.6 = (bf16[3,2,16,2048]{3,2,1,0:T(8,128)(2,1)}, bf16[3,2,16,2048]{3,2,1,0:T(8,128)(2,1)S(1)}, u32[]{:S(2)}, u32[]{:S(2)}) collective-permute-start(bf16[3,2,16,2048]{3,2,1,0:T(8,128)(2,1)} %pad_maximum_fusion.10), channel_id=1, source_target_pairs={{0,7},{1,4},{2,5},{3,6},{4,3},{5,0},{6,1},{7,2},{8,15},{9,12},{10,... | collective-permute-start | bytes 1179656 | tf_op jit(solution)/shard_map/ppermute | solution.py:244
  38.9 6.4 %collective-permute-start.8 = (bf16[2,64,32]{1,2,0:T(8,128)(2,1)}, bf16[2,64,32]{1,2,0:T(8,128)(2,1)}, u32[]{:S(2)}, u32[]{:S(2)}) collective-permute-start(bf16[2,64,32]{1,2,0:T(8,128)(2,1)} %param.16), channel_id=1, source_target_pairs={{0,4},{4,0},{1,5},{5,1},{2,6},{6,2},{3,7},{7,3},{8,12},{12,8},{9,1... | collective-permute-start | bytes 24584 | tf_op jit(solution)/shard_map/ppermute | solution.py:263
  38.9 31.1 %dynamic-slice-start = ((f32[16384]{0:T(1024)}, s32[]{:T(128)}), f32[2048]{0:T(1024)S(1)}, s32[]{:S(2)}) async-start(f32[16384]{0:T(1024)} %param.18, s32[]{:T(128)} %select_n.245), calls=%async_computation.5 | async-start | bytes 16896 | tf_op jit(solution)/shard_map/dynamic_slice | solution.py:270
  45.2 34.2 %collective-permute-start.2 = (bf16[3,2,16,2048]{3,2,1,0:T(8,128)(2,1)}, bf16[3,2,16,2048]{3,2,1,0:T(8,128)(2,1)S(1)}, u32[]{:S(2)}, u32[]{:S(2)}) collective-permute-start(bf16[3,2,16,2048]{3,2,1,0:T(8,128)(2,1)} %pad_maximum_fusion.6), channel_id=1, source_target_pairs={{0,3},{1,0},{2,1},{3,2},{4,7},{5,4},{6,5},{7,6},{8,11},{9,8},{10,9... | collective-permute-start | bytes 1179656 | tf_op jit(solution)/shard_map/ppermute | solution.py:244
  46.2 43.6 %copy-start.2 = (bf16[3,2,16,2048]{3,2,1,0:T(8,128)(2,1)}, bf16[3,2,16,2048]{3,2,1,0:T(8,128)(2,1)S(1)}, u32[]{:S(2)}) copy-start(bf16[3,2,16,2048]{3,2,1,0:T(8,128)(2,1)S(1)} %collective-permute-done.3.refs_4_) | copy-start | bytes 1179652
  46.2 33.2 %collective-permute-start.1 = (bf16[3,2,16,2048]{3,2,1,0:T(8,128)(2,1)}, bf16[3,2,16,2048]{3,2,1,0:T(8,128)(2,1)S(1)}, u32[]{:S(2)}, u32[]{:S(2)}) collective-permute-start(bf16[3,2,16,2048]{3,2,1,0:T(8,128)(2,1)} %pad_maximum_fusion.5), channel_id=1, source_target_pairs={{0,2},{1,3},{2,0},{3,1},{4,6},{5,7},{6,4},{7,5},{8,10},{9,11},{10,... | collective-permute-start | bytes 1179656 | tf_op jit(solution)/shard_map/ppermute | solution.py:244
  62.8 27.0 %copy-start.3 = (bf16[3,2,16,2048]{3,2,1,0:T(8,128)(2,1)}, bf16[3,2,16,2048]{3,2,1,0:T(8,128)(2,1)S(1)}, u32[]{:S(2)}) copy-start(bf16[3,2,16,2048]{3,2,1,0:T(8,128)(2,1)S(1)} %collective-permute-done.4.refs_5_) | copy-start | bytes 1179652
  62.8 16.7 %collective-permute-start = (bf16[3,2,16,2048]{3,2,1,0:T(8,128)(2,1)}, bf16[3,2,16,2048]{3,2,1,0:T(8,128)(2,1)S(1)}, u32[]{:S(2)}, u32[]{:S(2)}) collective-permute-start(bf16[3,2,16,2048]{3,2,1,0:T(8,128)(2,1)} %pad_maximum_fusion.4), channel_id=1, source_target_pairs={{0,1},{1,2},{2,3},{3,0},{4,5},{5,6},{6,7},{7,4},{8,9},{9,10},{10,1... | collective-permute-start | bytes 1179656 | tf_op jit(solution)/shard_map/ppermute | solution.py:244
  73.6 16.2 %copy-start.4 = (bf16[3,2,16,2048]{3,2,1,0:T(8,128)(2,1)}, bf16[3,2,16,2048]{3,2,1,0:T(8,128)(2,1)S(1)}, u32[]{:S(2)}) copy-start(bf16[3,2,16,2048]{3,2,1,0:T(8,128)(2,1)S(1)} %collective-permute-done.5.refs_6_) | copy-start | bytes 1179652
  73.6 31.1 %collective-permute-start.9 = (bf16[4,64,512]{2,1,0:T(8,128)(2,1)}, bf16[4,64,512]{2,1,0:T(8,128)(2,1)S(1)}, u32[]{:S(2)}, u32[]{:S(2)}) collective-permute-start(bf16[4,64,512]{2,1,0:T(8,128)(2,1)} %slice.74), channel_id=1, source_target_pairs={{0,224},{32,192},{64,160},{96,128},{128,96},{160,64},{192,32},{224... | collective-permute-start | bytes 786440 | tf_op jit(solution)/shard_map/ppermute | solution.py:258
  79.5 10.4 %copy-start.5 = (bf16[3,2,16,2048]{3,2,1,0:T(8,128)(2,1)}, bf16[3,2,16,2048]{3,2,1,0:T(8,128)(2,1)S(1)}, u32[]{:S(2)}) copy-start(bf16[3,2,16,2048]{3,2,1,0:T(8,128)(2,1)S(1)} %collective-permute-done.6.refs_7_) | copy-start | bytes 1179652
  79.5 10.4 %copy-start.6 = (bf16[3,2,16,2048]{3,2,1,0:T(8,128)(2,1)}, bf16[3,2,16,2048]{3,2,1,0:T(8,128)(2,1)S(1)}, u32[]{:S(2)}) copy-start(bf16[3,2,16,2048]{3,2,1,0:T(8,128)(2,1)S(1)} %collective-permute-done.2.refs_3_) | copy-start | bytes 1179652
  79.5 10.4 %copy-start.7 = (bf16[3,2,16,2048]{3,2,1,0:T(8,128)(2,1)}, bf16[3,2,16,2048]{3,2,1,0:T(8,128)(2,1)S(1)}, u32[]{:S(2)}) copy-start(bf16[3,2,16,2048]{3,2,1,0:T(8,128)(2,1)S(1)} %collective-permute-done.1.refs_2_) | copy-start | bytes 1179652
  79.5 10.3 %copy-start.8 = (bf16[3,2,16,2048]{3,2,1,0:T(8,128)(2,1)}, bf16[3,2,16,2048]{3,2,1,0:T(8,128)(2,1)S(1)}, u32[]{:S(2)}) copy-start(bf16[3,2,16,2048]{3,2,1,0:T(8,128)(2,1)S(1)} %collective-permute-done.refs_1_) | copy-start | bytes 1179652
  79.7 8.1 %collective-permute-start.7 = (bf16[2,3,2048]{2,1,0:T(4,128)(2,1)S(1)}, bf16[2,3,2048]{2,1,0:T(4,128)(2,1)S(1)}, u32[]{:S(2)}, u32[]{:S(2)}) collective-permute-start(bf16[2,3,2048]{2,1,0:T(4,128)(2,1)S(1)} %fusion.1), channel_id=1, source_target_pairs={{0,8},{8,16},{16,24},{24,32},{32,40},{40,48},{48,56},{56,64},{64,7... | collective-permute-start | bytes 73736 | tf_op jit(solution)/shard_map/ppermute | solution.py:251
  87.8 2.0 copy-start.26
  104.7 14.1 %copy-start.11 = (bf16[4,64,512]{2,1,0:T(8,128)(2,1)}, bf16[4,64,512]{2,1,0:T(8,128)(2,1)S(1)}, u32[]{:S(2)}) copy-start(bf16[4,64,512]{2,1,0:T(8,128)(2,1)S(1)} %collective-permute-done.9.far_ref) | copy-start | bytes 786436
  104.7 27.4 %all-to-all-start.1 = ((bf16[32,24,128]{2,1,0:T(8,128)(2,1)}), bf16[32,24,128]{2,1,0:T(8,128)(2,1)S(1)}, u32[]{:S(2)}, u32[]{:S(2)}) async-start(bf16[32,24,128]{2,1,0:T(8,128)(2,1)} %get-tuple-element.23), calls=%async_computation.1 | async-start | bytes 393216 | tf_op jit(solution)/shard_map/all_to_all | solution.py:321
  132.2 0.7 copy-start.12
  134.5 27.2 %all-to-all-start.2 = ((bf16[32,16,128]{2,1,0:T(8,128)(2,1)}), bf16[32,16,128]{2,1,0:T(8,128)(2,1)S(1)}, u32[]{:S(2)}, u32[]{:S(2)}) async-start(bf16[32,16,128]{2,1,0:T(8,128)(2,1)} %prefix_pass.1), calls=%async_computation.2 | async-start | bytes 262144 | tf_op jit(solution)/shard_map/all_to_all | solution.py:335
  144.3 17.4 %collective-permute-start.10 = (bf16[4,64,256]{2,1,0:T(8,128)(2,1)}, bf16[4,64,256]{2,1,0:T(8,128)(2,1)S(1)}, u32[]{:S(2)}, u32[]{:S(2)}) collective-permute-start(bf16[4,64,256]{2,1,0:T(8,128)(2,1)} %get-tuple-element.32), channel_id=1, source_target_pairs={{0,224},{32,192},{64,160},{96,128},{128,96},{160,64},{192,32},{224... | collective-permute-start | bytes 393224 | tf_op jit(solution)/shard_map/ppermute | solution.py:324
  161.7 2.0 copy-start.13
  163.7 16.3 %copy-start.27 = (bf16[4,64,256]{2,1,0:T(8,128)(2,1)S(1)}, bf16[4,64,256]{2,1,0:T(8,128)(2,1)}, u32[]{:S(2)}) copy-start(bf16[4,64,256]{2,1,0:T(8,128)(2,1)} %get-tuple-element.37) | copy-start | bytes 393220
  163.7 25.3 %copy-start.24 = (bf16[4,64,256]{2,1,0:T(8,128)(2,1)S(1)}, bf16[4,64,256]{2,1,0:T(8,128)(2,1)}, u32[]{:S(2)}) copy-start(bf16[4,64,256]{2,1,0:T(8,128)(2,1)} %get-tuple-element.34) | copy-start | bytes 393220
  163.7 25.3 %copy-start.25 = (bf16[4,64,256]{2,1,0:T(8,128)(2,1)S(1)}, bf16[4,64,256]{2,1,0:T(8,128)(2,1)}, u32[]{:S(2)}) copy-start(bf16[4,64,256]{2,1,0:T(8,128)(2,1)} %get-tuple-element.35) | copy-start | bytes 393220
  178.7 15.5 %copy-start.1 = (bf16[2,128,2048]{2,1,0:T(8,128)(2,1)S(1)}, bf16[2,128,2048]{2,1,0:T(8,128)(2,1)}, u32[]{:S(2)}) copy-start(bf16[2,128,2048]{2,1,0:T(8,128)(2,1)} %second_pass.1) | copy-start | bytes 3145732
  179.9 14.3 %collective-permute-start.11 = (bf16[2,64,2048]{2,1,0:T(8,128)(2,1)S(1)}, bf16[2,64,2048]{2,1,0:T(8,128)(2,1)S(1)}, u32[]{:S(2)}, u32[]{:S(2)}) collective-permute-start(bf16[2,64,2048]{2,1,0:T(8,128)(2,1)S(1)} %constant_dynamic-slice_fusion), channel_id=1, source_target_pairs={{0,4},{4,0},{1,5},{5,1},{2,6},{6,2},{3,7},{7,3},{8,12},{12,8},{9,1... | collective-permute-start | bytes 1572872 | tf_op jit(solution)/shard_map/ppermute | solution.py:370
  180.0 9.0 %collective-permute-start.12 = (bf16[4,64,256]{2,1,0:T(8,128)(2,1)S(1)}, bf16[4,64,256]{2,1,0:T(8,128)(2,1)S(1)}, u32[]{:S(2)}, u32[]{:S(2)}) collective-permute-start(bf16[4,64,256]{2,1,0:T(8,128)(2,1)S(1)} %copy-done.27), channel_id=1, source_target_pairs={{0,224},{32,192},{64,160},{96,128},{128,96},{160,64},{192,32},{224... | collective-permute-start | bytes 393224 | tf_op jit(solution)/shard_map/ppermute | solution.py:338
  189.9 13.5 %all-to-all-start.3 = ((bf16[4,64,1024]{2,1,0:T(8,128)(2,1)}), bf16[4,64,1024]{2,1,0:T(8,128)(2,1)S(1)}, u32[]{:S(2)}, u32[]{:S(2)}) async-start(bf16[4,64,1024]{2,1,0:T(8,128)(2,1)} %pad_maximum_fusion.1), calls=%async_computation.3 | async-start | bytes 1048576 | tf_op jit(solution)/shard_map/all_to_all | solution.py:376
Sparse Core Ops, SparseCore 0:
  30.1 38.2 all-gather.1

commit v3 on v2

--- a/solution.py
+++ b/solution.py
@@ -218,47 +218,48 @@
     quarter = decay_log.shape[1]
     vmem = pl.BlockSpec(memory_space=pltpu.VMEM)
 
+    turns = [(dc, dh) for dc in range(2) for dh in range(4)]
+
+    def slice_for(part, turn):
+        dc, dh = turn
+        at = (head + dh) % 4 * quarter + (core ^ dc) * half
+        return lax.dynamic_slice_in_dim(part, at, half, 2)
+
+    def turned(block, turn):
+        dc, dh = turn
+        route = [(c * 4 + h, (c ^ dc) * 4 + (h + dh) % 4) for c in range(2) for h in range(4)]
+        return block if dc + dh == 0 else lax.ppermute(block, group, route)
+
+    pieces = [
+        turned(jnp.stack([slice_for(mixer_input, turn), slice_for(step_input, turn)]), turn)
+        for turn in turns
+    ]
+    order = [(core ^ dc) * 4 + (head - dh) % 4 for dc, dh in turns]
     packed = pl.pallas_call(
         pack_pass,
         out_shape=jax.ShapeDtypeStruct((16, ROWS, 1280), BF16),
         in_specs=[vmem] * 3,
         out_specs=vmem,
     )(query_states, key_states, value_states)
-
-    def piece_for(to_core, to_head):
-        at = to_head * quarter + to_core * half
-        return jnp.stack(
-            [
-                lax.dynamic_slice_in_dim(part, at, half, 2)
-                for part in (mixer_input, step_input, gate_input)
-            ]
-        )
-
-    pieces, order = [], []
-    for dc in range(2):
-        for dh in range(4):
-            block = piece_for(core ^ dc, (head + dh) % 4)
-            route = [
-                (c * 4 + h, (c ^ dc) * 4 + (h + dh) % 4) for c in range(2) for h in range(4)
-            ]
-            pieces.append(block if dc + dh == 0 else lax.ppermute(block, group, route))
-            order.append((core ^ dc) * 4 + (head - dh) % 4)
+    received = lax.all_to_all(packed, ("x", "head"), 0, 0, tiled=True)
+    received, pieces[:5] = lax.optimization_barrier((received, pieces[:5]))
     last = sum(
         jnp.where(order[d] == PIECES - 1, pieces[d][0, :, ROWS - 3 :, :], jnp.zeros((), BF16))
         for d in range(PIECES)
     )
     chips = nz * nx
     tail = lax.ppermute(last, ("z", "x"), [(i, i + 1) for i in range(chips - 1)])
-
-    received = lax.all_to_all(packed, ("x", "head"), 0, 0, tiled=True)
     received = received.reshape(4, 64, 1280)
     kv_own = received[:, :, 1024:].reshape(1, 256, 256)
     kv_all = lax.all_gather(kv_own, ("z", "core"), axis=0, tiled=True)
-    mirror = [(i, nz - 1 - i) for i in range(nz)]
-    far = lax.ppermute(received[:, :, 512:1024], "z", mirror)
     info = jnp.stack(
         [z, nz - 1 - z, core, lax.dynamic_index_in_dim(lengths, x // 2, 0, keepdims=False)]
     ).astype(jnp.int32)
+
+    mirror = [(i, nz - 1 - i) for i in range(nz)]
+    far, tail, gate_input = lax.optimization_barrier((received[:, :, 512:1024], tail, gate_input))
+    far = lax.ppermute(far, "z", mirror)
+    gates = [turned(slice_for(gate_input, turn)[None], turn) for turn in turns[:4]]
 
     other = lax.ppermute(state_proj, "core", [(0, 1), (1, 0)])
     first = jnp.where(core == 0, state_proj, other)
@@ -282,9 +283,7 @@
     start_row = (z * nx + x) * SPAN
     order = jnp.stack(order + [start_row]).astype(jnp.int32)
 
-    blk = lambda arrays, which: pl.BlockSpec(
-        (arrays, 1, ROWS, WIDE), lambda c, b, o: (which, b, 0, c)
-    )
+    blk = lambda arrays: pl.BlockSpec((arrays, 1, ROWS, WIDE), lambda c, b, o: (0, b, 0, c))
     slab = pl.BlockSpec((1, 1, SPAN * 8, LANES), lambda c, b, o: (b, c, 0, 0))
     params_spec = pl.BlockSpec((8, WIDE), lambda c, b, o: (0, c))
     rate_spec = pl.BlockSpec((1, NST, 8, LANES), lambda c, b, o: (c, 0, 0, 0))
@@ -295,7 +294,7 @@
         grid_spec=pltpu.PrefetchScalarGridSpec(
             num_scalar_prefetch=1,
             grid=(2, 2),
-            in_specs=[blk(2, 0)] * PIECES
+            in_specs=[blk(2)] * PIECES
             + [
                 pl.BlockSpec((1, 3, WIDE), lambda c, b, o: (b, 0, c)),
                 params_spec,
@@ -317,10 +316,12 @@
         name="first_pass",
     )(order, *pieces, tail, params, rate, inflow)
 
-    message, far = lax.optimization_barrier((message, far))
+    message, far, gates, gate_input = lax.optimization_barrier((message, far, gates, gate_input))
+    late = [turned(slice_for(gate_input, turn)[None], turn) for turn in turns[4:]]
     sections = lax.all_to_all(message, ("z", "x"), 0, 0, tiled=True)
     own_0, far_0 = attend(0, info, received, far, kv_all)
-    sections, own_0, far_0 = lax.optimization_barrier((sections, own_0, far_0))
+    sections, own_0, far_0, late = lax.optimization_barrier((sections, own_0, far_0, late))
+    gates = gates + late
     back_0 = lax.ppermute(far_0, "z", mirror)
     chunk = (z * nx + x) % 16
     rate_chunk = lax.dynamic_slice_in_dim(rate_rows, chunk * LANES, LANES, 1)
@@ -342,7 +343,7 @@
         grid_spec=pltpu.PrefetchScalarGridSpec(
             num_scalar_prefetch=1,
             grid=(2, 2),
-            in_specs=[blk(1, 2)] * PIECES
+            in_specs=[blk(1)] * PIECES
             + [
                 slab,
                 slab,
@@ -362,8 +363,9 @@
         ),
         out_shape=jax.ShapeDtypeStruct((2, SPAN, half), BF16),
         name="second_pass",
-    )(order, *pieces, dt, conv, params, rate, inflow, readout, entering, lengths)
-
+    )(order, *gates, dt, conv, params, rate, inflow, readout, entering, lengths)
+
+    mixed, back_1 = lax.optimization_barrier((mixed, back_1))
     rows = SPAN // 2
     own = lax.dynamic_slice_in_dim(mixed, core * rows, rows, 1)
     away = lax.dynamic_slice_in_dim(mixed, (1 - core) * rows, rows, 1)

time: 212 us -> 194 us (0.915)
  waiting for transfers between devices: 47.8 us -> 33.6 us
  other arithmetic: 17.4 us -> 11 us
  starting transfers between devices: 52.1 us -> 57.5 us
  local copies, waits for them, and re-layouts: 19.2 us -> 16.5 us
    ppermute x8 -> x15, starting transfers between devices: 12.2 us -> 25.4 us  [the longest x14 19.4 us: turned(): return block if dc + dh == 0 else lax.ppermute(block, group, route)]
    all_to_all x1, waiting for transfers between devices: 11.6 us -> 0.01 us  [shards(): received = lax.all_to_all(packed, ('x', 'head'), 0, 0, tiled=True)]
    ppermute x1, waiting for transfers between devices: 7.53 us -> 0.01 us  [shards(): back_1 = lax.ppermute(far_1, 'z', mirror)]
    all_to_all x1, starting transfers between devices: 11.4 us -> 4.79 us  [shards(): sections = lax.all_to_all(message, ('z', 'x'), 0, 0, tiled=True)]
    another operation x8, other arithmetic: 8.21 us -> 2.32 us  [shards(): jnp.stack([slice_for(mixer_input, turn), slice_for(step_input, turn)])]
    ppermute x8 -> x15, waiting for transfers between devices: 14.7 us -> 20.5 us  [the longest x14 20.5 us: turned(): return block if dc + dh == 0 else lax.ppermute(block, group, route)]
    all_to_all x1, starting transfers between devices: 7.03 us -> 4.58 us  [shards(): received = lax.all_to_all(packed, ('x', 'head'), 0, 0, tiled=True)]
  transfers between devices with their start and end apart: 18 -> 25, of which waited for: 5 -> 6; matrix products, arithmetic and copies ran while one was open for 15% -> 11% of each run, Pallas kernels for 20% -> 30%
where the time goes in v3:
time: 194 us; the launch traced here: 193 us
  Pallas kernels  60.1 us (31%)
  starting transfers between devices  57.5 us (30%)
  waiting for transfers between devices  33.6 us (17%)
  local copies, waits for them, and re-layouts  16.5 us (9%)
  between operations  14.8 us (8%)
  other arithmetic  11 us (6%)
    pallas_call x2, Pallas kernels, attend(): pl.pallas_call(attend_pass, grid_spec=pltpu.PrefetchScalarGridSpec(num_sc...  26.7 us
    ppermute x14, waiting for transfers between devices, turned(): return block if dc + dh == 0 else lax.ppermute(block, group, route)  20.5 us
    ppermute x14, starting transfers between devices, turned(): return block if dc + dh == 0 else lax.ppermute(block, group, route)  19.4 us
    pallas_call x1, Pallas kernels, shards(): pl.pallas_call(second_pass, grid_spec=pltpu.PrefetchScalarGridSpec(num_sc...  15 us
    pallas_call x1, Pallas kernels, shards(): pl.pallas_call(first_pass, grid_spec=pltpu.PrefetchScalarGridSpec(num_sca...  14.8 us
    all_to_all x1, starting transfers between devices, shards(): entering = lax.all_to_all(prefix, ('z', 'x'), 0, 0, tiled=True)  9.78 us
    all_to_all x1, waiting for transfers between devices, shards(): home = lax.all_to_all(attended, 'x', 0, 0, tiled=True)  8.43 us
    ppermute x1, starting transfers between devices, shards(): far = lax.ppermute(far, 'z', mirror)  6.04 us
  transfers between devices with their start and end apart: 25, of which 6 were waited for; matrix products, arithmetic and copies ran while one was open for 11% of the time, Pallas kernels for 30%

profile of v3, /device:TPU:32, one launch (start us, length us, event | category | flops | bytes accessed | tf_op | source)
XLA Modules:
  0.0 193.4 jit_solution(6174840454593288801)
XLA Ops:
  7.3 1.8 dynamic-slice_bitcast_fusion.8
  9.1 0.1 collective-permute-start.3
  9.2 3.1 %collective-permute-start.2 = (bf16[2,2,16,2048]{3,2,1,0:T(8,128)(2,1)S(1)}, bf16[2,2,16,2048]{3,2,1,0:T(8,128)(2,1)S(1)}, u32[]{:S(2)}, u32[]{:S(2)}) collective-permute-start(bf16[2,2,16,2048]{3,2,1,0:T(8,128)(2,1)S(1)} %pad_maximum_fusion.6), channel_id=1, source_target_pairs={{0,3},{1,0},{2,1},{3,2},{4,7},{5,4},{6,5},{7,6},{8,11},{9,8},{10,9... | collective-permute-start | bytes 786440 | tf_op jit(solution)/shard_map/ppermute | solution.py:231
  12.3 2.0 %shard_map.140 = bf16[16,16,1280]{2,1,0:T(8,128)(2,1)} custom-call(bf16[2,16,8192]{2,1,0:T(8,128)(2,1)} %q.1, bf16[2,16,1024]{2,1,0:T(8,128)(2,1)} %k.1, bf16[2,16,1024]{2,1,0:T(8,128)(2,1)} %v.1), custom_call_target="tpu_custom_call" | custom-call | tf_op jit(solution)/shard_map/pallas_call | solution.py:238
  14.3 4.6 %all-to-all-start = ((bf16[16,16,1280]{2,1,0:T(8,128)(2,1)}), bf16[16,16,1280]{2,1,0:T(8,128)(2,1)S(1)}, u32[]{:S(2)}, u32[]{:S(2)}) async-start(bf16[16,16,1280]{2,1,0:T(8,128)(2,1)} %shard_map.140), calls=%async_computation | async-start | bytes 1310720 | tf_op jit(solution)/shard_map/all_to_all | solution.py:244
  18.9 3.5 %collective-permute-start.1 = (bf16[2,2,16,2048]{3,2,1,0:T(8,128)(2,1)S(1)}, bf16[2,2,16,2048]{3,2,1,0:T(8,128)(2,1)S(1)}, u32[]{:S(2)}, u32[]{:S(2)}) collective-permute-start(bf16[2,2,16,2048]{3,2,1,0:T(8,128)(2,1)S(1)} %pad_maximum_fusion.5), channel_id=1, source_target_pairs={{0,2},{1,3},{2,0},{3,1},{4,6},{5,7},{6,4},{7,5},{8,10},{9,11},{10,... | collective-permute-start | bytes 786440 | tf_op jit(solution)/shard_map/ppermute | solution.py:231
  22.5 0.6 collective-permute-start
  23.2 13.5 %collective-permute-done.1.refs_2_ = bf16[2,2,16,2048]{3,2,1,0:T(8,128)(2,1)S(1)} collective-permute-done((bf16[2,2,16,2048]{3,2,1,0:T(8,128)(2,1)S(1)}, bf16[2,2,16,2048]{3,2,1,0:T(8,128)(2,1)S(1)}, u32[]{:S(2)}, u32[]{:S(2)}) %collective-permute-start.1) | collective-permute-done | bytes 262176 | tf_op jit(solution)/shard_map/ppermute | solution.py:231
  36.7 4.4 %collective-permute-done.refs_1_ = bf16[2,2,16,2048]{3,2,1,0:T(8,128)(2,1)S(1)} collective-permute-done((bf16[2,2,16,2048]{3,2,1,0:T(8,128)(2,1)S(1)}, bf16[2,2,16,2048]{3,2,1,0:T(8,128)(2,1)S(1)}, u32[]{:S(2)}, u32[]{:S(2)}) %collective-permute-start) | collective-permute-done | bytes 262176 | tf_op jit(solution)/shard_map/ppermute | solution.py:231
  41.1 0.7 copy-done.10
  41.8 0.7 slice.69
  42.5 0.7 pad_maximum_fusion.9
  43.2 0.7 pad_maximum_fusion.10
  44.0 3.2 %collective-permute-start.6 = (bf16[2,2,16,2048]{3,2,1,0:T(8,128)(2,1)}, bf16[2,2,16,2048]{3,2,1,0:T(8,128)(2,1)S(1)}, u32[]{:S(2)}, u32[]{:S(2)}) collective-permute-start(bf16[2,2,16,2048]{3,2,1,0:T(8,128)(2,1)} %pad_maximum_fusion.10), channel_id=1, source_target_pairs={{0,7},{1,4},{2,5},{3,6},{4,3},{5,0},{6,1},{7,2},{8,15},{9,12},{10,... | collective-permute-start | bytes 786440 | tf_op jit(solution)/shard_map/ppermute | solution.py:231
  47.1 0.7 pad_maximum_fusion.8
  47.9 0.7 dynamic-slice_convert_fusion
  48.6 1.6 exponential_multiply_fusion
  50.2 0.9 fusion.5
  51.2 0.7 dynamic_slice.117
  51.9 0.7 dynamic_slice.118
  52.6 0.7 dynamic_slice.119
  53.4 0.7 copy.23
  54.0 1.3 dynamic_slice.125
  55.3 0.7 concatenate.18.refs_9_.refs_10_
  56.0 0.6 stack.133.order
  56.7 0.4 collective-permute-done.6.refs_7_
  57.0 2.2 %collective-permute-done.4.refs_5_ = bf16[2,2,16,2048]{3,2,1,0:T(8,128)(2,1)} collective-permute-done((bf16[2,2,16,2048]{3,2,1,0:T(8,128)(2,1)}, bf16[2,2,16,2048]{3,2,1,0:T(8,128)(2,1)}, u32[]{:S(2)}, u32[]{:S(2)}) %collective-permute-start.4) | collective-permute-done | bytes 262176 | tf_op jit(solution)/shard_map/ppermute | solution.py:231
  59.3 1.0 fusion.1
  60.3 3.4 %collective-permute-start.7 = (bf16[2,3,2048]{2,1,0:T(4,128)(2,1)S(1)}, bf16[2,3,2048]{2,1,0:T(4,128)(2,1)S(1)}, u32[]{:S(2)}, u32[]{:S(2)}) collective-permute-start(bf16[2,3,2048]{2,1,0:T(4,128)(2,1)S(1)} %fusion.1), channel_id=1, source_target_pairs={{0,8},{8,16},{16,24},{24,32},{32,40},{40,48},{48,56},{56,64},{64,7... | collective-permute-start | bytes 73736 | tf_op jit(solution)/shard_map/ppermute | solution.py:251
  63.8 4.6 %collective-permute-done.7.refs_8_ = bf16[2,3,2048]{2,1,0:T(4,128)(2,1)S(1)} collective-permute-done((bf16[2,3,2048]{2,1,0:T(4,128)(2,1)S(1)}, bf16[2,3,2048]{2,1,0:T(4,128)(2,1)S(1)}, u32[]{:S(2)}, u32[]{:S(2)}) %collective-permute-start.7) | collective-permute-done | bytes 24608 | tf_op jit(solution)/shard_map/ppermute | solution.py:251
  68.4 0.6 copy-done.22
  69.0 6.0 %collective-permute-start.9 = (bf16[4,64,512]{2,1,0:T(8,128)(2,1)S(1)}, bf16[4,64,512]{2,1,0:T(8,128)(2,1)S(1)}, u32[]{:S(2)}, u32[]{:S(2)}) collective-permute-start(bf16[4,64,512]{2,1,0:T(8,128)(2,1)S(1)} %slice.64), channel_id=1, source_target_pairs={{0,224},{32,192},{64,160},{96,128},{128,96},{160,64},{192,32},{224... | collective-permute-start | bytes 786440 | tf_op jit(solution)/shard_map/ppermute | solution.py:261
  75.1 0.7 dynamic-slice_bitcast_fusion.4
  75.8 0.2 collective-permute-start.10
  76.0 1.9 collective-permute-start.11
  77.9 1.7 collective-permute-start.12
  79.6 0.1 copy.19
  79.7 0.1 broadcast_in_dim.68
  79.8 2.0 %broadcast_in_dim.69.refs_11_.refs_12_ = f32[2,2048,128]{2,1,0:T(8,128)} broadcast(f32[2,2048]{1,0:T(2,128)S(1)} %broadcast_in_dim.68), dimensions={0,1} | broadcast | bytes 2113536 | tf_op jit(solution)/shard_map/broadcast_in_dim | solution.py:268
  81.8 14.8 %first_pass.1 = (f32[2,2,1024,128]{3,2,1,0:T(8,128)}, f32[2,2,1024,128]{3,2,1,0:T(8,128)}, bf16[32,24,128]{2,1,0:T(8,128)(2,1)}) custom-call(s32[9]{0:T(128)} %stack.133.order, bf16[2,2,16,2048]{3,2,1,0:T(8,128)(2,1)} %copy-done.2, bf16[2,2,16,2048]{3,2,1,0:T(8,128)(2,1)} %copy-done.10, bf16[2,2,16,2048]{3,2,1,0:T(8,128)(2,1)} %copy-done.9, ...), custom_call_target="tpu_custom_call" | custom-call | tf_op jit(solution)/shard_map/first_pass/pallas_call | solution.py:292
  96.7 4.8 %all-to-all-start.1 = ((bf16[32,24,128]{2,1,0:T(8,128)(2,1)}), bf16[32,24,128]{2,1,0:T(8,128)(2,1)S(1)}, u32[]{:S(2)}, u32[]{:S(2)}) async-start(bf16[32,24,128]{2,1,0:T(8,128)(2,1)} %get-tuple-element.54), calls=%async_computation.1 | async-start | bytes 393216 | tf_op jit(solution)/shard_map/all_to_all | solution.py:321
  101.5 0.3 collective-permute-start.13
  101.8 0.5 collective-permute-start.14
  102.3 1.9 collective-permute-start.15
  104.3 2.4 %collective-permute-start.16 = (bf16[1,2,16,2048]{3,2,1,0:T(8,128)(2,1)S(1)}, bf16[1,2,16,2048]{3,2,1,0:T(8,128)(2,1)S(1)}, u32[]{:S(2)}, u32[]{:S(2)}) collective-permute-start(bf16[1,2,16,2048]{3,2,1,0:T(8,128)(2,1)S(1)} %get-tuple-element.80), channel_id=1, source_target_pairs={{0,7},{1,4},{2,5},{3,6},{4,3},{5,0},{6,1},{7,2},{8,15},{9,12},{10,... | collective-permute-start | bytes 393224 | tf_op jit(solution)/shard_map/ppermute | solution.py:231
  106.6 1.3 pad_add_fusion.info
  107.9 1.3 constant_dynamic-slice_fusion.1.rate
  109.2 13.3 %attend_pass.2 = (bf16[4,64,256]{2,1,0:T(8,128)(2,1)}, bf16[4,64,256]{2,1,0:T(8,128)(2,1)}) custom-call(s32[4]{0:T(128)} %pad_add_fusion.info, bf16[4,64,1280]{2,1,0:T(8,128)(2,1)} %bitcast.88, bf16[4,64,512]{2,1,0:T(8,128)(2,1)} %copy-done.3, bf16[16,256,256]{2,1,0:T(8,128)(2,1)} %all-gather.2.cloned.1.call-done.kv_ref), custom_call_target="tpu_custom_call" | custom-call | tf_op jit(solution)/shard_map/attend_pass/pallas_call | solution.py:182
  122.7 0.8 copy-done.5
  123.4 1.7 prefix_pass.1
  125.1 9.8 %all-to-all-start.2 = ((bf16[32,16,128]{2,1,0:T(8,128)(2,1)}), bf16[32,16,128]{2,1,0:T(8,128)(2,1)S(1)}, u32[]{:S(2)}, u32[]{:S(2)}) async-start(bf16[32,16,128]{2,1,0:T(8,128)(2,1)} %prefix_pass.1), calls=%async_computation.2 | async-start | bytes 262144 | tf_op jit(solution)/shard_map/all_to_all | solution.py:336
  134.9 3.7 %collective-permute-start.17 = (bf16[4,64,256]{2,1,0:T(8,128)(2,1)}, bf16[4,64,256]{2,1,0:T(8,128)(2,1)S(1)}, u32[]{:S(2)}, u32[]{:S(2)}) collective-permute-start(bf16[4,64,256]{2,1,0:T(8,128)(2,1)} %get-tuple-element.70), channel_id=1, source_target_pairs={{0,224},{32,192},{64,160},{96,128},{128,96},{160,64},{192,32},{224... | collective-permute-start | bytes 393224 | tf_op jit(solution)/shard_map/ppermute | solution.py:325
  138.6 13.4 %attend_pass.3 = (bf16[4,64,256]{2,1,0:T(8,128)(2,1)}, bf16[4,64,256]{2,1,0:T(8,128)(2,1)}) custom-call(s32[4]{0:T(128)} %pad_add_fusion.info, bf16[4,64,1280]{2,1,0:T(8,128)(2,1)} %bitcast.89, bf16[4,64,512]{2,1,0:T(8,128)(2,1)} %copy-done.3, bf16[16,256,256]{2,1,0:T(8,128)(2,1)} %all-gather.2.cloned.1.call-done.kv_ref), custom_call_target="tpu_custom_call" | custom-call | tf_op jit(solution)/shard_map/attend_pass/pallas_call | solution.py:182
  151.9 1.5 collective-permute-start.18
  153.4 0.1 copy.20
  153.5 0.1 broadcast_in_dim.78
  153.7 2.0 %broadcast_in_dim.79.refs_13_ = f32[2,2048,128]{2,1,0:T(8,128)} broadcast(f32[2,2048]{1,0:T(2,128)S(1)} %broadcast_in_dim.78), dimensions={0,1} | broadcast | bytes 2113536 | tf_op jit(solution)/shard_map/broadcast_in_dim | solution.py:269
  155.7 15.0 %second_pass.1 = bf16[2,128,2048]{2,1,0:T(8,128)(2,1)} custom-call(s32[9]{0:T(128)} %stack.133.order, bf16[1,2,16,2048]{3,2,1,0:T(8,128)(2,1)} %get-tuple-element.50.refs_0_, bf16[1,2,16,2048]{3,2,1,0:T(8,128)(2,1)} %copy-done.13, bf16[1,2,16,2048]{3,2,1,0:T(8,128)(2,1)} %copy-done.14, bf16[1,2,16,2048]{3,2,1,0:T(8,128)(2,1)} %copy-done.15, ...), custom_call_target="tpu_custom_call" | custom-call | tf_op jit(solution)/shard_map/second_pass/pallas_call | solution.py:341
  170.7 0.9 pad_maximum_fusion.1
  171.5 4.2 %all-to-all-start.3 = ((bf16[4,64,1024]{2,1,0:T(8,128)(2,1)}), bf16[4,64,1024]{2,1,0:T(8,128)(2,1)S(1)}, u32[]{:S(2)}, u32[]{:S(2)}) async-start(bf16[4,64,1024]{2,1,0:T(8,128)(2,1)} %pad_maximum_fusion.1), calls=%async_computation.3 | async-start | bytes 1048576 | tf_op jit(solution)/shard_map/all_to_all | solution.py:378
  175.9 8.4 %all-to-all-done.3 = bf16[4,64,1024]{2,1,0:T(8,128)(2,1)S(1)} async-done(((bf16[4,64,1024]{2,1,0:T(8,128)(2,1)}), bf16[4,64,1024]{2,1,0:T(8,128)(2,1)S(1)}, u32[]{:S(2)}, u32[]{:S(2)}) %all-to-all-start.3) | async-done | bytes 524320 | tf_op jit(solution)/shard_map/all_to_all | solution.py:378
  184.4 0.8 pad_maximum_fusion.2
  185.3 0.2 broadcast_select_fusion.1
  185.5 1.0 pad_maximum_fusion
  (86 shorter events, 0.7 us)
Async XLA Ops:
  9.1 14.1 %collective-permute-start.3 = (bf16[2,2,16,2048]{3,2,1,0:T(8,128)(2,1)S(1)}, bf16[2,2,16,2048]{3,2,1,0:T(8,128)(2,1)S(1)}, u32[]{:S(2)}, u32[]{:S(2)}) collective-permute-start(bf16[2,2,16,2048]{3,2,1,0:T(8,128)(2,1)S(1)} %pad_maximum_fusion.7), channel_id=1, source_target_pairs={{0,4},{1,5},{2,6},{3,7},{4,0},{5,1},{6,2},{7,3},{8,12},{9,13},{10,... | collective-permute-start | bytes 786440 | tf_op jit(solution)/shard_map/ppermute | solution.py:231
  9.2 14.0 %collective-permute-start.2 = (bf16[2,2,16,2048]{3,2,1,0:T(8,128)(2,1)S(1)}, bf16[2,2,16,2048]{3,2,1,0:T(8,128)(2,1)S(1)}, u32[]{:S(2)}, u32[]{:S(2)}) collective-permute-start(bf16[2,2,16,2048]{3,2,1,0:T(8,128)(2,1)S(1)} %pad_maximum_fusion.6), channel_id=1, source_target_pairs={{0,3},{1,0},{2,1},{3,2},{4,7},{5,4},{6,5},{7,6},{8,11},{9,8},{10,9... | collective-permute-start | bytes 786440 | tf_op jit(solution)/shard_map/ppermute | solution.py:231
  14.3 26.9 %all-to-all-start = ((bf16[16,16,1280]{2,1,0:T(8,128)(2,1)}), bf16[16,16,1280]{2,1,0:T(8,128)(2,1)S(1)}, u32[]{:S(2)}, u32[]{:S(2)}) async-start(bf16[16,16,1280]{2,1,0:T(8,128)(2,1)} %shard_map.140), calls=%async_computation | async-start | bytes 1310720 | tf_op jit(solution)/shard_map/all_to_all | solution.py:244
  18.8 29.0 %copy-start.23 = (bf16[2,64,32]{1,2,0:T(8,128)(2,1)S(1)}, bf16[2,64,32]{1,2,0:T(8,128)(2,1)}, u32[]{:S(2)}) copy-start(bf16[2,64,32]{1,2,0:T(8,128)(2,1)} %param.16) | copy-start | bytes 24580
  18.9 90.4 %all-gather.2.cloned.1.call-start = ((), (), s32[]{:S(2)}) async-start(), calls=%async_computation.4 | async-start | bytes 2228224 | tf_op jit(solution)/shard_map/all_gather | solution.py:254
  18.9 17.7 %collective-permute-start.1 = (bf16[2,2,16,2048]{3,2,1,0:T(8,128)(2,1)S(1)}, bf16[2,2,16,2048]{3,2,1,0:T(8,128)(2,1)S(1)}, u32[]{:S(2)}, u32[]{:S(2)}) collective-permute-start(bf16[2,2,16,2048]{3,2,1,0:T(8,128)(2,1)S(1)} %pad_maximum_fusion.5), channel_id=1, source_target_pairs={{0,2},{1,3},{2,0},{3,1},{4,6},{5,7},{6,4},{7,5},{8,10},{9,11},{10,... | collective-permute-start | bytes 786440 | tf_op jit(solution)/shard_map/ppermute | solution.py:231
  22.5 18.6 %collective-permute-start = (bf16[2,2,16,2048]{3,2,1,0:T(8,128)(2,1)S(1)}, bf16[2,2,16,2048]{3,2,1,0:T(8,128)(2,1)S(1)}, u32[]{:S(2)}, u32[]{:S(2)}) collective-permute-start(bf16[2,2,16,2048]{3,2,1,0:T(8,128)(2,1)S(1)} %pad_maximum_fusion.4), channel_id=1, source_target_pairs={{0,1},{1,2},{2,3},{3,0},{4,5},{5,6},{6,7},{7,4},{8,9},{9,10},{10,1... | collective-permute-start | bytes 786440 | tf_op jit(solution)/shard_map/ppermute | solution.py:231
  23.2 40.6 %copy-start.2 = (bf16[2,2,16,2048]{3,2,1,0:T(8,128)(2,1)}, bf16[2,2,16,2048]{3,2,1,0:T(8,128)(2,1)S(1)}, u32[]{:S(2)}) copy-start(bf16[2,2,16,2048]{3,2,1,0:T(8,128)(2,1)S(1)} %pad_maximum_fusion.3.refs_0_) | copy-start | bytes 786436
  23.2 40.6 %copy-start.7 = (bf16[2,2,16,2048]{3,2,1,0:T(8,128)(2,1)}, bf16[2,2,16,2048]{3,2,1,0:T(8,128)(2,1)S(1)}, u32[]{:S(2)}) copy-start(bf16[2,2,16,2048]{3,2,1,0:T(8,128)(2,1)S(1)} %collective-permute-done.3.refs_4_) | copy-start | bytes 786436
  23.2 40.6 %copy-start.8 = (bf16[2,2,16,2048]{3,2,1,0:T(8,128)(2,1)}, bf16[2,2,16,2048]{3,2,1,0:T(8,128)(2,1)S(1)}, u32[]{:S(2)}) copy-start(bf16[2,2,16,2048]{3,2,1,0:T(8,128)(2,1)S(1)} %collective-permute-done.2.refs_3_) | copy-start | bytes 786436
  36.7 27.2 %copy-start.9 = (bf16[2,2,16,2048]{3,2,1,0:T(8,128)(2,1)}, bf16[2,2,16,2048]{3,2,1,0:T(8,128)(2,1)S(1)}, u32[]{:S(2)}) copy-start(bf16[2,2,16,2048]{3,2,1,0:T(8,128)(2,1)S(1)} %collective-permute-done.1.refs_2_) | copy-start | bytes 786436
  41.1 0.7 copy-start.10
  41.1 22.7 %copy-start = (bf16[16,16,1280]{2,1,0:T(8,128)(2,1)}, bf16[16,16,1280]{2,1,0:T(8,128)(2,1)S(1)}, u32[]{:S(2)}) copy-start(bf16[16,16,1280]{2,1,0:T(8,128)(2,1)S(1)} %all-to-all-done) | copy-start | bytes 1966084
  42.5 32.6 %copy-start.4 = (bf16[2,16,16384]{2,1,0:T(8,128)(2,1)S(1)}, bf16[2,16,16384]{2,1,0:T(8,128)(2,1)}, u32[]{:S(2)}) copy-start(bf16[2,16,16384]{2,1,0:T(8,128)(2,1)} %param.14) | copy-start | bytes 3145732
  43.2 13.4 %collective-permute-start.5 = (bf16[2,2,16,2048]{3,2,1,0:T(8,128)(2,1)}, bf16[2,2,16,2048]{3,2,1,0:T(8,128)(2,1)S(1)}, u32[]{:S(2)}, u32[]{:S(2)}) collective-permute-start(bf16[2,2,16,2048]{3,2,1,0:T(8,128)(2,1)} %pad_maximum_fusion.9), channel_id=1, source_target_pairs={{0,6},{1,7},{2,4},{3,5},{4,2},{5,3},{6,0},{7,1},{8,14},{9,15},{10,... | collective-permute-start | bytes 786440 | tf_op jit(solution)/shard_map/ppermute | solution.py:231
  44.0 13.1 %collective-permute-start.6 = (bf16[2,2,16,2048]{3,2,1,0:T(8,128)(2,1)}, bf16[2,2,16,2048]{3,2,1,0:T(8,128)(2,1)S(1)}, u32[]{:S(2)}, u32[]{:S(2)}) collective-permute-start(bf16[2,2,16,2048]{3,2,1,0:T(8,128)(2,1)} %pad_maximum_fusion.10), channel_id=1, source_target_pairs={{0,7},{1,4},{2,5},{3,6},{4,3},{5,0},{6,1},{7,2},{8,15},{9,12},{10,... | collective-permute-start | bytes 786440 | tf_op jit(solution)/shard_map/ppermute | solution.py:231
  47.9 11.4 %collective-permute-start.4 = (bf16[2,2,16,2048]{3,2,1,0:T(8,128)(2,1)}, bf16[2,2,16,2048]{3,2,1,0:T(8,128)(2,1)}, u32[]{:S(2)}, u32[]{:S(2)}) collective-permute-start(bf16[2,2,16,2048]{3,2,1,0:T(8,128)(2,1)} %pad_maximum_fusion.8), channel_id=1, source_target_pairs={{0,5},{1,6},{2,7},{3,4},{4,1},{5,2},{6,3},{7,0},{8,13},{9,14},{10,... | collective-permute-start | bytes 786440 | tf_op jit(solution)/shard_map/ppermute | solution.py:231
  47.9 8.8 %collective-permute-start.8 = (bf16[2,64,32]{1,2,0:T(8,128)(2,1)S(1)}, bf16[2,64,32]{1,2,0:T(8,128)(2,1)S(1)}, u32[]{:S(2)}, u32[]{:S(2)}) collective-permute-start(bf16[2,64,32]{1,2,0:T(8,128)(2,1)S(1)} %copy-done.23), channel_id=1, source_target_pairs={{0,4},{4,0},{1,5},{5,1},{2,6},{6,2},{3,7},{7,3},{8,12},{12,8},{9,1... | collective-permute-start | bytes 24584 | tf_op jit(solution)/shard_map/ppermute | solution.py:264
  56.6 25.1 %copy-start.11 = (bf16[2,2,16,2048]{3,2,1,0:T(8,128)(2,1)}, bf16[2,2,16,2048]{3,2,1,0:T(8,128)(2,1)S(1)}, u32[]{:S(2)}) copy-start(bf16[2,2,16,2048]{3,2,1,0:T(8,128)(2,1)S(1)} %collective-permute-done.5.refs_6_) | copy-start | bytes 786436
  57.0 24.7 %copy-start.12 = (bf16[2,2,16,2048]{3,2,1,0:T(8,128)(2,1)}, bf16[2,2,16,2048]{3,2,1,0:T(8,128)(2,1)S(1)}, u32[]{:S(2)}) copy-start(bf16[2,2,16,2048]{3,2,1,0:T(8,128)(2,1)S(1)} %collective-permute-done.6.refs_7_) | copy-start | bytes 786436
  60.3 8.1 %collective-permute-start.7 = (bf16[2,3,2048]{2,1,0:T(4,128)(2,1)S(1)}, bf16[2,3,2048]{2,1,0:T(4,128)(2,1)S(1)}, u32[]{:S(2)}, u32[]{:S(2)}) collective-permute-start(bf16[2,3,2048]{2,1,0:T(4,128)(2,1)S(1)} %fusion.1), channel_id=1, source_target_pairs={{0,8},{8,16},{16,24},{24,32},{32,40},{40,48},{48,56},{56,64},{64,7... | collective-permute-start | bytes 73736 | tf_op jit(solution)/shard_map/ppermute | solution.py:251
  68.4 0.6 copy-start.22
  69.0 27.6 %collective-permute-start.9 = (bf16[4,64,512]{2,1,0:T(8,128)(2,1)S(1)}, bf16[4,64,512]{2,1,0:T(8,128)(2,1)S(1)}, u32[]{:S(2)}, u32[]{:S(2)}) collective-permute-start(bf16[4,64,512]{2,1,0:T(8,128)(2,1)S(1)} %slice.64), channel_id=1, source_target_pairs={{0,224},{32,192},{64,160},{96,128},{128,96},{160,64},{192,32},{224... | collective-permute-start | bytes 786440 | tf_op jit(solution)/shard_map/ppermute | solution.py:261
  75.8 20.8 %collective-permute-start.10 = (bf16[1,2,16,2048]{3,2,1,0:T(8,128)(2,1)S(1)}, bf16[1,2,16,2048]{3,2,1,0:T(8,128)(2,1)S(1)}, u32[]{:S(2)}, u32[]{:S(2)}) collective-permute-start(bf16[1,2,16,2048]{3,2,1,0:T(8,128)(2,1)S(1)} %get-tuple-element.86), channel_id=1, source_target_pairs={{0,1},{1,2},{2,3},{3,0},{4,5},{5,6},{6,7},{7,4},{8,9},{9,10},{10,1... | collective-permute-start | bytes 393224 | tf_op jit(solution)/shard_map/ppermute | solution.py:231
  76.0 20.6 %collective-permute-start.11 = (bf16[1,2,16,2048]{3,2,1,0:T(8,128)(2,1)S(1)}, bf16[1,2,16,2048]{3,2,1,0:T(8,128)(2,1)S(1)}, u32[]{:S(2)}, u32[]{:S(2)}) collective-permute-start(bf16[1,2,16,2048]{3,2,1,0:T(8,128)(2,1)S(1)} %get-tuple-element.85), channel_id=1, source_target_pairs={{0,2},{1,3},{2,0},{3,1},{4,6},{5,7},{6,4},{7,5},{8,10},{9,11},{10,... | collective-permute-start | bytes 393224 | tf_op jit(solution)/shard_map/ppermute | solution.py:231
  77.9 18.7 %collective-permute-start.12 = (bf16[1,2,16,2048]{3,2,1,0:T(8,128)(2,1)S(1)}, bf16[1,2,16,2048]{3,2,1,0:T(8,128)(2,1)S(1)}, u32[]{:S(2)}, u32[]{:S(2)}) collective-permute-start(bf16[1,2,16,2048]{3,2,1,0:T(8,128)(2,1)S(1)} %get-tuple-element.84), channel_id=1, source_target_pairs={{0,3},{1,0},{2,1},{3,2},{4,7},{5,4},{6,5},{7,6},{8,11},{9,8},{10,9... | collective-permute-start | bytes 393224 | tf_op jit(solution)/shard_map/ppermute | solution.py:231
  96.6 25.9 %copy-start.13 = (bf16[1,2,16,2048]{3,2,1,0:T(8,128)(2,1)}, bf16[1,2,16,2048]{3,2,1,0:T(8,128)(2,1)S(1)}, u32[]{:S(2)}) copy-start(bf16[1,2,16,2048]{3,2,1,0:T(8,128)(2,1)S(1)} %collective-permute-done.10.refs_1_) | copy-start | bytes 393220
  96.6 25.9 %copy-start.14 = (bf16[1,2,16,2048]{3,2,1,0:T(8,128)(2,1)}, bf16[1,2,16,2048]{3,2,1,0:T(8,128)(2,1)S(1)}, u32[]{:S(2)}) copy-start(bf16[1,2,16,2048]{3,2,1,0:T(8,128)(2,1)S(1)} %collective-permute-done.11.refs_2_) | copy-start | bytes 393220
  96.6 25.9 %copy-start.15 = (bf16[1,2,16,2048]{3,2,1,0:T(8,128)(2,1)}, bf16[1,2,16,2048]{3,2,1,0:T(8,128)(2,1)S(1)}, u32[]{:S(2)}) copy-start(bf16[1,2,16,2048]{3,2,1,0:T(8,128)(2,1)S(1)} %collective-permute-done.12.refs_3_) | copy-start | bytes 393220
  96.7 12.6 %copy-start.3 = (bf16[4,64,512]{2,1,0:T(8,128)(2,1)}, bf16[4,64,512]{2,1,0:T(8,128)(2,1)S(1)}, u32[]{:S(2)}) copy-start(bf16[4,64,512]{2,1,0:T(8,128)(2,1)S(1)} %collective-permute-done.9.far_ref) | copy-start | bytes 786436
  96.7 26.0 %all-to-all-start.1 = ((bf16[32,24,128]{2,1,0:T(8,128)(2,1)}), bf16[32,24,128]{2,1,0:T(8,128)(2,1)S(1)}, u32[]{:S(2)}, u32[]{:S(2)}) async-start(bf16[32,24,128]{2,1,0:T(8,128)(2,1)} %get-tuple-element.54), calls=%async_computation.1 | async-start | bytes 393216 | tf_op jit(solution)/shard_map/all_to_all | solution.py:321
  101.5 21.0 %collective-permute-start.13 = (bf16[1,2,16,2048]{3,2,1,0:T(8,128)(2,1)S(1)}, bf16[1,2,16,2048]{3,2,1,0:T(8,128)(2,1)S(1)}, u32[]{:S(2)}, u32[]{:S(2)}) collective-permute-start(bf16[1,2,16,2048]{3,2,1,0:T(8,128)(2,1)S(1)} %get-tuple-element.83), channel_id=1, source_target_pairs={{0,4},{1,5},{2,6},{3,7},{4,0},{5,1},{6,2},{7,3},{8,12},{9,13},{10,... | collective-permute-start | bytes 393224 | tf_op jit(solution)/shard_map/ppermute | solution.py:231
  101.8 20.8 %collective-permute-start.14 = (bf16[1,2,16,2048]{3,2,1,0:T(8,128)(2,1)S(1)}, bf16[1,2,16,2048]{3,2,1,0:T(8,128)(2,1)S(1)}, u32[]{:S(2)}, u32[]{:S(2)}) collective-permute-start(bf16[1,2,16,2048]{3,2,1,0:T(8,128)(2,1)S(1)} %get-tuple-element.82), channel_id=1, source_target_pairs={{0,5},{1,6},{2,7},{3,4},{4,1},{5,2},{6,3},{7,0},{8,13},{9,14},{10,... | collective-permute-start | bytes 393224 | tf_op jit(solution)/shard_map/ppermute | solution.py:231
  102.3 20.2 %collective-permute-start.15 = (bf16[1,2,16,2048]{3,2,1,0:T(8,128)(2,1)S(1)}, bf16[1,2,16,2048]{3,2,1,0:T(8,128)(2,1)S(1)}, u32[]{:S(2)}, u32[]{:S(2)}) collective-permute-start(bf16[1,2,16,2048]{3,2,1,0:T(8,128)(2,1)S(1)} %get-tuple-element.81), channel_id=1, source_target_pairs={{0,6},{1,7},{2,4},{3,5},{4,2},{5,3},{6,0},{7,1},{8,14},{9,15},{10,... | collective-permute-start | bytes 393224 | tf_op jit(solution)/shard_map/ppermute | solution.py:231
  104.3 18.3 %collective-permute-start.16 = (bf16[1,2,16,2048]{3,2,1,0:T(8,128)(2,1)S(1)}, bf16[1,2,16,2048]{3,2,1,0:T(8,128)(2,1)S(1)}, u32[]{:S(2)}, u32[]{:S(2)}) collective-permute-start(bf16[1,2,16,2048]{3,2,1,0:T(8,128)(2,1)S(1)} %get-tuple-element.80), channel_id=1, source_target_pairs={{0,7},{1,4},{2,5},{3,6},{4,3},{5,0},{6,1},{7,2},{8,15},{9,12},{10,... | collective-permute-start | bytes 393224 | tf_op jit(solution)/shard_map/ppermute | solution.py:231
  122.6 33.1 %copy-start.16 = (bf16[1,2,16,2048]{3,2,1,0:T(8,128)(2,1)}, bf16[1,2,16,2048]{3,2,1,0:T(8,128)(2,1)S(1)}, u32[]{:S(2)}) copy-start(bf16[1,2,16,2048]{3,2,1,0:T(8,128)(2,1)S(1)} %collective-permute-done.13.refs_4_) | copy-start | bytes 393220
  122.6 33.0 %copy-start.17 = (bf16[1,2,16,2048]{3,2,1,0:T(8,128)(2,1)}, bf16[1,2,16,2048]{3,2,1,0:T(8,128)(2,1)S(1)}, u32[]{:S(2)}) copy-start(bf16[1,2,16,2048]{3,2,1,0:T(8,128)(2,1)S(1)} %collective-permute-done.14.refs_5_) | copy-start | bytes 393220
  122.6 33.0 %copy-start.18 = (bf16[1,2,16,2048]{3,2,1,0:T(8,128)(2,1)}, bf16[1,2,16,2048]{3,2,1,0:T(8,128)(2,1)S(1)}, u32[]{:S(2)}) copy-start(bf16[1,2,16,2048]{3,2,1,0:T(8,128)(2,1)S(1)} %collective-permute-done.15.refs_6_) | copy-start | bytes 393220
  122.6 33.0 %copy-start.19 = (bf16[1,2,16,2048]{3,2,1,0:T(8,128)(2,1)}, bf16[1,2,16,2048]{3,2,1,0:T(8,128)(2,1)S(1)}, u32[]{:S(2)}) copy-start(bf16[1,2,16,2048]{3,2,1,0:T(8,128)(2,1)S(1)} %collective-permute-done.16.refs_7_) | copy-start | bytes 393220
  122.6 0.8 copy-start.5
  125.1 26.9 %all-to-all-start.2 = ((bf16[32,16,128]{2,1,0:T(8,128)(2,1)}), bf16[32,16,128]{2,1,0:T(8,128)(2,1)S(1)}, u32[]{:S(2)}, u32[]{:S(2)}) async-start(bf16[32,16,128]{2,1,0:T(8,128)(2,1)} %prefix_pass.1), calls=%async_computation.2 | async-start | bytes 262144 | tf_op jit(solution)/shard_map/all_to_all | solution.py:336
  134.9 17.1 %collective-permute-start.17 = (bf16[4,64,256]{2,1,0:T(8,128)(2,1)}, bf16[4,64,256]{2,1,0:T(8,128)(2,1)S(1)}, u32[]{:S(2)}, u32[]{:S(2)}) collective-permute-start(bf16[4,64,256]{2,1,0:T(8,128)(2,1)} %get-tuple-element.70), channel_id=1, source_target_pairs={{0,224},{32,192},{64,160},{96,128},{128,96},{160,64},{192,32},{224... | collective-permute-start | bytes 393224 | tf_op jit(solution)/shard_map/ppermute | solution.py:325
  151.9 3.7 %copy-start.6 = (bf16[32,16,128]{2,1,0:T(8,128)(2,1)}, bf16[32,16,128]{2,1,0:T(8,128)(2,1)S(1)}, u32[]{:S(2)}) copy-start(bf16[32,16,128]{2,1,0:T(8,128)(2,1)S(1)} %all-to-all-done.2.refs_14_) | copy-start | bytes 393220
  151.9 18.7 %collective-permute-start.18 = (bf16[4,64,256]{2,1,0:T(8,128)(2,1)}, bf16[4,64,256]{2,1,0:T(8,128)(2,1)S(1)}, u32[]{:S(2)}, u32[]{:S(2)}) collective-permute-start(bf16[4,64,256]{2,1,0:T(8,128)(2,1)} %get-tuple-element.72), channel_id=1, source_target_pairs={{0,224},{32,192},{64,160},{96,128},{128,96},{160,64},{192,32},{224... | collective-permute-start | bytes 393224 | tf_op jit(solution)/shard_map/ppermute | solution.py:339
  155.6 15.0 %copy-start.20 = (bf16[4,64,256]{2,1,0:T(8,128)(2,1)S(1)}, bf16[4,64,256]{2,1,0:T(8,128)(2,1)}, u32[]{:S(2)}) copy-start(bf16[4,64,256]{2,1,0:T(8,128)(2,1)} %get-tuple-element.74) | copy-start | bytes 393220
  155.7 15.0 %copy-start.21 = (bf16[4,64,256]{2,1,0:T(8,128)(2,1)S(1)}, bf16[4,64,256]{2,1,0:T(8,128)(2,1)}, u32[]{:S(2)}) copy-start(bf16[4,64,256]{2,1,0:T(8,128)(2,1)} %get-tuple-element.75) | copy-start | bytes 393220
  170.6 5.1 %copy-start.1 = (bf16[2,128,2048]{2,1,0:T(8,128)(2,1)S(1)}, bf16[2,128,2048]{2,1,0:T(8,128)(2,1)}, u32[]{:S(2)}) copy-start(bf16[2,128,2048]{2,1,0:T(8,128)(2,1)} %second_pass.1) | copy-start | bytes 3145732
  171.5 12.8 %all-to-all-start.3 = ((bf16[4,64,1024]{2,1,0:T(8,128)(2,1)}), bf16[4,64,1024]{2,1,0:T(8,128)(2,1)S(1)}, u32[]{:S(2)}, u32[]{:S(2)}) async-start(bf16[4,64,1024]{2,1,0:T(8,128)(2,1)} %pad_maximum_fusion.1), calls=%async_computation.3 | async-start | bytes 1048576 | tf_op jit(solution)/shard_map/all_to_all | solution.py:378
  175.8 9.5 %collective-permute-start.19 = (bf16[2,64,2048]{2,1,0:T(8,128)(2,1)S(1)}, bf16[2,64,2048]{2,1,0:T(8,128)(2,1)S(1)}, u32[]{:S(2)}, u32[]{:S(2)}) collective-permute-start(bf16[2,64,2048]{2,1,0:T(8,128)(2,1)S(1)} %constant_dynamic-slice_fusion), channel_id=1, source_target_pairs={{0,4},{4,0},{1,5},{5,1},{2,6},{6,2},{3,7},{7,3},{8,12},{12,8},{9,1... | collective-permute-start | bytes 1572872 | tf_op jit(solution)/shard_map/ppermute | solution.py:372
Sparse Core Ops, SparseCore 0:
  42.6 44.8 all-gather.1

commit v4 on v3

--- a/solution.py
+++ b/solution.py
@@ -132,9 +132,10 @@
 
 
 def attend_pass(info, own_ref, far_ref, kv_ref, own_out, far_out):
-    own = pl.program_id(0) < 2
+    own = pl.program_id(0) == 0
     z, core, live = jnp.where(own, info[0], info[1]), info[2], info[3]
-    qs = jnp.where(own, own_ref[...], far_ref[...]).reshape(256, HD)
+    both = jnp.where(own, own_ref[...], far_ref[...])
+    qs = jnp.concatenate([both[:, :, :HD].reshape(256, HD), both[:, :, HD:].reshape(256, HD)])
     factor = LOG2E / math.sqrt(HD)
 
     def block(zz, carry, masked):
@@ -143,8 +144,8 @@
         keys, values = kv[:, :HD], kv[:, HD:]
         scores = lax.dot_general(keys, qs, (((1,), (1,)), ((), ())), preferred_element_type=F32) * factor
         if masked:
-            kr = lax.broadcasted_iota(jnp.int32, (512, 256), 0)
-            qr = lax.broadcasted_iota(jnp.int32, (512, 256), 1)
+            kr = lax.broadcasted_iota(jnp.int32, (512, 512), 0)
+            qr = lax.broadcasted_iota(jnp.int32, (512, 512), 1) % 256
             kp = ((kr // 64) % 4) * 128 + (kr // 256) * 64 + kr % 64
             qp = (qr // 64) * 128 + core * 64 + qr % 64
             scores = jnp.where(kp <= qp, scores, neg_large)
@@ -157,39 +158,40 @@
         )
         return new_peak, divisor, acc * fade + update
 
-    start = (jnp.full((1, 256), neg_large, F32), jnp.zeros((1, 256), F32), jnp.zeros((HD, 256), F32))
+    start = (jnp.full((1, 512), neg_large, F32), jnp.zeros((1, 512), F32), jnp.zeros((HD, 512), F32))
     carry = lax.fori_loop(0, z, lambda zz, c: block(zz, c, False), start)
     _, divisor, acc = block(z, carry, True)
     result = jnp.transpose(acc / divisor)
-    r = lax.broadcasted_iota(jnp.int32, (256, HD), 0)
+    r = lax.broadcasted_iota(jnp.int32, (512, HD), 0) % 256
     pos = z * 512 + (r // 64) * 128 + core * 64 + r % 64
-    kept = jnp.where(pos < live, result, 0.0).astype(BF16).reshape(4, 64, HD)
+    kept = jnp.where(pos < live, result, 0.0).astype(BF16)
+    kept = [kept[i * 256 : (i + 1) * 256].reshape(4, 64, HD) for i in range(2)]
 
     @pl.when(own)
     def _():
-        own_out[...] = kept
+        own_out[:, :, :HD] = kept[0]
+        own_out[:, :, HD:] = kept[1]
 
     @pl.when(jnp.logical_not(own))
     def _():
-        far_out[...] = kept
+        far_out[:, :, :HD] = kept[0]
+        far_out[:, :, HD:] = kept[1]
 
 
 def attend(part, info, own, far, kv):
-    own_at = lambda i: jnp.minimum(i, 1)
-    far_at = lambda i: jnp.maximum(i - 2, 0)
-    block = lambda at, base: pl.BlockSpec((4, 64, HD), lambda i, o: (0, 0, base + at(i)))
+    block = lambda at: pl.BlockSpec((4, 64, 2 * HD), lambda i, o: (0, 0, at))
     shape = jax.ShapeDtypeStruct((4, 64, 256), BF16)
     return pl.pallas_call(
         attend_pass,
         grid_spec=pltpu.PrefetchScalarGridSpec(
             num_scalar_prefetch=1,
-            grid=(4,),
+            grid=(2,),
             in_specs=[
-                block(own_at, 2 * part),
-                block(far_at, 2 * part),
+                block(part),
+                block(part),
                 pl.BlockSpec((16, 256, 256), lambda i, o: (0, 0, 0)),
             ],
-            out_specs=[block(own_at, 0), block(far_at, 0)],
+            out_specs=[block(0), block(0)],
         ),
         out_shape=[shape, shape],
         name="attend_pass",
@@ -248,6 +250,7 @@
         for d in range(PIECES)
     )
     chips = nz * nx
+    last, gate_input = lax.optimization_barrier((last, gate_input))
     tail = lax.ppermute(last, ("z", "x"), [(i, i + 1) for i in range(chips - 1)])
     received = received.reshape(4, 64, 1280)
     kv_own = received[:, :, 1024:].reshape(1, 256, 256)
@@ -257,8 +260,6 @@
     ).astype(jnp.int32)
 
     mirror = [(i, nz - 1 - i) for i in range(nz)]
-    far, tail, gate_input = lax.optimization_barrier((received[:, :, 512:1024], tail, gate_input))
-    far = lax.ppermute(far, "z", mirror)
     gates = [turned(slice_for(gate_input, turn)[None], turn) for turn in turns[:4]]
 
     other = lax.ppermute(state_proj, "core", [(0, 1), (1, 0)])
@@ -267,6 +268,8 @@
     proj = jnp.concatenate([first, second], axis=1).astype(F32)
     inflow = jnp.broadcast_to(proj[:, :, :NST, None], (2, SPAN, NST, LANES)).reshape(2, SPAN * NST, LANES)
     readout = jnp.broadcast_to(proj[:, :, NST:, None], (2, SPAN, NST, LANES)).reshape(2, SPAN * NST, LANES)
+    far, tail, inflow = lax.optimization_barrier((received[:, :, 512:1024], tail, inflow))
+    far = lax.ppermute(far, "z", mirror)
     mine = lambda part, dim: lax.dynamic_slice_in_dim(part, core * half, half, dim)
     whole = lambda part, dim: lax.dynamic_slice_in_dim(part, head * quarter + core * half, half, dim)
     params = jnp.concatenate(

time: 194 us -> 185 us (0.954)
  Pallas kernels: 60.1 us -> 52.7 us
    pallas_call x2, Pallas kernels: 26.7 us -> 19.2 us  [attend(): pl.pallas_call(attend_pass, grid_spec=pltpu.PrefetchScalarGridSpec(num_sc...]
    ppermute x14, waiting for transfers between devices: 20.5 us -> 22.8 us  [turned(): return block if dc + dh == 0 else lax.ppermute(block, group, route)]
  transfers between devices with their start and end apart: 25 -> 25, of which waited for: 6 -> 6; matrix products, arithmetic and copies ran while one was open for 11% -> 10% of each run, Pallas kernels for 30% -> 28%
where the time goes in v4:
time: 185 us; the launch traced here: 184 us
  starting transfers between devices  57.5 us (31%)
  Pallas kernels  52.7 us (28%)
  waiting for transfers between devices  34.9 us (19%)
  local copies, waits for them, and re-layouts  15.4 us (8%)
  between operations  14.8 us (8%)
  other arithmetic  9.23 us (5%)
    ppermute x14, waiting for transfers between devices, turned(): return block if dc + dh == 0 else lax.ppermute(block, group, route)  22.8 us
    ppermute x14, starting transfers between devices, turned(): return block if dc + dh == 0 else lax.ppermute(block, group, route)  19.3 us
    pallas_call x2, Pallas kernels, attend(): pl.pallas_call(attend_pass, grid_spec=pltpu.PrefetchScalarGridSpec(num_sc...  19.2 us
    pallas_call x1, Pallas kernels, shards(): pl.pallas_call(second_pass, grid_spec=pltpu.PrefetchScalarGridSpec(num_sc...  15 us
    pallas_call x1, Pallas kernels, shards(): pl.pallas_call(first_pass, grid_spec=pltpu.PrefetchScalarGridSpec(num_sca...  14.8 us
    all_to_all x1, starting transfers between devices, shards(): entering = lax.all_to_all(prefix, ('z', 'x'), 0, 0, tiled=True)  9.78 us
    all_to_all x1, waiting for transfers between devices, shards(): home = lax.all_to_all(attended, 'x', 0, 0, tiled=True)  8.44 us
    ppermute x1, starting transfers between devices, shards(): far = lax.ppermute(far, 'z', mirror)  6.09 us
  transfers between devices with their start and end apart: 25, of which 6 were waited for; matrix products, arithmetic and copies ran while one was open for 10% of the time, Pallas kernels for 28%

profile of v4, /device:TPU:32, one launch (start us, length us, event | category | flops | bytes accessed | tf_op | source)
XLA Modules:
  0.0 184.4 jit_solution(1033403703081050124)
XLA Ops:
  7.3 1.8 dynamic-slice_bitcast_fusion.8
  9.1 0.1 collective-permute-start.3
  9.2 0.7 pad_maximum_fusion.6
  9.9 3.0 %collective-permute-start.2 = (bf16[2,2,16,2048]{3,2,1,0:T(8,128)(2,1)}, bf16[2,2,16,2048]{3,2,1,0:T(8,128)(2,1)S(1)}, u32[]{:S(2)}, u32[]{:S(2)}) collective-permute-start(bf16[2,2,16,2048]{3,2,1,0:T(8,128)(2,1)} %pad_maximum_fusion.6), channel_id=1, source_target_pairs={{0,3},{1,0},{2,1},{3,2},{4,7},{5,4},{6,5},{7,6},{8,11},{9,8},{10,9... | collective-permute-start | bytes 786440 | tf_op jit(solution)/shard_map/ppermute | solution.py:233
  12.9 2.0 %shard_map.140 = bf16[16,16,1280]{2,1,0:T(8,128)(2,1)} custom-call(bf16[2,16,8192]{2,1,0:T(8,128)(2,1)} %q.1, bf16[2,16,1024]{2,1,0:T(8,128)(2,1)} %k.1, bf16[2,16,1024]{2,1,0:T(8,128)(2,1)} %v.1), custom_call_target="tpu_custom_call" | custom-call | tf_op jit(solution)/shard_map/pallas_call | solution.py:240
  14.9 4.6 %all-to-all-start = ((bf16[16,16,1280]{2,1,0:T(8,128)(2,1)}), bf16[16,16,1280]{2,1,0:T(8,128)(2,1)S(1)}, u32[]{:S(2)}, u32[]{:S(2)}) async-start(bf16[16,16,1280]{2,1,0:T(8,128)(2,1)} %shard_map.140), calls=%async_computation | async-start | bytes 1310720 | tf_op jit(solution)/shard_map/all_to_all | solution.py:246
  19.6 3.5 %collective-permute-start.1 = (bf16[2,2,16,2048]{3,2,1,0:T(8,128)(2,1)S(1)}, bf16[2,2,16,2048]{3,2,1,0:T(8,128)(2,1)S(1)}, u32[]{:S(2)}, u32[]{:S(2)}) collective-permute-start(bf16[2,2,16,2048]{3,2,1,0:T(8,128)(2,1)S(1)} %pad_maximum_fusion.5), channel_id=1, source_target_pairs={{0,2},{1,3},{2,0},{3,1},{4,6},{5,7},{6,4},{7,5},{8,10},{9,11},{10,... | collective-permute-start | bytes 786440 | tf_op jit(solution)/shard_map/ppermute | solution.py:233
  23.1 0.6 collective-permute-start
  23.9 13.4 %collective-permute-done.1.refs_2_ = bf16[2,2,16,2048]{3,2,1,0:T(8,128)(2,1)S(1)} collective-permute-done((bf16[2,2,16,2048]{3,2,1,0:T(8,128)(2,1)S(1)}, bf16[2,2,16,2048]{3,2,1,0:T(8,128)(2,1)S(1)}, u32[]{:S(2)}, u32[]{:S(2)}) %collective-permute-start.1) | collective-permute-done | bytes 262176 | tf_op jit(solution)/shard_map/ppermute | solution.py:233
  37.3 4.4 %collective-permute-done.refs_1_ = bf16[2,2,16,2048]{3,2,1,0:T(8,128)(2,1)S(1)} collective-permute-done((bf16[2,2,16,2048]{3,2,1,0:T(8,128)(2,1)S(1)}, bf16[2,2,16,2048]{3,2,1,0:T(8,128)(2,1)S(1)}, u32[]{:S(2)}, u32[]{:S(2)}) %collective-permute-start) | collective-permute-done | bytes 262176 | tf_op jit(solution)/shard_map/ppermute | solution.py:233
  41.8 0.7 slice.69
  42.5 0.7 pad_maximum_fusion.9
  43.2 0.7 pad_maximum_fusion.10
  43.9 3.2 %collective-permute-start.6 = (bf16[2,2,16,2048]{3,2,1,0:T(8,128)(2,1)}, bf16[2,2,16,2048]{3,2,1,0:T(8,128)(2,1)}, u32[]{:S(2)}, u32[]{:S(2)}) collective-permute-start(bf16[2,2,16,2048]{3,2,1,0:T(8,128)(2,1)} %pad_maximum_fusion.10), channel_id=1, source_target_pairs={{0,7},{1,4},{2,5},{3,6},{4,3},{5,0},{6,1},{7,2},{8,15},{9,12},{10,... | collective-permute-start | bytes 786440 | tf_op jit(solution)/shard_map/ppermute | solution.py:233
  47.1 0.7 pad_maximum_fusion.8
  47.8 0.7 dynamic-slice_convert_fusion
  48.7 0.8 dynamic_slice.117
  49.5 0.7 dynamic_slice.118
  50.2 0.7 dynamic_slice.119
  50.9 0.6 copy.23
  51.6 1.3 dynamic_slice.125
  52.9 0.7 concatenate.19.refs_9_.refs_10_
  53.6 0.7 stack.133.order
  54.3 0.1 maximum_convert_fusion
  54.3 2.8 %collective-permute-done.6.refs_7_ = bf16[2,2,16,2048]{3,2,1,0:T(8,128)(2,1)} collective-permute-done((bf16[2,2,16,2048]{3,2,1,0:T(8,128)(2,1)}, bf16[2,2,16,2048]{3,2,1,0:T(8,128)(2,1)}, u32[]{:S(2)}, u32[]{:S(2)}) %collective-permute-start.6) | collective-permute-done | bytes 262176 | tf_op jit(solution)/shard_map/ppermute | solution.py:233
  57.1 2.1 %collective-permute-done.4.refs_5_ = bf16[2,2,16,2048]{3,2,1,0:T(8,128)(2,1)} collective-permute-done((bf16[2,2,16,2048]{3,2,1,0:T(8,128)(2,1)}, bf16[2,2,16,2048]{3,2,1,0:T(8,128)(2,1)}, u32[]{:S(2)}, u32[]{:S(2)}) %collective-permute-start.4) | collective-permute-done | bytes 262176 | tf_op jit(solution)/shard_map/ppermute | solution.py:233
  59.2 1.0 fusion.1
  60.3 3.4 %collective-permute-start.7 = (bf16[2,3,2048]{2,1,0:T(4,128)(2,1)S(1)}, bf16[2,3,2048]{2,1,0:T(4,128)(2,1)S(1)}, u32[]{:S(2)}, u32[]{:S(2)}) collective-permute-start(bf16[2,3,2048]{2,1,0:T(4,128)(2,1)S(1)} %fusion.1), channel_id=1, source_target_pairs={{0,8},{8,16},{16,24},{24,32},{32,40},{40,48},{48,56},{56,64},{64,7... | collective-permute-start | bytes 73736 | tf_op jit(solution)/shard_map/ppermute | solution.py:254
  63.7 0.1 copy.18
  63.8 0.1 broadcast_in_dim.64
  63.9 0.7 slice.64
  64.7 3.6 %collective-permute-done.7.refs_8_ = bf16[2,3,2048]{2,1,0:T(4,128)(2,1)S(1)} collective-permute-done((bf16[2,3,2048]{2,1,0:T(4,128)(2,1)S(1)}, bf16[2,3,2048]{2,1,0:T(4,128)(2,1)S(1)}, u32[]{:S(2)}, u32[]{:S(2)}) %collective-permute-start.7) | collective-permute-done | bytes 24608 | tf_op jit(solution)/shard_map/ppermute | solution.py:254
  68.3 2.0 %broadcast_in_dim.65.refs_11_.refs_12_ = f32[2,2048,128]{2,1,0:T(8,128)} broadcast(f32[2,2048]{1,0:T(2,128)S(1)} %broadcast_in_dim.64), dimensions={0,1} | broadcast | bytes 2113536 | tf_op jit(solution)/shard_map/broadcast_in_dim | solution.py:269
  70.3 6.1 %collective-permute-start.9 = (bf16[4,64,512]{2,1,0:T(8,128)(2,1)}, bf16[4,64,512]{2,1,0:T(8,128)(2,1)S(1)}, u32[]{:S(2)}, u32[]{:S(2)}) collective-permute-start(bf16[4,64,512]{2,1,0:T(8,128)(2,1)} %slice.64), channel_id=1, source_target_pairs={{0,224},{32,192},{64,160},{96,128},{128,96},{160,64},{192,32},{224... | collective-permute-start | bytes 786440 | tf_op jit(solution)/shard_map/ppermute | solution.py:272
  76.4 0.7 dynamic-slice_bitcast_fusion.4
  77.1 0.2 collective-permute-start.10
  77.3 1.5 collective-permute-start.11
  78.7 2.1 %collective-permute-start.12 = (bf16[1,2,16,2048]{3,2,1,0:T(8,128)(2,1)S(1)}, bf16[1,2,16,2048]{3,2,1,0:T(8,128)(2,1)S(1)}, u32[]{:S(2)}, u32[]{:S(2)}) collective-permute-start(bf16[1,2,16,2048]{3,2,1,0:T(8,128)(2,1)S(1)} %get-tuple-element.88), channel_id=1, source_target_pairs={{0,3},{1,0},{2,1},{3,2},{4,7},{5,4},{6,5},{7,6},{8,11},{9,8},{10,9... | collective-permute-start | bytes 393224 | tf_op jit(solution)/shard_map/ppermute | solution.py:233
  80.9 14.8 %first_pass.1 = (f32[2,2,1024,128]{3,2,1,0:T(8,128)}, f32[2,2,1024,128]{3,2,1,0:T(8,128)}, bf16[32,24,128]{2,1,0:T(8,128)(2,1)}) custom-call(s32[9]{0:T(128)} %stack.133.order, bf16[2,2,16,2048]{3,2,1,0:T(8,128)(2,1)} %copy-done.2, bf16[2,2,16,2048]{3,2,1,0:T(8,128)(2,1)} %copy-done.10, bf16[2,2,16,2048]{3,2,1,0:T(8,128)(2,1)} %copy-done.9, ...), custom_call_target="tpu_custom_call" | custom-call | tf_op jit(solution)/shard_map/first_pass/pallas_call | solution.py:295
  95.9 4.8 %all-to-all-start.1 = ((bf16[32,24,128]{2,1,0:T(8,128)(2,1)}), bf16[32,24,128]{2,1,0:T(8,128)(2,1)S(1)}, u32[]{:S(2)}, u32[]{:S(2)}) async-start(bf16[32,24,128]{2,1,0:T(8,128)(2,1)} %get-tuple-element.58), calls=%async_computation.1 | async-start | bytes 393216 | tf_op jit(solution)/shard_map/all_to_all | solution.py:324
  100.7 0.3 collective-permute-start.13
  101.0 0.4 collective-permute-start.14
  101.4 2.0 %collective-permute-start.15 = (bf16[1,2,16,2048]{3,2,1,0:T(8,128)(2,1)S(1)}, bf16[1,2,16,2048]{3,2,1,0:T(8,128)(2,1)S(1)}, u32[]{:S(2)}, u32[]{:S(2)}) collective-permute-start(bf16[1,2,16,2048]{3,2,1,0:T(8,128)(2,1)S(1)} %get-tuple-element.85), channel_id=1, source_target_pairs={{0,6},{1,7},{2,4},{3,5},{4,2},{5,3},{6,0},{7,1},{8,14},{9,15},{10,... | collective-permute-start | bytes 393224 | tf_op jit(solution)/shard_map/ppermute | solution.py:233
  103.4 2.4 %collective-permute-start.16 = (bf16[1,2,16,2048]{3,2,1,0:T(8,128)(2,1)S(1)}, bf16[1,2,16,2048]{3,2,1,0:T(8,128)(2,1)S(1)}, u32[]{:S(2)}, u32[]{:S(2)}) collective-permute-start(bf16[1,2,16,2048]{3,2,1,0:T(8,128)(2,1)S(1)} %get-tuple-element.84), channel_id=1, source_target_pairs={{0,7},{1,4},{2,5},{3,6},{4,3},{5,0},{6,1},{7,2},{8,15},{9,12},{10,... | collective-permute-start | bytes 393224 | tf_op jit(solution)/shard_map/ppermute | solution.py:233
  105.8 1.3 pad_add_fusion.info
  107.1 0.6 constant_dynamic-slice_fusion.1.rate
  107.7 9.6 %attend_pass.2 = (bf16[4,64,256]{2,1,0:T(8,128)(2,1)}, bf16[4,64,256]{2,1,0:T(8,128)(2,1)}) custom-call(s32[4]{0:T(128)} %pad_add_fusion.info, bf16[4,64,1280]{2,1,0:T(8,128)(2,1)} %bitcast.88, bf16[4,64,512]{2,1,0:T(8,128)(2,1)} %copy-done.3, bf16[16,256,256]{2,1,0:T(8,128)(2,1)} %all-gather.2.cloned.1.call-done.kv_ref), custom_call_target="tpu_custom_call" | custom-call | tf_op jit(solution)/shard_map/attend_pass/pallas_call | solution.py:184
  117.4 0.8 copy-done.5
  118.2 1.7 prefix_pass.1
  119.8 9.8 %all-to-all-start.2 = ((bf16[32,16,128]{2,1,0:T(8,128)(2,1)}), bf16[32,16,128]{2,1,0:T(8,128)(2,1)S(1)}, u32[]{:S(2)}, u32[]{:S(2)}) async-start(bf16[32,16,128]{2,1,0:T(8,128)(2,1)} %prefix_pass.1), calls=%async_computation.2 | async-start | bytes 262144 | tf_op jit(solution)/shard_map/all_to_all | solution.py:339
  129.6 3.7 %collective-permute-start.17 = (bf16[4,64,256]{2,1,0:T(8,128)(2,1)}, bf16[4,64,256]{2,1,0:T(8,128)(2,1)S(1)}, u32[]{:S(2)}, u32[]{:S(2)}) collective-permute-start(bf16[4,64,256]{2,1,0:T(8,128)(2,1)} %get-tuple-element.74), channel_id=1, source_target_pairs={{0,224},{32,192},{64,160},{96,128},{128,96},{160,64},{192,32},{224... | collective-permute-start | bytes 393224 | tf_op jit(solution)/shard_map/ppermute | solution.py:328
  133.3 9.6 %attend_pass.3 = (bf16[4,64,256]{2,1,0:T(8,128)(2,1)}, bf16[4,64,256]{2,1,0:T(8,128)(2,1)}) custom-call(s32[4]{0:T(128)} %pad_add_fusion.info, bf16[4,64,1280]{2,1,0:T(8,128)(2,1)} %bitcast.89, bf16[4,64,512]{2,1,0:T(8,128)(2,1)} %copy-done.3, bf16[16,256,256]{2,1,0:T(8,128)(2,1)} %all-gather.2.cloned.1.call-done.kv_ref), custom_call_target="tpu_custom_call" | custom-call | tf_op jit(solution)/shard_map/attend_pass/pallas_call | solution.py:184
  143.0 1.5 collective-permute-start.18
  144.5 0.1 copy.20
  144.6 0.1 broadcast_in_dim.78
  144.7 1.9 %broadcast_in_dim.79.refs_13_ = f32[2,2048,128]{2,1,0:T(8,128)} broadcast(f32[2,2048]{1,0:T(2,128)S(1)} %broadcast_in_dim.78), dimensions={0,1} | broadcast | bytes 2113536 | tf_op jit(solution)/shard_map/broadcast_in_dim | solution.py:270
  146.7 15.0 %second_pass.1 = bf16[2,128,2048]{2,1,0:T(8,128)(2,1)} custom-call(s32[9]{0:T(128)} %stack.133.order, bf16[1,2,16,2048]{3,2,1,0:T(8,128)(2,1)} %get-tuple-element.54.refs_0_, bf16[1,2,16,2048]{3,2,1,0:T(8,128)(2,1)} %copy-done.14, bf16[1,2,16,2048]{3,2,1,0:T(8,128)(2,1)} %copy-done.15, bf16[1,2,16,2048]{3,2,1,0:T(8,128)(2,1)} %copy-done.16, ...), custom_call_target="tpu_custom_call" | custom-call | tf_op jit(solution)/shard_map/second_pass/pallas_call | solution.py:344
  161.7 0.9 pad_maximum_fusion.1
  162.6 4.2 %all-to-all-start.3 = ((bf16[4,64,1024]{2,1,0:T(8,128)(2,1)}), bf16[4,64,1024]{2,1,0:T(8,128)(2,1)S(1)}, u32[]{:S(2)}, u32[]{:S(2)}) async-start(bf16[4,64,1024]{2,1,0:T(8,128)(2,1)} %pad_maximum_fusion.1), calls=%async_computation.3 | async-start | bytes 1048576 | tf_op jit(solution)/shard_map/all_to_all | solution.py:381
  166.8 0.1 collective-permute-start.19
  166.9 8.4 %all-to-all-done.3 = bf16[4,64,1024]{2,1,0:T(8,128)(2,1)S(1)} async-done(((bf16[4,64,1024]{2,1,0:T(8,128)(2,1)}), bf16[4,64,1024]{2,1,0:T(8,128)(2,1)S(1)}, u32[]{:S(2)}, u32[]{:S(2)}) %all-to-all-start.3) | async-done | bytes 524320 | tf_op jit(solution)/shard_map/all_to_all | solution.py:381
  175.5 0.8 pad_maximum_fusion.2
  176.3 0.2 broadcast_select_fusion.1
  176.6 1.0 pad_maximum_fusion
  (88 shorter events, 0.6 us)
Async XLA Ops:
  9.1 14.8 %collective-permute-start.3 = (bf16[2,2,16,2048]{3,2,1,0:T(8,128)(2,1)S(1)}, bf16[2,2,16,2048]{3,2,1,0:T(8,128)(2,1)S(1)}, u32[]{:S(2)}, u32[]{:S(2)}) collective-permute-start(bf16[2,2,16,2048]{3,2,1,0:T(8,128)(2,1)S(1)} %pad_maximum_fusion.7), channel_id=1, source_target_pairs={{0,4},{1,5},{2,6},{3,7},{4,0},{5,1},{6,2},{7,3},{8,12},{9,13},{10,... | collective-permute-start | bytes 786440 | tf_op jit(solution)/shard_map/ppermute | solution.py:233
  9.9 13.9 %collective-permute-start.2 = (bf16[2,2,16,2048]{3,2,1,0:T(8,128)(2,1)}, bf16[2,2,16,2048]{3,2,1,0:T(8,128)(2,1)S(1)}, u32[]{:S(2)}, u32[]{:S(2)}) collective-permute-start(bf16[2,2,16,2048]{3,2,1,0:T(8,128)(2,1)} %pad_maximum_fusion.6), channel_id=1, source_target_pairs={{0,3},{1,0},{2,1},{3,2},{4,7},{5,4},{6,5},{7,6},{8,11},{9,8},{10,9... | collective-permute-start | bytes 786440 | tf_op jit(solution)/shard_map/ppermute | solution.py:233
  14.9 26.9 %all-to-all-start = ((bf16[16,16,1280]{2,1,0:T(8,128)(2,1)}), bf16[16,16,1280]{2,1,0:T(8,128)(2,1)S(1)}, u32[]{:S(2)}, u32[]{:S(2)}) async-start(bf16[16,16,1280]{2,1,0:T(8,128)(2,1)} %shard_map.140), calls=%async_computation | async-start | bytes 1310720 | tf_op jit(solution)/shard_map/all_to_all | solution.py:246
  19.5 28.3 %copy-start.24 = (bf16[2,64,32]{1,2,0:T(8,128)(2,1)S(1)}, bf16[2,64,32]{1,2,0:T(8,128)(2,1)}, u32[]{:S(2)}) copy-start(bf16[2,64,32]{1,2,0:T(8,128)(2,1)} %param.16) | copy-start | bytes 24580
  19.5 29.1 %copy-start.12 = (f32[16,4096]{1,0:T(8,128)S(1)}, f32[16,4096]{1,0:T(8,128)}, u32[]{:S(2)}) copy-start(f32[16,4096]{1,0:T(8,128)} %param.20) | copy-start | bytes 786436
  19.5 88.2 %all-gather.2.cloned.1.call-start = ((), (), s32[]{:S(2)}) async-start(), calls=%async_computation.4 | async-start | bytes 2228224 | tf_op jit(solution)/shard_map/all_gather | solution.py:257
  19.6 17.7 %collective-permute-start.1 = (bf16[2,2,16,2048]{3,2,1,0:T(8,128)(2,1)S(1)}, bf16[2,2,16,2048]{3,2,1,0:T(8,128)(2,1)S(1)}, u32[]{:S(2)}, u32[]{:S(2)}) collective-permute-start(bf16[2,2,16,2048]{3,2,1,0:T(8,128)(2,1)S(1)} %pad_maximum_fusion.5), channel_id=1, source_target_pairs={{0,2},{1,3},{2,0},{3,1},{4,6},{5,7},{6,4},{7,5},{8,10},{9,11},{10,... | collective-permute-start | bytes 786440 | tf_op jit(solution)/shard_map/ppermute | solution.py:233
  23.1 18.6 %collective-permute-start = (bf16[2,2,16,2048]{3,2,1,0:T(8,128)(2,1)S(1)}, bf16[2,2,16,2048]{3,2,1,0:T(8,128)(2,1)S(1)}, u32[]{:S(2)}, u32[]{:S(2)}) collective-permute-start(bf16[2,2,16,2048]{3,2,1,0:T(8,128)(2,1)S(1)} %pad_maximum_fusion.4), channel_id=1, source_target_pairs={{0,1},{1,2},{2,3},{3,0},{4,5},{5,6},{6,7},{7,4},{8,9},{9,10},{10,1... | collective-permute-start | bytes 786440 | tf_op jit(solution)/shard_map/ppermute | solution.py:233
  23.8 40.8 %copy-start.2 = (bf16[2,2,16,2048]{3,2,1,0:T(8,128)(2,1)}, bf16[2,2,16,2048]{3,2,1,0:T(8,128)(2,1)S(1)}, u32[]{:S(2)}) copy-start(bf16[2,2,16,2048]{3,2,1,0:T(8,128)(2,1)S(1)} %pad_maximum_fusion.3.refs_0_) | copy-start | bytes 786436
  23.8 40.8 %copy-start.7 = (bf16[2,2,16,2048]{3,2,1,0:T(8,128)(2,1)}, bf16[2,2,16,2048]{3,2,1,0:T(8,128)(2,1)S(1)}, u32[]{:S(2)}) copy-start(bf16[2,2,16,2048]{3,2,1,0:T(8,128)(2,1)S(1)} %collective-permute-done.3.refs_4_) | copy-start | bytes 786436
  23.8 40.8 %copy-start.8 = (bf16[2,2,16,2048]{3,2,1,0:T(8,128)(2,1)}, bf16[2,2,16,2048]{3,2,1,0:T(8,128)(2,1)S(1)}, u32[]{:S(2)}) copy-start(bf16[2,2,16,2048]{3,2,1,0:T(8,128)(2,1)S(1)} %collective-permute-done.2.refs_3_) | copy-start | bytes 786436
  37.3 27.4 %copy-start.9 = (bf16[2,2,16,2048]{3,2,1,0:T(8,128)(2,1)}, bf16[2,2,16,2048]{3,2,1,0:T(8,128)(2,1)S(1)}, u32[]{:S(2)}) copy-start(bf16[2,2,16,2048]{3,2,1,0:T(8,128)(2,1)S(1)} %collective-permute-done.1.refs_2_) | copy-start | bytes 786436
  41.7 22.9 %copy-start.10 = (bf16[2,2,16,2048]{3,2,1,0:T(8,128)(2,1)}, bf16[2,2,16,2048]{3,2,1,0:T(8,128)(2,1)S(1)}, u32[]{:S(2)}) copy-start(bf16[2,2,16,2048]{3,2,1,0:T(8,128)(2,1)S(1)} %collective-permute-done.refs_1_) | copy-start | bytes 786436
  41.7 22.9 %copy-start = (bf16[16,16,1280]{2,1,0:T(8,128)(2,1)}, bf16[16,16,1280]{2,1,0:T(8,128)(2,1)S(1)}, u32[]{:S(2)}) copy-start(bf16[16,16,1280]{2,1,0:T(8,128)(2,1)S(1)} %all-to-all-done) | copy-start | bytes 1966084
  43.2 11.1 %collective-permute-start.5 = (bf16[2,2,16,2048]{3,2,1,0:T(8,128)(2,1)}, bf16[2,2,16,2048]{3,2,1,0:T(8,128)(2,1)S(1)}, u32[]{:S(2)}, u32[]{:S(2)}) collective-permute-start(bf16[2,2,16,2048]{3,2,1,0:T(8,128)(2,1)} %pad_maximum_fusion.9), channel_id=1, source_target_pairs={{0,6},{1,7},{2,4},{3,5},{4,2},{5,3},{6,0},{7,1},{8,14},{9,15},{10,... | collective-permute-start | bytes 786440 | tf_op jit(solution)/shard_map/ppermute | solution.py:233
  43.9 13.2 %collective-permute-start.6 = (bf16[2,2,16,2048]{3,2,1,0:T(8,128)(2,1)}, bf16[2,2,16,2048]{3,2,1,0:T(8,128)(2,1)}, u32[]{:S(2)}, u32[]{:S(2)}) collective-permute-start(bf16[2,2,16,2048]{3,2,1,0:T(8,128)(2,1)} %pad_maximum_fusion.10), channel_id=1, source_target_pairs={{0,7},{1,4},{2,5},{3,6},{4,3},{5,0},{6,1},{7,2},{8,15},{9,12},{10,... | collective-permute-start | bytes 786440 | tf_op jit(solution)/shard_map/ppermute | solution.py:233
  47.8 11.4 %collective-permute-start.4 = (bf16[2,2,16,2048]{3,2,1,0:T(8,128)(2,1)}, bf16[2,2,16,2048]{3,2,1,0:T(8,128)(2,1)}, u32[]{:S(2)}, u32[]{:S(2)}) collective-permute-start(bf16[2,2,16,2048]{3,2,1,0:T(8,128)(2,1)} %pad_maximum_fusion.8), channel_id=1, source_target_pairs={{0,5},{1,6},{2,7},{3,4},{4,1},{5,2},{6,3},{7,0},{8,13},{9,14},{10,... | collective-permute-start | bytes 786440 | tf_op jit(solution)/shard_map/ppermute | solution.py:233
  47.8 6.4 %collective-permute-start.8 = (bf16[2,64,32]{1,2,0:T(8,128)(2,1)S(1)}, bf16[2,64,32]{1,2,0:T(8,128)(2,1)S(1)}, u32[]{:S(2)}, u32[]{:S(2)}) collective-permute-start(bf16[2,64,32]{1,2,0:T(8,128)(2,1)S(1)} %copy-done.24), channel_id=1, source_target_pairs={{0,4},{4,0},{1,5},{5,1},{2,6},{6,2},{3,7},{7,3},{8,12},{12,8},{9,1... | collective-permute-start | bytes 24584 | tf_op jit(solution)/shard_map/ppermute | solution.py:265
  48.7 27.7 %copy-start.4 = (bf16[2,16,16384]{2,1,0:T(8,128)(2,1)S(1)}, bf16[2,16,16384]{2,1,0:T(8,128)(2,1)}, u32[]{:S(2)}) copy-start(bf16[2,16,16384]{2,1,0:T(8,128)(2,1)} %param.14) | copy-start | bytes 3145732
  54.3 22.7 %copy-start.11 = (bf16[2,2,16,2048]{3,2,1,0:T(8,128)(2,1)}, bf16[2,2,16,2048]{3,2,1,0:T(8,128)(2,1)S(1)}, u32[]{:S(2)}) copy-start(bf16[2,2,16,2048]{3,2,1,0:T(8,128)(2,1)S(1)} %collective-permute-done.5.refs_6_) | copy-start | bytes 786436
  60.3 8.0 %collective-permute-start.7 = (bf16[2,3,2048]{2,1,0:T(4,128)(2,1)S(1)}, bf16[2,3,2048]{2,1,0:T(4,128)(2,1)S(1)}, u32[]{:S(2)}, u32[]{:S(2)}) collective-permute-start(bf16[2,3,2048]{2,1,0:T(4,128)(2,1)S(1)} %fusion.1), channel_id=1, source_target_pairs={{0,8},{8,16},{16,24},{24,32},{32,40},{40,48},{48,56},{56,64},{64,7... | collective-permute-start | bytes 73736 | tf_op jit(solution)/shard_map/ppermute | solution.py:254
  63.9 17.0 %copy-start.13 = (f32[16,4096]{1,0:T(8,128)S(1)}, f32[16,4096]{1,0:T(8,128)}, u32[]{:S(2)}) copy-start(f32[16,4096]{1,0:T(8,128)} %param.20) | copy-start | bytes 786436
  68.3 12.6 %copy-start.23 = (bf16[2,3,2048]{2,1,0:T(4,128)(2,1)}, bf16[2,3,2048]{2,1,0:T(4,128)(2,1)S(1)}, u32[]{:S(2)}) copy-start(bf16[2,3,2048]{2,1,0:T(4,128)(2,1)S(1)} %collective-permute-done.7.refs_8_) | copy-start | bytes 73732
  70.3 25.6 %collective-permute-start.9 = (bf16[4,64,512]{2,1,0:T(8,128)(2,1)}, bf16[4,64,512]{2,1,0:T(8,128)(2,1)S(1)}, u32[]{:S(2)}, u32[]{:S(2)}) collective-permute-start(bf16[4,64,512]{2,1,0:T(8,128)(2,1)} %slice.64), channel_id=1, source_target_pairs={{0,224},{32,192},{64,160},{96,128},{128,96},{160,64},{192,32},{224... | collective-permute-start | bytes 786440 | tf_op jit(solution)/shard_map/ppermute | solution.py:272
  77.1 18.7 %collective-permute-start.10 = (bf16[1,2,16,2048]{3,2,1,0:T(8,128)(2,1)S(1)}, bf16[1,2,16,2048]{3,2,1,0:T(8,128)(2,1)S(1)}, u32[]{:S(2)}, u32[]{:S(2)}) collective-permute-start(bf16[1,2,16,2048]{3,2,1,0:T(8,128)(2,1)S(1)} %get-tuple-element.90), channel_id=1, source_target_pairs={{0,1},{1,2},{2,3},{3,0},{4,5},{5,6},{6,7},{7,4},{8,9},{9,10},{10,1... | collective-permute-start | bytes 393224 | tf_op jit(solution)/shard_map/ppermute | solution.py:233
  77.3 18.5 %collective-permute-start.11 = (bf16[1,2,16,2048]{3,2,1,0:T(8,128)(2,1)S(1)}, bf16[1,2,16,2048]{3,2,1,0:T(8,128)(2,1)S(1)}, u32[]{:S(2)}, u32[]{:S(2)}) collective-permute-start(bf16[1,2,16,2048]{3,2,1,0:T(8,128)(2,1)S(1)} %get-tuple-element.89), channel_id=1, source_target_pairs={{0,2},{1,3},{2,0},{3,1},{4,6},{5,7},{6,4},{7,5},{8,10},{9,11},{10,... | collective-permute-start | bytes 393224 | tf_op jit(solution)/shard_map/ppermute | solution.py:233
  78.7 17.1 %collective-permute-start.12 = (bf16[1,2,16,2048]{3,2,1,0:T(8,128)(2,1)S(1)}, bf16[1,2,16,2048]{3,2,1,0:T(8,128)(2,1)S(1)}, u32[]{:S(2)}, u32[]{:S(2)}) collective-permute-start(bf16[1,2,16,2048]{3,2,1,0:T(8,128)(2,1)S(1)} %get-tuple-element.88), channel_id=1, source_target_pairs={{0,3},{1,0},{2,1},{3,2},{4,7},{5,4},{6,5},{7,6},{8,11},{9,8},{10,9... | collective-permute-start | bytes 393224 | tf_op jit(solution)/shard_map/ppermute | solution.py:233
  95.8 21.5 %copy-start.14 = (bf16[1,2,16,2048]{3,2,1,0:T(8,128)(2,1)}, bf16[1,2,16,2048]{3,2,1,0:T(8,128)(2,1)S(1)}, u32[]{:S(2)}) copy-start(bf16[1,2,16,2048]{3,2,1,0:T(8,128)(2,1)S(1)} %collective-permute-done.10.refs_1_) | copy-start | bytes 393220
  95.8 21.5 %copy-start.15 = (bf16[1,2,16,2048]{3,2,1,0:T(8,128)(2,1)}, bf16[1,2,16,2048]{3,2,1,0:T(8,128)(2,1)S(1)}, u32[]{:S(2)}) copy-start(bf16[1,2,16,2048]{3,2,1,0:T(8,128)(2,1)S(1)} %collective-permute-done.11.refs_2_) | copy-start | bytes 393220
  95.8 21.5 %copy-start.16 = (bf16[1,2,16,2048]{3,2,1,0:T(8,128)(2,1)}, bf16[1,2,16,2048]{3,2,1,0:T(8,128)(2,1)S(1)}, u32[]{:S(2)}) copy-start(bf16[1,2,16,2048]{3,2,1,0:T(8,128)(2,1)S(1)} %collective-permute-done.12.refs_3_) | copy-start | bytes 393220
  95.8 11.8 %copy-start.3 = (bf16[4,64,512]{2,1,0:T(8,128)(2,1)}, bf16[4,64,512]{2,1,0:T(8,128)(2,1)S(1)}, u32[]{:S(2)}) copy-start(bf16[4,64,512]{2,1,0:T(8,128)(2,1)S(1)} %collective-permute-done.9.far_ref) | copy-start | bytes 786436
  95.9 21.6 %all-to-all-start.1 = ((bf16[32,24,128]{2,1,0:T(8,128)(2,1)}), bf16[32,24,128]{2,1,0:T(8,128)(2,1)S(1)}, u32[]{:S(2)}, u32[]{:S(2)}) async-start(bf16[32,24,128]{2,1,0:T(8,128)(2,1)} %get-tuple-element.58), calls=%async_computation.1 | async-start | bytes 393216 | tf_op jit(solution)/shard_map/all_to_all | solution.py:324
  100.7 16.6 %collective-permute-start.13 = (bf16[1,2,16,2048]{3,2,1,0:T(8,128)(2,1)S(1)}, bf16[1,2,16,2048]{3,2,1,0:T(8,128)(2,1)S(1)}, u32[]{:S(2)}, u32[]{:S(2)}) collective-permute-start(bf16[1,2,16,2048]{3,2,1,0:T(8,128)(2,1)S(1)} %get-tuple-element.87), channel_id=1, source_target_pairs={{0,4},{1,5},{2,6},{3,7},{4,0},{5,1},{6,2},{7,3},{8,12},{9,13},{10,... | collective-permute-start | bytes 393224 | tf_op jit(solution)/shard_map/ppermute | solution.py:233
  101.0 16.4 %collective-permute-start.14 = (bf16[1,2,16,2048]{3,2,1,0:T(8,128)(2,1)S(1)}, bf16[1,2,16,2048]{3,2,1,0:T(8,128)(2,1)S(1)}, u32[]{:S(2)}, u32[]{:S(2)}) collective-permute-start(bf16[1,2,16,2048]{3,2,1,0:T(8,128)(2,1)S(1)} %get-tuple-element.86), channel_id=1, source_target_pairs={{0,5},{1,6},{2,7},{3,4},{4,1},{5,2},{6,3},{7,0},{8,13},{9,14},{10,... | collective-permute-start | bytes 393224 | tf_op jit(solution)/shard_map/ppermute | solution.py:233
  101.4 16.0 %collective-permute-start.15 = (bf16[1,2,16,2048]{3,2,1,0:T(8,128)(2,1)S(1)}, bf16[1,2,16,2048]{3,2,1,0:T(8,128)(2,1)S(1)}, u32[]{:S(2)}, u32[]{:S(2)}) collective-permute-start(bf16[1,2,16,2048]{3,2,1,0:T(8,128)(2,1)S(1)} %get-tuple-element.85), channel_id=1, source_target_pairs={{0,6},{1,7},{2,4},{3,5},{4,2},{5,3},{6,0},{7,1},{8,14},{9,15},{10,... | collective-permute-start | bytes 393224 | tf_op jit(solution)/shard_map/ppermute | solution.py:233
  103.4 14.0 %collective-permute-start.16 = (bf16[1,2,16,2048]{3,2,1,0:T(8,128)(2,1)S(1)}, bf16[1,2,16,2048]{3,2,1,0:T(8,128)(2,1)S(1)}, u32[]{:S(2)}, u32[]{:S(2)}) collective-permute-start(bf16[1,2,16,2048]{3,2,1,0:T(8,128)(2,1)S(1)} %get-tuple-element.84), channel_id=1, source_target_pairs={{0,7},{1,4},{2,5},{3,6},{4,3},{5,0},{6,1},{7,2},{8,15},{9,12},{10,... | collective-permute-start | bytes 393224 | tf_op jit(solution)/shard_map/ppermute | solution.py:233
  117.3 29.3 %copy-start.17 = (bf16[1,2,16,2048]{3,2,1,0:T(8,128)(2,1)}, bf16[1,2,16,2048]{3,2,1,0:T(8,128)(2,1)S(1)}, u32[]{:S(2)}) copy-start(bf16[1,2,16,2048]{3,2,1,0:T(8,128)(2,1)S(1)} %collective-permute-done.13.refs_4_) | copy-start | bytes 393220
  117.3 29.3 %copy-start.18 = (bf16[1,2,16,2048]{3,2,1,0:T(8,128)(2,1)}, bf16[1,2,16,2048]{3,2,1,0:T(8,128)(2,1)S(1)}, u32[]{:S(2)}) copy-start(bf16[1,2,16,2048]{3,2,1,0:T(8,128)(2,1)S(1)} %collective-permute-done.14.refs_5_) | copy-start | bytes 393220
  117.4 29.3 %copy-start.19 = (bf16[1,2,16,2048]{3,2,1,0:T(8,128)(2,1)}, bf16[1,2,16,2048]{3,2,1,0:T(8,128)(2,1)S(1)}, u32[]{:S(2)}) copy-start(bf16[1,2,16,2048]{3,2,1,0:T(8,128)(2,1)S(1)} %collective-permute-done.15.refs_6_) | copy-start | bytes 393220
  117.4 29.3 %copy-start.20 = (bf16[1,2,16,2048]{3,2,1,0:T(8,128)(2,1)}, bf16[1,2,16,2048]{3,2,1,0:T(8,128)(2,1)S(1)}, u32[]{:S(2)}) copy-start(bf16[1,2,16,2048]{3,2,1,0:T(8,128)(2,1)S(1)} %collective-permute-done.16.refs_7_) | copy-start | bytes 393220
  117.4 0.8 copy-start.5
  119.8 23.1 %all-to-all-start.2 = ((bf16[32,16,128]{2,1,0:T(8,128)(2,1)}), bf16[32,16,128]{2,1,0:T(8,128)(2,1)S(1)}, u32[]{:S(2)}, u32[]{:S(2)}) async-start(bf16[32,16,128]{2,1,0:T(8,128)(2,1)} %prefix_pass.1), calls=%async_computation.2 | async-start | bytes 262144 | tf_op jit(solution)/shard_map/all_to_all | solution.py:339
  129.6 13.3 %collective-permute-start.17 = (bf16[4,64,256]{2,1,0:T(8,128)(2,1)}, bf16[4,64,256]{2,1,0:T(8,128)(2,1)S(1)}, u32[]{:S(2)}, u32[]{:S(2)}) collective-permute-start(bf16[4,64,256]{2,1,0:T(8,128)(2,1)} %get-tuple-element.74), channel_id=1, source_target_pairs={{0,224},{32,192},{64,160},{96,128},{128,96},{160,64},{192,32},{224... | collective-permute-start | bytes 393224 | tf_op jit(solution)/shard_map/ppermute | solution.py:328
  143.0 3.7 %copy-start.6 = (bf16[32,16,128]{2,1,0:T(8,128)(2,1)}, bf16[32,16,128]{2,1,0:T(8,128)(2,1)S(1)}, u32[]{:S(2)}) copy-start(bf16[32,16,128]{2,1,0:T(8,128)(2,1)S(1)} %all-to-all-done.2.refs_14_) | copy-start | bytes 393220
  143.0 18.7 %collective-permute-start.18 = (bf16[4,64,256]{2,1,0:T(8,128)(2,1)}, bf16[4,64,256]{2,1,0:T(8,128)(2,1)S(1)}, u32[]{:S(2)}, u32[]{:S(2)}) collective-permute-start(bf16[4,64,256]{2,1,0:T(8,128)(2,1)} %get-tuple-element.76), channel_id=1, source_target_pairs={{0,224},{32,192},{64,160},{96,128},{128,96},{160,64},{192,32},{224... | collective-permute-start | bytes 393224 | tf_op jit(solution)/shard_map/ppermute | solution.py:342
  146.7 15.0 %copy-start.21 = (bf16[4,64,256]{2,1,0:T(8,128)(2,1)S(1)}, bf16[4,64,256]{2,1,0:T(8,128)(2,1)}, u32[]{:S(2)}) copy-start(bf16[4,64,256]{2,1,0:T(8,128)(2,1)} %get-tuple-element.78) | copy-start | bytes 393220
  146.7 15.0 %copy-start.22 = (bf16[4,64,256]{2,1,0:T(8,128)(2,1)S(1)}, bf16[4,64,256]{2,1,0:T(8,128)(2,1)}, u32[]{:S(2)}) copy-start(bf16[4,64,256]{2,1,0:T(8,128)(2,1)} %get-tuple-element.79) | copy-start | bytes 393220
  161.7 5.1 %copy-start.1 = (bf16[2,128,2048]{2,1,0:T(8,128)(2,1)S(1)}, bf16[2,128,2048]{2,1,0:T(8,128)(2,1)}, u32[]{:S(2)}) copy-start(bf16[2,128,2048]{2,1,0:T(8,128)(2,1)} %second_pass.1) | copy-start | bytes 3145732
  162.6 12.8 %all-to-all-start.3 = ((bf16[4,64,1024]{2,1,0:T(8,128)(2,1)}), bf16[4,64,1024]{2,1,0:T(8,128)(2,1)S(1)}, u32[]{:S(2)}, u32[]{:S(2)}) async-start(bf16[4,64,1024]{2,1,0:T(8,128)(2,1)} %pad_maximum_fusion.1), calls=%async_computation.3 | async-start | bytes 1048576 | tf_op jit(solution)/shard_map/all_to_all | solution.py:381
  166.8 9.5 %collective-permute-start.19 = (bf16[2,64,2048]{2,1,0:T(8,128)(2,1)S(1)}, bf16[2,64,2048]{2,1,0:T(8,128)(2,1)S(1)}, u32[]{:S(2)}, u32[]{:S(2)}) collective-permute-start(bf16[2,64,2048]{2,1,0:T(8,128)(2,1)S(1)} %constant_dynamic-slice_fusion), channel_id=1, source_target_pairs={{0,4},{4,0},{1,5},{5,1},{2,6},{6,2},{3,7},{7,3},{8,12},{12,8},{9,1... | collective-permute-start | bytes 1572872 | tf_op jit(solution)/shard_map/ppermute | solution.py:375
Sparse Core Ops, SparseCore 0:
  42.6 41.2 all-gather.1

commit v5 on v4

--- a/solution.py
+++ b/solution.py
@@ -65,7 +65,7 @@
         return tuple(new), elapsed + dt
 
     zero = jnp.zeros((8, LANES), F32)
-    states, elapsed = lax.fori_loop(0, SPAN, step, ((zero,) * NST, zero), unroll=2)
+    states, elapsed = lax.fori_loop(0, SPAN, step, ((zero,) * NST, zero), unroll=4)
     for n in range(NST):
         tmp[pl.ds(n, 8, stride=MSG), :] = states[n]
     high = elapsed.astype(BF16).astype(F32)
@@ -111,7 +111,7 @@
         return tuple(new)
 
     start = tuple(tmp[pl.ds(n, 8, stride=NST), :] for n in range(NST))
-    lax.fori_loop(0, SPAN, step, start, unroll=2)
+    lax.fori_loop(0, SPAN, step, start, unroll=4)
     rows = order[PIECES] + lax.broadcasted_iota(jnp.int32, (SPAN, LANES), 0)
     keep = rows < live[pl.program_id(1)]
     for j in range(8):

time: 185 us -> 184 us (level)
  transfers between devices with their start and end apart: 25 -> 25, of which waited for: 6 -> 6; matrix products, arithmetic and copies ran while one was open for 10% -> 10% of each run, Pallas kernels for 28% -> 27%
where the time goes in v5:
time: 184 us; the launch traced here: 183 us
  starting transfers between devices  57.5 us (31%)
  Pallas kernels  51.3 us (28%)
  waiting for transfers between devices  34.9 us (19%)
  local copies, waits for them, and re-layouts  15.4 us (8%)
  between operations  14.8 us (8%)
  other arithmetic  9.23 us (5%)
    ppermute x14, waiting for transfers between devices, turned(): return block if dc + dh == 0 else lax.ppermute(block, group, route)  22.8 us
    ppermute x14, starting transfers between devices, turned(): return block if dc + dh == 0 else lax.ppermute(block, group, route)  19.3 us
    pallas_call x2, Pallas kernels, attend(): pl.pallas_call(attend_pass, grid_spec=pltpu.PrefetchScalarGridSpec(num_sc...  19.2 us
    pallas_call x1, Pallas kernels, shards(): pl.pallas_call(second_pass, grid_spec=pltpu.PrefetchScalarGridSpec(num_sc...  14.2 us
    pallas_call x1, Pallas kernels, shards(): pl.pallas_call(first_pass, grid_spec=pltpu.PrefetchScalarGridSpec(num_sca...  14.2 us
    all_to_all x1, starting transfers between devices, shards(): entering = lax.all_to_all(prefix, ('z', 'x'), 0, 0, tiled=True)  9.78 us
    all_to_all x1, waiting for transfers between devices, shards(): home = lax.all_to_all(attended, 'x', 0, 0, tiled=True)  8.44 us
    ppermute x1, starting transfers between devices, shards(): far = lax.ppermute(far, 'z', mirror)  6.09 us
  transfers between devices with their start and end apart: 25, of which 6 were waited for; matrix products, arithmetic and copies ran while one was open for 10% of the time, Pallas kernels for 27%

profile of v5, /device:TPU:32, one launch (start us, length us, event | category | flops | bytes accessed | tf_op | source)
XLA Modules:
  0.0 183.1 jit_solution(3772777257808610485)
XLA Ops:
  7.3 1.8 dynamic-slice_bitcast_fusion.8
  9.1 0.1 collective-permute-start.3
  9.2 0.7 pad_maximum_fusion.6
  9.9 3.0 %collective-permute-start.2 = (bf16[2,2,16,2048]{3,2,1,0:T(8,128)(2,1)}, bf16[2,2,16,2048]{3,2,1,0:T(8,128)(2,1)S(1)}, u32[]{:S(2)}, u32[]{:S(2)}) collective-permute-start(bf16[2,2,16,2048]{3,2,1,0:T(8,128)(2,1)} %pad_maximum_fusion.6), channel_id=1, source_target_pairs={{0,3},{1,0},{2,1},{3,2},{4,7},{5,4},{6,5},{7,6},{8,11},{9,8},{10,9... | collective-permute-start | bytes 786440 | tf_op jit(solution)/shard_map/ppermute | solution.py:233
  12.9 2.0 %shard_map.140 = bf16[16,16,1280]{2,1,0:T(8,128)(2,1)} custom-call(bf16[2,16,8192]{2,1,0:T(8,128)(2,1)} %q.1, bf16[2,16,1024]{2,1,0:T(8,128)(2,1)} %k.1, bf16[2,16,1024]{2,1,0:T(8,128)(2,1)} %v.1), custom_call_target="tpu_custom_call" | custom-call | tf_op jit(solution)/shard_map/pallas_call | solution.py:240
  14.9 4.6 %all-to-all-start = ((bf16[16,16,1280]{2,1,0:T(8,128)(2,1)}), bf16[16,16,1280]{2,1,0:T(8,128)(2,1)S(1)}, u32[]{:S(2)}, u32[]{:S(2)}) async-start(bf16[16,16,1280]{2,1,0:T(8,128)(2,1)} %shard_map.140), calls=%async_computation | async-start | bytes 1310720 | tf_op jit(solution)/shard_map/all_to_all | solution.py:246
  19.6 3.5 %collective-permute-start.1 = (bf16[2,2,16,2048]{3,2,1,0:T(8,128)(2,1)S(1)}, bf16[2,2,16,2048]{3,2,1,0:T(8,128)(2,1)S(1)}, u32[]{:S(2)}, u32[]{:S(2)}) collective-permute-start(bf16[2,2,16,2048]{3,2,1,0:T(8,128)(2,1)S(1)} %pad_maximum_fusion.5), channel_id=1, source_target_pairs={{0,2},{1,3},{2,0},{3,1},{4,6},{5,7},{6,4},{7,5},{8,10},{9,11},{10,... | collective-permute-start | bytes 786440 | tf_op jit(solution)/shard_map/ppermute | solution.py:233
  23.1 0.6 collective-permute-start
  23.9 13.4 %collective-permute-done.1.refs_2_ = bf16[2,2,16,2048]{3,2,1,0:T(8,128)(2,1)S(1)} collective-permute-done((bf16[2,2,16,2048]{3,2,1,0:T(8,128)(2,1)S(1)}, bf16[2,2,16,2048]{3,2,1,0:T(8,128)(2,1)S(1)}, u32[]{:S(2)}, u32[]{:S(2)}) %collective-permute-start.1) | collective-permute-done | bytes 262176 | tf_op jit(solution)/shard_map/ppermute | solution.py:233
  37.3 4.4 %collective-permute-done.refs_1_ = bf16[2,2,16,2048]{3,2,1,0:T(8,128)(2,1)S(1)} collective-permute-done((bf16[2,2,16,2048]{3,2,1,0:T(8,128)(2,1)S(1)}, bf16[2,2,16,2048]{3,2,1,0:T(8,128)(2,1)S(1)}, u32[]{:S(2)}, u32[]{:S(2)}) %collective-permute-start) | collective-permute-done | bytes 262176 | tf_op jit(solution)/shard_map/ppermute | solution.py:233
  41.8 0.7 slice.69
  42.5 0.7 pad_maximum_fusion.9
  43.2 0.7 pad_maximum_fusion.10
  43.9 3.2 %collective-permute-start.6 = (bf16[2,2,16,2048]{3,2,1,0:T(8,128)(2,1)}, bf16[2,2,16,2048]{3,2,1,0:T(8,128)(2,1)}, u32[]{:S(2)}, u32[]{:S(2)}) collective-permute-start(bf16[2,2,16,2048]{3,2,1,0:T(8,128)(2,1)} %pad_maximum_fusion.10), channel_id=1, source_target_pairs={{0,7},{1,4},{2,5},{3,6},{4,3},{5,0},{6,1},{7,2},{8,15},{9,12},{10,... | collective-permute-start | bytes 786440 | tf_op jit(solution)/shard_map/ppermute | solution.py:233
  47.1 0.7 pad_maximum_fusion.8
  47.8 0.7 dynamic-slice_convert_fusion
  48.7 0.8 dynamic_slice.117
  49.5 0.7 dynamic_slice.118
  50.2 0.7 dynamic_slice.119
  50.9 0.6 copy.23
  51.6 1.3 dynamic_slice.125
  52.9 0.7 concatenate.19.refs_9_.refs_10_
  53.6 0.7 stack.133.order
  54.3 0.1 maximum_convert_fusion
  54.3 2.8 %collective-permute-done.6.refs_7_ = bf16[2,2,16,2048]{3,2,1,0:T(8,128)(2,1)} collective-permute-done((bf16[2,2,16,2048]{3,2,1,0:T(8,128)(2,1)}, bf16[2,2,16,2048]{3,2,1,0:T(8,128)(2,1)}, u32[]{:S(2)}, u32[]{:S(2)}) %collective-permute-start.6) | collective-permute-done | bytes 262176 | tf_op jit(solution)/shard_map/ppermute | solution.py:233
  57.1 2.1 %collective-permute-done.4.refs_5_ = bf16[2,2,16,2048]{3,2,1,0:T(8,128)(2,1)} collective-permute-done((bf16[2,2,16,2048]{3,2,1,0:T(8,128)(2,1)}, bf16[2,2,16,2048]{3,2,1,0:T(8,128)(2,1)}, u32[]{:S(2)}, u32[]{:S(2)}) %collective-permute-start.4) | collective-permute-done | bytes 262176 | tf_op jit(solution)/shard_map/ppermute | solution.py:233
  59.2 1.0 fusion.1
  60.3 3.4 %collective-permute-start.7 = (bf16[2,3,2048]{2,1,0:T(4,128)(2,1)S(1)}, bf16[2,3,2048]{2,1,0:T(4,128)(2,1)S(1)}, u32[]{:S(2)}, u32[]{:S(2)}) collective-permute-start(bf16[2,3,2048]{2,1,0:T(4,128)(2,1)S(1)} %fusion.1), channel_id=1, source_target_pairs={{0,8},{8,16},{16,24},{24,32},{32,40},{40,48},{48,56},{56,64},{64,7... | collective-permute-start | bytes 73736 | tf_op jit(solution)/shard_map/ppermute | solution.py:254
  63.7 0.1 copy.18
  63.8 0.1 broadcast_in_dim.64
  63.9 0.7 slice.64
  64.7 3.6 %collective-permute-done.7.refs_8_ = bf16[2,3,2048]{2,1,0:T(4,128)(2,1)S(1)} collective-permute-done((bf16[2,3,2048]{2,1,0:T(4,128)(2,1)S(1)}, bf16[2,3,2048]{2,1,0:T(4,128)(2,1)S(1)}, u32[]{:S(2)}, u32[]{:S(2)}) %collective-permute-start.7) | collective-permute-done | bytes 24608 | tf_op jit(solution)/shard_map/ppermute | solution.py:254
  68.3 2.0 %broadcast_in_dim.65.refs_11_.refs_12_ = f32[2,2048,128]{2,1,0:T(8,128)} broadcast(f32[2,2048]{1,0:T(2,128)S(1)} %broadcast_in_dim.64), dimensions={0,1} | broadcast | bytes 2113536 | tf_op jit(solution)/shard_map/broadcast_in_dim | solution.py:269
  70.3 6.1 %collective-permute-start.9 = (bf16[4,64,512]{2,1,0:T(8,128)(2,1)}, bf16[4,64,512]{2,1,0:T(8,128)(2,1)S(1)}, u32[]{:S(2)}, u32[]{:S(2)}) collective-permute-start(bf16[4,64,512]{2,1,0:T(8,128)(2,1)} %slice.64), channel_id=1, source_target_pairs={{0,224},{32,192},{64,160},{96,128},{128,96},{160,64},{192,32},{224... | collective-permute-start | bytes 786440 | tf_op jit(solution)/shard_map/ppermute | solution.py:272
  76.4 0.7 dynamic-slice_bitcast_fusion.4
  77.1 0.2 collective-permute-start.10
  77.3 1.5 collective-permute-start.11
  78.7 2.1 %collective-permute-start.12 = (bf16[1,2,16,2048]{3,2,1,0:T(8,128)(2,1)S(1)}, bf16[1,2,16,2048]{3,2,1,0:T(8,128)(2,1)S(1)}, u32[]{:S(2)}, u32[]{:S(2)}) collective-permute-start(bf16[1,2,16,2048]{3,2,1,0:T(8,128)(2,1)S(1)} %get-tuple-element.88), channel_id=1, source_target_pairs={{0,3},{1,0},{2,1},{3,2},{4,7},{5,4},{6,5},{7,6},{8,11},{9,8},{10,9... | collective-permute-start | bytes 393224 | tf_op jit(solution)/shard_map/ppermute | solution.py:233
  80.9 14.2 %first_pass.1 = (f32[2,2,1024,128]{3,2,1,0:T(8,128)}, f32[2,2,1024,128]{3,2,1,0:T(8,128)}, bf16[32,24,128]{2,1,0:T(8,128)(2,1)}) custom-call(s32[9]{0:T(128)} %stack.133.order, bf16[2,2,16,2048]{3,2,1,0:T(8,128)(2,1)} %copy-done.2, bf16[2,2,16,2048]{3,2,1,0:T(8,128)(2,1)} %copy-done.10, bf16[2,2,16,2048]{3,2,1,0:T(8,128)(2,1)} %copy-done.9, ...), custom_call_target="tpu_custom_call" | custom-call | tf_op jit(solution)/shard_map/first_pass/pallas_call | solution.py:295
  95.2 4.8 %all-to-all-start.1 = ((bf16[32,24,128]{2,1,0:T(8,128)(2,1)}), bf16[32,24,128]{2,1,0:T(8,128)(2,1)S(1)}, u32[]{:S(2)}, u32[]{:S(2)}) async-start(bf16[32,24,128]{2,1,0:T(8,128)(2,1)} %get-tuple-element.58), calls=%async_computation.1 | async-start | bytes 393216 | tf_op jit(solution)/shard_map/all_to_all | solution.py:324
  100.1 0.3 collective-permute-start.13
  100.4 0.4 collective-permute-start.14
  100.8 2.0 %collective-permute-start.15 = (bf16[1,2,16,2048]{3,2,1,0:T(8,128)(2,1)S(1)}, bf16[1,2,16,2048]{3,2,1,0:T(8,128)(2,1)S(1)}, u32[]{:S(2)}, u32[]{:S(2)}) collective-permute-start(bf16[1,2,16,2048]{3,2,1,0:T(8,128)(2,1)S(1)} %get-tuple-element.85), channel_id=1, source_target_pairs={{0,6},{1,7},{2,4},{3,5},{4,2},{5,3},{6,0},{7,1},{8,14},{9,15},{10,... | collective-permute-start | bytes 393224 | tf_op jit(solution)/shard_map/ppermute | solution.py:233
  102.8 2.4 %collective-permute-start.16 = (bf16[1,2,16,2048]{3,2,1,0:T(8,128)(2,1)S(1)}, bf16[1,2,16,2048]{3,2,1,0:T(8,128)(2,1)S(1)}, u32[]{:S(2)}, u32[]{:S(2)}) collective-permute-start(bf16[1,2,16,2048]{3,2,1,0:T(8,128)(2,1)S(1)} %get-tuple-element.84), channel_id=1, source_target_pairs={{0,7},{1,4},{2,5},{3,6},{4,3},{5,0},{6,1},{7,2},{8,15},{9,12},{10,... | collective-permute-start | bytes 393224 | tf_op jit(solution)/shard_map/ppermute | solution.py:233
  105.2 1.3 pad_add_fusion.info
  106.5 0.6 constant_dynamic-slice_fusion.1.rate
  107.1 9.6 %attend_pass.2 = (bf16[4,64,256]{2,1,0:T(8,128)(2,1)}, bf16[4,64,256]{2,1,0:T(8,128)(2,1)}) custom-call(s32[4]{0:T(128)} %pad_add_fusion.info, bf16[4,64,1280]{2,1,0:T(8,128)(2,1)} %bitcast.88, bf16[4,64,512]{2,1,0:T(8,128)(2,1)} %copy-done.3, bf16[16,256,256]{2,1,0:T(8,128)(2,1)} %all-gather.2.cloned.1.call-done.kv_ref), custom_call_target="tpu_custom_call" | custom-call | tf_op jit(solution)/shard_map/attend_pass/pallas_call | solution.py:184
  116.8 0.8 copy-done.5
  117.6 1.7 prefix_pass.1
  119.2 9.8 %all-to-all-start.2 = ((bf16[32,16,128]{2,1,0:T(8,128)(2,1)}), bf16[32,16,128]{2,1,0:T(8,128)(2,1)S(1)}, u32[]{:S(2)}, u32[]{:S(2)}) async-start(bf16[32,16,128]{2,1,0:T(8,128)(2,1)} %prefix_pass.1), calls=%async_computation.2 | async-start | bytes 262144 | tf_op jit(solution)/shard_map/all_to_all | solution.py:339
  129.0 3.7 %collective-permute-start.17 = (bf16[4,64,256]{2,1,0:T(8,128)(2,1)}, bf16[4,64,256]{2,1,0:T(8,128)(2,1)S(1)}, u32[]{:S(2)}, u32[]{:S(2)}) collective-permute-start(bf16[4,64,256]{2,1,0:T(8,128)(2,1)} %get-tuple-element.74), channel_id=1, source_target_pairs={{0,224},{32,192},{64,160},{96,128},{128,96},{160,64},{192,32},{224... | collective-permute-start | bytes 393224 | tf_op jit(solution)/shard_map/ppermute | solution.py:328
  132.7 9.6 %attend_pass.3 = (bf16[4,64,256]{2,1,0:T(8,128)(2,1)}, bf16[4,64,256]{2,1,0:T(8,128)(2,1)}) custom-call(s32[4]{0:T(128)} %pad_add_fusion.info, bf16[4,64,1280]{2,1,0:T(8,128)(2,1)} %bitcast.89, bf16[4,64,512]{2,1,0:T(8,128)(2,1)} %copy-done.3, bf16[16,256,256]{2,1,0:T(8,128)(2,1)} %all-gather.2.cloned.1.call-done.kv_ref), custom_call_target="tpu_custom_call" | custom-call | tf_op jit(solution)/shard_map/attend_pass/pallas_call | solution.py:184
  142.4 1.5 collective-permute-start.18
  143.9 0.1 copy.20
  144.0 0.1 broadcast_in_dim.78
  144.1 1.9 %broadcast_in_dim.79.refs_13_ = f32[2,2048,128]{2,1,0:T(8,128)} broadcast(f32[2,2048]{1,0:T(2,128)S(1)} %broadcast_in_dim.78), dimensions={0,1} | broadcast | bytes 2113536 | tf_op jit(solution)/shard_map/broadcast_in_dim | solution.py:270
  146.1 14.2 %second_pass.1 = bf16[2,128,2048]{2,1,0:T(8,128)(2,1)} custom-call(s32[9]{0:T(128)} %stack.133.order, bf16[1,2,16,2048]{3,2,1,0:T(8,128)(2,1)} %get-tuple-element.54.refs_0_, bf16[1,2,16,2048]{3,2,1,0:T(8,128)(2,1)} %copy-done.14, bf16[1,2,16,2048]{3,2,1,0:T(8,128)(2,1)} %copy-done.15, bf16[1,2,16,2048]{3,2,1,0:T(8,128)(2,1)} %copy-done.16, ...), custom_call_target="tpu_custom_call" | custom-call | tf_op jit(solution)/shard_map/second_pass/pallas_call | solution.py:344
  160.3 0.9 pad_maximum_fusion.1
  161.2 4.2 %all-to-all-start.3 = ((bf16[4,64,1024]{2,1,0:T(8,128)(2,1)}), bf16[4,64,1024]{2,1,0:T(8,128)(2,1)S(1)}, u32[]{:S(2)}, u32[]{:S(2)}) async-start(bf16[4,64,1024]{2,1,0:T(8,128)(2,1)} %pad_maximum_fusion.1), calls=%async_computation.3 | async-start | bytes 1048576 | tf_op jit(solution)/shard_map/all_to_all | solution.py:381
  165.5 0.1 collective-permute-start.19
  165.6 8.4 %all-to-all-done.3 = bf16[4,64,1024]{2,1,0:T(8,128)(2,1)S(1)} async-done(((bf16[4,64,1024]{2,1,0:T(8,128)(2,1)}), bf16[4,64,1024]{2,1,0:T(8,128)(2,1)S(1)}, u32[]{:S(2)}, u32[]{:S(2)}) %all-to-all-start.3) | async-done | bytes 524320 | tf_op jit(solution)/shard_map/all_to_all | solution.py:381
  174.1 0.8 pad_maximum_fusion.2
  175.0 0.2 broadcast_select_fusion.1
  175.2 1.0 pad_maximum_fusion
  (88 shorter events, 0.6 us)
Async XLA Ops:
  9.1 14.8 %collective-permute-start.3 = (bf16[2,2,16,2048]{3,2,1,0:T(8,128)(2,1)S(1)}, bf16[2,2,16,2048]{3,2,1,0:T(8,128)(2,1)S(1)}, u32[]{:S(2)}, u32[]{:S(2)}) collective-permute-start(bf16[2,2,16,2048]{3,2,1,0:T(8,128)(2,1)S(1)} %pad_maximum_fusion.7), channel_id=1, source_target_pairs={{0,4},{1,5},{2,6},{3,7},{4,0},{5,1},{6,2},{7,3},{8,12},{9,13},{10,... | collective-permute-start | bytes 786440 | tf_op jit(solution)/shard_map/ppermute | solution.py:233
  9.9 13.9 %collective-permute-start.2 = (bf16[2,2,16,2048]{3,2,1,0:T(8,128)(2,1)}, bf16[2,2,16,2048]{3,2,1,0:T(8,128)(2,1)S(1)}, u32[]{:S(2)}, u32[]{:S(2)}) collective-permute-start(bf16[2,2,16,2048]{3,2,1,0:T(8,128)(2,1)} %pad_maximum_fusion.6), channel_id=1, source_target_pairs={{0,3},{1,0},{2,1},{3,2},{4,7},{5,4},{6,5},{7,6},{8,11},{9,8},{10,9... | collective-permute-start | bytes 786440 | tf_op jit(solution)/shard_map/ppermute | solution.py:233
  14.9 26.9 %all-to-all-start = ((bf16[16,16,1280]{2,1,0:T(8,128)(2,1)}), bf16[16,16,1280]{2,1,0:T(8,128)(2,1)S(1)}, u32[]{:S(2)}, u32[]{:S(2)}) async-start(bf16[16,16,1280]{2,1,0:T(8,128)(2,1)} %shard_map.140), calls=%async_computation | async-start | bytes 1310720 | tf_op jit(solution)/shard_map/all_to_all | solution.py:246
  19.5 28.3 %copy-start.24 = (bf16[2,64,32]{1,2,0:T(8,128)(2,1)S(1)}, bf16[2,64,32]{1,2,0:T(8,128)(2,1)}, u32[]{:S(2)}) copy-start(bf16[2,64,32]{1,2,0:T(8,128)(2,1)} %param.16) | copy-start | bytes 24580
  19.5 29.1 %copy-start.12 = (f32[16,4096]{1,0:T(8,128)S(1)}, f32[16,4096]{1,0:T(8,128)}, u32[]{:S(2)}) copy-start(f32[16,4096]{1,0:T(8,128)} %param.20) | copy-start | bytes 786436
  19.5 87.6 %all-gather.2.cloned.1.call-start = ((), (), s32[]{:S(2)}) async-start(), calls=%async_computation.4 | async-start | bytes 2228224 | tf_op jit(solution)/shard_map/all_gather | solution.py:257
  19.6 17.7 %collective-permute-start.1 = (bf16[2,2,16,2048]{3,2,1,0:T(8,128)(2,1)S(1)}, bf16[2,2,16,2048]{3,2,1,0:T(8,128)(2,1)S(1)}, u32[]{:S(2)}, u32[]{:S(2)}) collective-permute-start(bf16[2,2,16,2048]{3,2,1,0:T(8,128)(2,1)S(1)} %pad_maximum_fusion.5), channel_id=1, source_target_pairs={{0,2},{1,3},{2,0},{3,1},{4,6},{5,7},{6,4},{7,5},{8,10},{9,11},{10,... | collective-permute-start | bytes 786440 | tf_op jit(solution)/shard_map/ppermute | solution.py:233
  23.1 18.6 %collective-permute-start = (bf16[2,2,16,2048]{3,2,1,0:T(8,128)(2,1)S(1)}, bf16[2,2,16,2048]{3,2,1,0:T(8,128)(2,1)S(1)}, u32[]{:S(2)}, u32[]{:S(2)}) collective-permute-start(bf16[2,2,16,2048]{3,2,1,0:T(8,128)(2,1)S(1)} %pad_maximum_fusion.4), channel_id=1, source_target_pairs={{0,1},{1,2},{2,3},{3,0},{4,5},{5,6},{6,7},{7,4},{8,9},{9,10},{10,1... | collective-permute-start | bytes 786440 | tf_op jit(solution)/shard_map/ppermute | solution.py:233
  23.8 40.8 %copy-start.2 = (bf16[2,2,16,2048]{3,2,1,0:T(8,128)(2,1)}, bf16[2,2,16,2048]{3,2,1,0:T(8,128)(2,1)S(1)}, u32[]{:S(2)}) copy-start(bf16[2,2,16,2048]{3,2,1,0:T(8,128)(2,1)S(1)} %pad_maximum_fusion.3.refs_0_) | copy-start | bytes 786436
  23.8 40.8 %copy-start.7 = (bf16[2,2,16,2048]{3,2,1,0:T(8,128)(2,1)}, bf16[2,2,16,2048]{3,2,1,0:T(8,128)(2,1)S(1)}, u32[]{:S(2)}) copy-start(bf16[2,2,16,2048]{3,2,1,0:T(8,128)(2,1)S(1)} %collective-permute-done.3.refs_4_) | copy-start | bytes 786436
  23.8 40.8 %copy-start.8 = (bf16[2,2,16,2048]{3,2,1,0:T(8,128)(2,1)}, bf16[2,2,16,2048]{3,2,1,0:T(8,128)(2,1)S(1)}, u32[]{:S(2)}) copy-start(bf16[2,2,16,2048]{3,2,1,0:T(8,128)(2,1)S(1)} %collective-permute-done.2.refs_3_) | copy-start | bytes 786436
  37.3 27.4 %copy-start.9 = (bf16[2,2,16,2048]{3,2,1,0:T(8,128)(2,1)}, bf16[2,2,16,2048]{3,2,1,0:T(8,128)(2,1)S(1)}, u32[]{:S(2)}) copy-start(bf16[2,2,16,2048]{3,2,1,0:T(8,128)(2,1)S(1)} %collective-permute-done.1.refs_2_) | copy-start | bytes 786436
  41.7 22.9 %copy-start.10 = (bf16[2,2,16,2048]{3,2,1,0:T(8,128)(2,1)}, bf16[2,2,16,2048]{3,2,1,0:T(8,128)(2,1)S(1)}, u32[]{:S(2)}) copy-start(bf16[2,2,16,2048]{3,2,1,0:T(8,128)(2,1)S(1)} %collective-permute-done.refs_1_) | copy-start | bytes 786436
  41.7 22.9 %copy-start = (bf16[16,16,1280]{2,1,0:T(8,128)(2,1)}, bf16[16,16,1280]{2,1,0:T(8,128)(2,1)S(1)}, u32[]{:S(2)}) copy-start(bf16[16,16,1280]{2,1,0:T(8,128)(2,1)S(1)} %all-to-all-done) | copy-start | bytes 1966084
  43.2 11.1 %collective-permute-start.5 = (bf16[2,2,16,2048]{3,2,1,0:T(8,128)(2,1)}, bf16[2,2,16,2048]{3,2,1,0:T(8,128)(2,1)S(1)}, u32[]{:S(2)}, u32[]{:S(2)}) collective-permute-start(bf16[2,2,16,2048]{3,2,1,0:T(8,128)(2,1)} %pad_maximum_fusion.9), channel_id=1, source_target_pairs={{0,6},{1,7},{2,4},{3,5},{4,2},{5,3},{6,0},{7,1},{8,14},{9,15},{10,... | collective-permute-start | bytes 786440 | tf_op jit(solution)/shard_map/ppermute | solution.py:233
  43.9 13.2 %collective-permute-start.6 = (bf16[2,2,16,2048]{3,2,1,0:T(8,128)(2,1)}, bf16[2,2,16,2048]{3,2,1,0:T(8,128)(2,1)}, u32[]{:S(2)}, u32[]{:S(2)}) collective-permute-start(bf16[2,2,16,2048]{3,2,1,0:T(8,128)(2,1)} %pad_maximum_fusion.10), channel_id=1, source_target_pairs={{0,7},{1,4},{2,5},{3,6},{4,3},{5,0},{6,1},{7,2},{8,15},{9,12},{10,... | collective-permute-start | bytes 786440 | tf_op jit(solution)/shard_map/ppermute | solution.py:233
  47.8 11.4 %collective-permute-start.4 = (bf16[2,2,16,2048]{3,2,1,0:T(8,128)(2,1)}, bf16[2,2,16,2048]{3,2,1,0:T(8,128)(2,1)}, u32[]{:S(2)}, u32[]{:S(2)}) collective-permute-start(bf16[2,2,16,2048]{3,2,1,0:T(8,128)(2,1)} %pad_maximum_fusion.8), channel_id=1, source_target_pairs={{0,5},{1,6},{2,7},{3,4},{4,1},{5,2},{6,3},{7,0},{8,13},{9,14},{10,... | collective-permute-start | bytes 786440 | tf_op jit(solution)/shard_map/ppermute | solution.py:233
  47.8 6.4 %collective-permute-start.8 = (bf16[2,64,32]{1,2,0:T(8,128)(2,1)S(1)}, bf16[2,64,32]{1,2,0:T(8,128)(2,1)S(1)}, u32[]{:S(2)}, u32[]{:S(2)}) collective-permute-start(bf16[2,64,32]{1,2,0:T(8,128)(2,1)S(1)} %copy-done.24), channel_id=1, source_target_pairs={{0,4},{4,0},{1,5},{5,1},{2,6},{6,2},{3,7},{7,3},{8,12},{12,8},{9,1... | collective-permute-start | bytes 24584 | tf_op jit(solution)/shard_map/ppermute | solution.py:265
  48.7 27.7 %copy-start.4 = (bf16[2,16,16384]{2,1,0:T(8,128)(2,1)S(1)}, bf16[2,16,16384]{2,1,0:T(8,128)(2,1)}, u32[]{:S(2)}) copy-start(bf16[2,16,16384]{2,1,0:T(8,128)(2,1)} %param.14) | copy-start | bytes 3145732
  54.3 22.7 %copy-start.11 = (bf16[2,2,16,2048]{3,2,1,0:T(8,128)(2,1)}, bf16[2,2,16,2048]{3,2,1,0:T(8,128)(2,1)S(1)}, u32[]{:S(2)}) copy-start(bf16[2,2,16,2048]{3,2,1,0:T(8,128)(2,1)S(1)} %collective-permute-done.5.refs_6_) | copy-start | bytes 786436
  60.3 8.0 %collective-permute-start.7 = (bf16[2,3,2048]{2,1,0:T(4,128)(2,1)S(1)}, bf16[2,3,2048]{2,1,0:T(4,128)(2,1)S(1)}, u32[]{:S(2)}, u32[]{:S(2)}) collective-permute-start(bf16[2,3,2048]{2,1,0:T(4,128)(2,1)S(1)} %fusion.1), channel_id=1, source_target_pairs={{0,8},{8,16},{16,24},{24,32},{32,40},{40,48},{48,56},{56,64},{64,7... | collective-permute-start | bytes 73736 | tf_op jit(solution)/shard_map/ppermute | solution.py:254
  63.9 17.0 %copy-start.13 = (f32[16,4096]{1,0:T(8,128)S(1)}, f32[16,4096]{1,0:T(8,128)}, u32[]{:S(2)}) copy-start(f32[16,4096]{1,0:T(8,128)} %param.20) | copy-start | bytes 786436
  68.3 12.6 %copy-start.23 = (bf16[2,3,2048]{2,1,0:T(4,128)(2,1)}, bf16[2,3,2048]{2,1,0:T(4,128)(2,1)S(1)}, u32[]{:S(2)}) copy-start(bf16[2,3,2048]{2,1,0:T(4,128)(2,1)S(1)} %collective-permute-done.7.refs_8_) | copy-start | bytes 73732
  70.3 24.9 %collective-permute-start.9 = (bf16[4,64,512]{2,1,0:T(8,128)(2,1)}, bf16[4,64,512]{2,1,0:T(8,128)(2,1)S(1)}, u32[]{:S(2)}, u32[]{:S(2)}) collective-permute-start(bf16[4,64,512]{2,1,0:T(8,128)(2,1)} %slice.64), channel_id=1, source_target_pairs={{0,224},{32,192},{64,160},{96,128},{128,96},{160,64},{192,32},{224... | collective-permute-start | bytes 786440 | tf_op jit(solution)/shard_map/ppermute | solution.py:272
  77.1 18.1 %collective-permute-start.10 = (bf16[1,2,16,2048]{3,2,1,0:T(8,128)(2,1)S(1)}, bf16[1,2,16,2048]{3,2,1,0:T(8,128)(2,1)S(1)}, u32[]{:S(2)}, u32[]{:S(2)}) collective-permute-start(bf16[1,2,16,2048]{3,2,1,0:T(8,128)(2,1)S(1)} %get-tuple-element.90), channel_id=1, source_target_pairs={{0,1},{1,2},{2,3},{3,0},{4,5},{5,6},{6,7},{7,4},{8,9},{9,10},{10,1... | collective-permute-start | bytes 393224 | tf_op jit(solution)/shard_map/ppermute | solution.py:233
  77.3 17.9 %collective-permute-start.11 = (bf16[1,2,16,2048]{3,2,1,0:T(8,128)(2,1)S(1)}, bf16[1,2,16,2048]{3,2,1,0:T(8,128)(2,1)S(1)}, u32[]{:S(2)}, u32[]{:S(2)}) collective-permute-start(bf16[1,2,16,2048]{3,2,1,0:T(8,128)(2,1)S(1)} %get-tuple-element.89), channel_id=1, source_target_pairs={{0,2},{1,3},{2,0},{3,1},{4,6},{5,7},{6,4},{7,5},{8,10},{9,11},{10,... | collective-permute-start | bytes 393224 | tf_op jit(solution)/shard_map/ppermute | solution.py:233
  78.7 16.5 %collective-permute-start.12 = (bf16[1,2,16,2048]{3,2,1,0:T(8,128)(2,1)S(1)}, bf16[1,2,16,2048]{3,2,1,0:T(8,128)(2,1)S(1)}, u32[]{:S(2)}, u32[]{:S(2)}) collective-permute-start(bf16[1,2,16,2048]{3,2,1,0:T(8,128)(2,1)S(1)} %get-tuple-element.88), channel_id=1, source_target_pairs={{0,3},{1,0},{2,1},{3,2},{4,7},{5,4},{6,5},{7,6},{8,11},{9,8},{10,9... | collective-permute-start | bytes 393224 | tf_op jit(solution)/shard_map/ppermute | solution.py:233
  95.2 21.5 %copy-start.14 = (bf16[1,2,16,2048]{3,2,1,0:T(8,128)(2,1)}, bf16[1,2,16,2048]{3,2,1,0:T(8,128)(2,1)S(1)}, u32[]{:S(2)}) copy-start(bf16[1,2,16,2048]{3,2,1,0:T(8,128)(2,1)S(1)} %collective-permute-done.10.refs_1_) | copy-start | bytes 393220
  95.2 21.5 %copy-start.15 = (bf16[1,2,16,2048]{3,2,1,0:T(8,128)(2,1)}, bf16[1,2,16,2048]{3,2,1,0:T(8,128)(2,1)S(1)}, u32[]{:S(2)}) copy-start(bf16[1,2,16,2048]{3,2,1,0:T(8,128)(2,1)S(1)} %collective-permute-done.11.refs_2_) | copy-start | bytes 393220
  95.2 21.5 %copy-start.16 = (bf16[1,2,16,2048]{3,2,1,0:T(8,128)(2,1)}, bf16[1,2,16,2048]{3,2,1,0:T(8,128)(2,1)S(1)}, u32[]{:S(2)}) copy-start(bf16[1,2,16,2048]{3,2,1,0:T(8,128)(2,1)S(1)} %collective-permute-done.12.refs_3_) | copy-start | bytes 393220
  95.2 11.8 %copy-start.3 = (bf16[4,64,512]{2,1,0:T(8,128)(2,1)}, bf16[4,64,512]{2,1,0:T(8,128)(2,1)S(1)}, u32[]{:S(2)}) copy-start(bf16[4,64,512]{2,1,0:T(8,128)(2,1)S(1)} %collective-permute-done.9.far_ref) | copy-start | bytes 786436
  95.2 21.6 %all-to-all-start.1 = ((bf16[32,24,128]{2,1,0:T(8,128)(2,1)}), bf16[32,24,128]{2,1,0:T(8,128)(2,1)S(1)}, u32[]{:S(2)}, u32[]{:S(2)}) async-start(bf16[32,24,128]{2,1,0:T(8,128)(2,1)} %get-tuple-element.58), calls=%async_computation.1 | async-start | bytes 393216 | tf_op jit(solution)/shard_map/all_to_all | solution.py:324
  100.1 16.6 %collective-permute-start.13 = (bf16[1,2,16,2048]{3,2,1,0:T(8,128)(2,1)S(1)}, bf16[1,2,16,2048]{3,2,1,0:T(8,128)(2,1)S(1)}, u32[]{:S(2)}, u32[]{:S(2)}) collective-permute-start(bf16[1,2,16,2048]{3,2,1,0:T(8,128)(2,1)S(1)} %get-tuple-element.87), channel_id=1, source_target_pairs={{0,4},{1,5},{2,6},{3,7},{4,0},{5,1},{6,2},{7,3},{8,12},{9,13},{10,... | collective-permute-start | bytes 393224 | tf_op jit(solution)/shard_map/ppermute | solution.py:233
  100.4 16.4 %collective-permute-start.14 = (bf16[1,2,16,2048]{3,2,1,0:T(8,128)(2,1)S(1)}, bf16[1,2,16,2048]{3,2,1,0:T(8,128)(2,1)S(1)}, u32[]{:S(2)}, u32[]{:S(2)}) collective-permute-start(bf16[1,2,16,2048]{3,2,1,0:T(8,128)(2,1)S(1)} %get-tuple-element.86), channel_id=1, source_target_pairs={{0,5},{1,6},{2,7},{3,4},{4,1},{5,2},{6,3},{7,0},{8,13},{9,14},{10,... | collective-permute-start | bytes 393224 | tf_op jit(solution)/shard_map/ppermute | solution.py:233
  100.8 16.0 %collective-permute-start.15 = (bf16[1,2,16,2048]{3,2,1,0:T(8,128)(2,1)S(1)}, bf16[1,2,16,2048]{3,2,1,0:T(8,128)(2,1)S(1)}, u32[]{:S(2)}, u32[]{:S(2)}) collective-permute-start(bf16[1,2,16,2048]{3,2,1,0:T(8,128)(2,1)S(1)} %get-tuple-element.85), channel_id=1, source_target_pairs={{0,6},{1,7},{2,4},{3,5},{4,2},{5,3},{6,0},{7,1},{8,14},{9,15},{10,... | collective-permute-start | bytes 393224 | tf_op jit(solution)/shard_map/ppermute | solution.py:233
  102.8 14.0 %collective-permute-start.16 = (bf16[1,2,16,2048]{3,2,1,0:T(8,128)(2,1)S(1)}, bf16[1,2,16,2048]{3,2,1,0:T(8,128)(2,1)S(1)}, u32[]{:S(2)}, u32[]{:S(2)}) collective-permute-start(bf16[1,2,16,2048]{3,2,1,0:T(8,128)(2,1)S(1)} %get-tuple-element.84), channel_id=1, source_target_pairs={{0,7},{1,4},{2,5},{3,6},{4,3},{5,0},{6,1},{7,2},{8,15},{9,12},{10,... | collective-permute-start | bytes 393224 | tf_op jit(solution)/shard_map/ppermute | solution.py:233
  116.7 29.3 %copy-start.17 = (bf16[1,2,16,2048]{3,2,1,0:T(8,128)(2,1)}, bf16[1,2,16,2048]{3,2,1,0:T(8,128)(2,1)S(1)}, u32[]{:S(2)}) copy-start(bf16[1,2,16,2048]{3,2,1,0:T(8,128)(2,1)S(1)} %collective-permute-done.13.refs_4_) | copy-start | bytes 393220
  116.7 29.3 %copy-start.18 = (bf16[1,2,16,2048]{3,2,1,0:T(8,128)(2,1)}, bf16[1,2,16,2048]{3,2,1,0:T(8,128)(2,1)S(1)}, u32[]{:S(2)}) copy-start(bf16[1,2,16,2048]{3,2,1,0:T(8,128)(2,1)S(1)} %collective-permute-done.14.refs_5_) | copy-start | bytes 393220
  116.8 29.3 %copy-start.19 = (bf16[1,2,16,2048]{3,2,1,0:T(8,128)(2,1)}, bf16[1,2,16,2048]{3,2,1,0:T(8,128)(2,1)S(1)}, u32[]{:S(2)}) copy-start(bf16[1,2,16,2048]{3,2,1,0:T(8,128)(2,1)S(1)} %collective-permute-done.15.refs_6_) | copy-start | bytes 393220
  116.8 29.3 %copy-start.20 = (bf16[1,2,16,2048]{3,2,1,0:T(8,128)(2,1)}, bf16[1,2,16,2048]{3,2,1,0:T(8,128)(2,1)S(1)}, u32[]{:S(2)}) copy-start(bf16[1,2,16,2048]{3,2,1,0:T(8,128)(2,1)S(1)} %collective-permute-done.16.refs_7_) | copy-start | bytes 393220
  116.8 0.8 copy-start.5
  119.2 23.1 %all-to-all-start.2 = ((bf16[32,16,128]{2,1,0:T(8,128)(2,1)}), bf16[32,16,128]{2,1,0:T(8,128)(2,1)S(1)}, u32[]{:S(2)}, u32[]{:S(2)}) async-start(bf16[32,16,128]{2,1,0:T(8,128)(2,1)} %prefix_pass.1), calls=%async_computation.2 | async-start | bytes 262144 | tf_op jit(solution)/shard_map/all_to_all | solution.py:339
  129.0 13.3 %collective-permute-start.17 = (bf16[4,64,256]{2,1,0:T(8,128)(2,1)}, bf16[4,64,256]{2,1,0:T(8,128)(2,1)S(1)}, u32[]{:S(2)}, u32[]{:S(2)}) collective-permute-start(bf16[4,64,256]{2,1,0:T(8,128)(2,1)} %get-tuple-element.74), channel_id=1, source_target_pairs={{0,224},{32,192},{64,160},{96,128},{128,96},{160,64},{192,32},{224... | collective-permute-start | bytes 393224 | tf_op jit(solution)/shard_map/ppermute | solution.py:328
  142.3 3.7 %copy-start.6 = (bf16[32,16,128]{2,1,0:T(8,128)(2,1)}, bf16[32,16,128]{2,1,0:T(8,128)(2,1)S(1)}, u32[]{:S(2)}) copy-start(bf16[32,16,128]{2,1,0:T(8,128)(2,1)S(1)} %all-to-all-done.2.refs_14_) | copy-start | bytes 393220
  142.4 18.0 %collective-permute-start.18 = (bf16[4,64,256]{2,1,0:T(8,128)(2,1)}, bf16[4,64,256]{2,1,0:T(8,128)(2,1)S(1)}, u32[]{:S(2)}, u32[]{:S(2)}) collective-permute-start(bf16[4,64,256]{2,1,0:T(8,128)(2,1)} %get-tuple-element.76), channel_id=1, source_target_pairs={{0,224},{32,192},{64,160},{96,128},{128,96},{160,64},{192,32},{224... | collective-permute-start | bytes 393224 | tf_op jit(solution)/shard_map/ppermute | solution.py:342
  146.1 14.3 %copy-start.21 = (bf16[4,64,256]{2,1,0:T(8,128)(2,1)S(1)}, bf16[4,64,256]{2,1,0:T(8,128)(2,1)}, u32[]{:S(2)}) copy-start(bf16[4,64,256]{2,1,0:T(8,128)(2,1)} %get-tuple-element.78) | copy-start | bytes 393220
  146.1 14.3 %copy-start.22 = (bf16[4,64,256]{2,1,0:T(8,128)(2,1)S(1)}, bf16[4,64,256]{2,1,0:T(8,128)(2,1)}, u32[]{:S(2)}) copy-start(bf16[4,64,256]{2,1,0:T(8,128)(2,1)} %get-tuple-element.79) | copy-start | bytes 393220
  160.3 5.1 %copy-start.1 = (bf16[2,128,2048]{2,1,0:T(8,128)(2,1)S(1)}, bf16[2,128,2048]{2,1,0:T(8,128)(2,1)}, u32[]{:S(2)}) copy-start(bf16[2,128,2048]{2,1,0:T(8,128)(2,1)} %second_pass.1) | copy-start | bytes 3145732
  161.2 12.8 %all-to-all-start.3 = ((bf16[4,64,1024]{2,1,0:T(8,128)(2,1)}), bf16[4,64,1024]{2,1,0:T(8,128)(2,1)S(1)}, u32[]{:S(2)}, u32[]{:S(2)}) async-start(bf16[4,64,1024]{2,1,0:T(8,128)(2,1)} %pad_maximum_fusion.1), calls=%async_computation.3 | async-start | bytes 1048576 | tf_op jit(solution)/shard_map/all_to_all | solution.py:381
  165.5 9.5 %collective-permute-start.19 = (bf16[2,64,2048]{2,1,0:T(8,128)(2,1)S(1)}, bf16[2,64,2048]{2,1,0:T(8,128)(2,1)S(1)}, u32[]{:S(2)}, u32[]{:S(2)}) collective-permute-start(bf16[2,64,2048]{2,1,0:T(8,128)(2,1)S(1)} %constant_dynamic-slice_fusion), channel_id=1, source_target_pairs={{0,4},{4,0},{1,5},{5,1},{2,6},{6,2},{3,7},{7,3},{8,12},{12,8},{9,1... | collective-permute-start | bytes 1572872 | tf_op jit(solution)/shard_map/ppermute | solution.py:375
Sparse Core Ops, SparseCore 0:
  42.6 41.2 all-gather.1
